TPU v7x, 32 devices: a whole 2x2x4 slice. The times are simulated.
32 devices in a mesh: gx: 4 (over y, core), gy: 8 (over z, x).
Axes of the slice: x: 2, y: 2, z: 4, core: 2. Of those that a mesh axis runs over, the one named last changes fastest.
Arguments:
- points: float32 [8192, 512], P(('gx', 'gy')), may hold values from -6 to 6
- upstream: float32 [8192, 512], P(('gx', 'gy')), may hold values from -6 to 6
- gains: float32 [2, 512], replicated, may hold values from 0.1 to 1.9
- w_qkv: float32 [2, 512, 1536], replicated, may hold values from -20 to 20
- w_proj: float32 [2, 512, 512], replicated, may hold values from -0.25 to 0.25
- z_route: int32 [512, 2], P(('gx', 'gy')), may hold values from 0 to 31, as said below
- h_route: int32 [512, 2], P(('gx', 'gy')), may hold values from 0 to 31, as said below
Outputs:
- point_grad: float32 [8192, 512], P(('gx', 'gy'))
- gain_grad: float32 [2, 512], P(None, ('gx', 'gy'))
- qkv_grad: float32 [2, 512, 1536], P(None, ('gx', 'gy'))
- proj_grad: float32 [2, 512, 512], P(None, ('gx', 'gy'))
Inputs may be any that keep to these rules, and one draw needn't show every extreme that they name: `z_route`: column 0 names the owner device (gx index times 8 plus gy index), which has the same gx index as the device that holds the segment; column 1 names the slot at the owner, below 16. Every slot of every device is named exactly once, and each device sends exactly 2 of its segments to each owner of its gx index. `h_route`: column 0 names the owner device (gx index times 8 plus gy index), which has the same gy index as the device that holds the segment; column 1 names the slot at the owner, below 16. Every slot of every device is named exactly once, and each device sends exactly 4 of its segments to each owner of its gy index.
All inputs are finite; a program needn't handle non-finite values.
Results may differ from a plain program's by a relative error of at most 0.00085.
Values sent between devices are 32-bit elements; how exact they have to be, the bound alone decides.
A program may use at most 128 MiB of HBM per device.

v0:
```python
import math

import jax
import jax.numpy as jnp
from jax import lax
from jax.sharding import PartitionSpec as P

D = 512
HEADS = 32
PATCH = 128
SEG = 16


exact_mode = lax.Precision.HIGHEST
epsilon = 1e-05


def attend_block(rows_in, gain_row, qkv_weight, proj_weight):
    row_count = rows_in.shape[0]
    head_dim = D // HEADS
    row_mean = jnp.mean(rows_in, axis=-1, keepdims=True)
    centered = rows_in - row_mean
    row_var = jnp.mean(centered * centered, axis=-1, keepdims=True)
    normed = centered * lax.rsqrt(row_var + epsilon) * gain_row
    projected = jnp.dot(normed, qkv_weight, precision=exact_mode)
    projected = projected.reshape(row_count // PATCH, PATCH, 3, HEADS, head_dim)
    queries = projected[:, :, 0]
    key_rows = projected[:, :, 1]
    value_rows = projected[:, :, 2]
    scores = jnp.einsum("pihd,pjhd->phij", queries, key_rows, precision=exact_mode) * (
        1.0 / math.sqrt(head_dim)
    )
    attention = jax.nn.softmax(scores, axis=-1)
    mixed_rows = jnp.einsum("phij,pjhd->pihd", attention, value_rows, precision=exact_mode)
    return rows_in + jnp.dot(mixed_rows.reshape(row_count, D), proj_weight, precision=exact_mode)


def occupancy(owner_index):
    count = owner_index.shape[0]
    same = owner_index[None, :] == owner_index[:, None]
    earlier = jnp.arange(count)[None, :] < jnp.arange(count)[:, None]
    return jnp.sum(same & earlier, axis=1)


def spread_out(rows_in, owner_index, dest_slot, peer_count):
    segments = rows_in.reshape(-1, SEG, rows_in.shape[1])
    seg_count = segments.shape[0]
    per_peer = seg_count // peer_count
    occur = occupancy(owner_index)
    buffer = (
        jnp.zeros((peer_count, per_peer) + segments.shape[1:], rows_in.dtype)
        .at[owner_index, occur]
        .set(segments)
    )
    labels = (
        jnp.full((peer_count, per_peer), seg_count, jnp.int32).at[owner_index, occur].set(dest_slot)
    )
    return (buffer, labels, occur)


def settle_in(received, got_labels, seg_count):
    flat = received.reshape((-1,) + received.shape[2:])
    flat_labels = got_labels.reshape(-1)
    matches = flat_labels[None, :] == jnp.arange(seg_count, dtype=jnp.int32)[:, None]
    source = jnp.sum(
        jnp.where(matches, jnp.arange(flat_labels.shape[0], dtype=jnp.int32)[None, :], 0), axis=1
    )
    return (flat[source].reshape(-1, flat.shape[2]), source)


def pack_back(rows_in, source, peer_count):
    segments = rows_in.reshape(-1, SEG, rows_in.shape[1])
    placed = jnp.zeros_like(segments).at[source].set(segments)
    return placed.reshape((peer_count, -1) + segments.shape[1:])


def to_zorder(rows_in, route):
    peer_count = lax.axis_size("gy")
    owner_index = route[:, 0] % peer_count
    buffer, labels, occur = spread_out(rows_in, owner_index, route[:, 1], peer_count)
    received, got_labels = (
        lax.all_to_all(buffer, "gy", split_axis=0, concat_axis=0, tiled=True),
        lax.all_to_all(labels, "gy", split_axis=0, concat_axis=0, tiled=True),
    )
    rows_out, source = settle_in(received, got_labels, route.shape[0])
    return (rows_out, source, occur)


def from_zorder(rows_in, source, occur, route):
    peer_count = lax.axis_size("gy")
    buffer = pack_back(rows_in, source, peer_count)
    received = lax.all_to_all(buffer, "gy", split_axis=0, concat_axis=0, tiled=True)
    return received[route[:, 0] % peer_count, occur].reshape(-1, rows_in.shape[1])


def to_hilbert(rows_in, route):
    peer_count = lax.axis_size("gx")
    owner_index = route[:, 0] // lax.axis_size("gy")
    buffer, labels, occur = spread_out(rows_in, owner_index, route[:, 1], peer_count)
    received, got_labels = (
        lax.all_to_all(buffer, "gx", split_axis=0, concat_axis=0, tiled=True),
        lax.all_to_all(labels, "gx", split_axis=0, concat_axis=0, tiled=True),
    )
    rows_out, source = settle_in(received, got_labels, route.shape[0])
    return (rows_out, source, occur)


def from_hilbert(rows_in, source, occur, route):
    peer_count = lax.axis_size("gx")
    buffer = pack_back(rows_in, source, peer_count)
    received = lax.all_to_all(buffer, "gx", split_axis=0, concat_axis=0, tiled=True)
    return received[route[:, 0] // lax.axis_size("gy"), occur].reshape(-1, rows_in.shape[1])


def reduce_grads(gain_part, qkv_part, proj_part):
    return (
        lax.psum_scatter(gain_part, ("gx", "gy"), scatter_dimension=1, tiled=True),
        lax.psum_scatter(qkv_part, ("gx", "gy"), scatter_dimension=1, tiled=True),
        lax.psum_scatter(proj_part, ("gx", "gy"), scatter_dimension=1, tiled=True),
    )


def per_device(points, upstream, gains, w_qkv, w_proj, z_route, h_route):
    curve_first, z_source, z_occur = to_zorder(points, z_route)
    first_out, pull_first = jax.vjp(attend_block, curve_first, gains[0], w_qkv[0], w_proj[0])
    middle = from_zorder(first_out, z_source, z_occur, z_route)
    curve_second, h_source, h_occur = to_hilbert(middle, h_route)
    grad_curve, unused_source, unused_occur = to_hilbert(upstream, h_route)
    second_out, pull_second = jax.vjp(attend_block, curve_second, gains[1], w_qkv[1], w_proj[1])
    grad_second, gain_second, qkv_second, proj_second = pull_second(grad_curve)
    grad_middle = from_hilbert(grad_second, h_source, h_occur, h_route)
    middle_curve, unused_again, unused_spots = to_zorder(grad_middle, z_route)
    grad_first, gain_first, qkv_first, proj_first = pull_first(middle_curve)
    point_grad = from_zorder(grad_first, z_source, z_occur, z_route)
    gain_grad, qkv_grad, proj_grad = reduce_grads(
        jnp.stack([gain_first, gain_second]),
        jnp.stack([qkv_first, qkv_second]),
        jnp.stack([proj_first, proj_second]),
    )
    return (point_grad, gain_grad, qkv_grad, proj_grad)


def solution(mesh):
    return jax.shard_map(
        per_device,
        mesh=mesh,
        in_specs=(
            P(("gx", "gy"), None),
            P(("gx", "gy"), None),
            P(),
            P(),
            P(),
            P(("gx", "gy"), None),
            P(("gx", "gy"), None),
        ),
        out_specs=(
            P(("gx", "gy"), None),
            P(None, ("gx", "gy")),
            P(None, ("gx", "gy"), None),
            P(None, ("gx", "gy"), None),
        ),
        check_vma=False,
    )
```

profile of v0, /device:TPU:0, one launch (start us, length us, event | category | flops | bytes accessed | tf_op | source)
XLA Modules:
  0.0 660.8 jit_solution(6267822907081232121)
XLA Ops:
  10.8 7.3 %all-to-all-start = ((s32[8,1,2]{2,1,0:T(1,128)}), s32[8,1,2]{2,1,0:T(1,128)S(1)}, u32[]{:S(2)}, u32[]{:S(2)}) async-start(s32[8,1,2]{2,1,0:T(1,128)} %copy.107), calls=%async_computation | async-start | bytes 8192 | tf_op jit(solution)/shard_map/all_to_all | solution.py:83
  19.5 5.9 fusion.74
  29.1 6.1 all-to-all-start.3
  42.7 6.6 all-to-all-done.3
  58.7 4.2 fusion.6
  63.9 6.7 %multiply_reduce_fusion.3 = (f32[2,32,128]{2,1,0:T(8,128)S(1)}, f32[2,32,128,128]{2,3,1,0:T(8,128)S(1)}) fusion(f32[2,128,32,16]{1,2,3,0:T(8,128)S(1)} %get-tuple-element.24, f32[2,128,32,16]{1,2,3,0:T(8,128)S(1)} %get-tuple-element.25), kind=kOutput, calls=%fused_computation.24 | convolution fusion | flops 203415552 | bytes 5275648 | tf_op jit(solution)/shard_map/jvp(pihd,pjhd->phij)/dot_general | solution.py:30
  71.9 4.3 convolution_bitcast_fusion.13
  81.3 4.1 all-to-all-start.4
  91.8 9.0 %all-to-all-done.4 = f32[8,2,16,512]{3,2,1,0:T(8,128)} async-done(((f32[8,2,16,512]{3,2,1,0:T(8,128)}), f32[8,2,16,512]{3,2,1,0:T(8,128)}, u32[]{:S(2)}, u32[]{:S(2)}) %all-to-all-start.4) | async-done | bytes 524320 | tf_op jit(solution)/shard_map/all_to_all | solution.py:92
  100.8 4.1 all-to-all-start.2
  115.4 4.5 all-to-all-start.5
  122.4 3.7 convolution_bitcast_fusion.5
  134.4 4.2 fusion.4
  138.8 6.9 %multiply_reduce_fusion.2 = (f32[2,32,128]{2,1,0:T(8,128)S(1)}, f32[2,32,128,128]{2,3,1,0:T(8,128)S(1)}) fusion(f32[2,128,32,16]{1,2,3,0:T(8,128)S(1)} %get-tuple-element.22, f32[2,128,32,16]{1,2,3,0:T(8,128)S(1)} %get-tuple-element.20), kind=kOutput, calls=%fused_computation.23 | convolution fusion | flops 203415552 | bytes 5275648 | tf_op jit(solution)/shard_map/jvp(pihd,pjhd->phij)/dot_general | solution.py:30
  146.8 6.7 %convolution_bitcast_fusion.12 = f32[2,128,1,32,16]{1,4,3,0,2:T(8,128)S(1)} fusion(f32[2,32,128]{2,1,0:T(8,128)S(1)} %fusion.11, f32[2,32,128]{2,1,0:T(8,128)S(1)} %get-tuple-element.38, f32[2,32,128,128]{2,3,1,0:T(8,128)S(1)} %get-tuple-element.39, f32[2,32,16,128]{3,1,2,0:T(8,128)S(1)} %copy-done.22), kind=kOutput, calls=%fused_computation.63 | convolution fusion | flops 204472320 | bytes 5308416 | tf_op jit(solution)/shard_map/transpose(jvp(phij,pjhd->pihd))/dot_general | solution.py:34
  153.5 7.4 %multiply_reduce_fusion.1 = (f32[2,32,128]{2,1,0:T(8,128)S(1)}, f32[2,32,128,128]{2,3,1,0:T(8,128)S(1)}) fusion(f32[2,32,128]{2,1,0:T(8,128)S(1)} %multiply_divide_fusion.1, f32[2,32,128]{2,1,0:T(8,128)S(1)} %get-tuple-element.38, f32[2,32,128,128]{2,3,1,0:T(8,128)S(1)} %get-tuple-element.39, f32[2,128,32,16]{1,2,3,0:T(8,128)S(1)} %get-tuple-element.21, ...), kind=kOutput, calls=%fused_computation.20 | convolution fusion | flops 206561280 | bytes 9535488 | tf_op jit(solution)/shard_map/transpose(jvp(phij,pjhd->pihd))/dot_general | solution.py:34
  162.6 6.7 %convolution_bitcast_fusion.11 = f32[2,128,1,32,16]{1,4,3,0,2:T(8,128)S(1)} fusion(f32[2,32,128,128]{2,3,1,0:T(8,128)S(1)} %multiply_multiply_fusion.1, f32[2,128,32,16]{1,2,3,0:T(8,128)S(1)} %get-tuple-element.20), kind=kOutput, calls=%fused_computation.62 | convolution fusion | flops 201326592 | bytes 5242880 | tf_op jit(solution)/shard_map/transpose(jvp(pihd,pjhd->phij))/dot_general | solution.py:30
  169.3 3.8 convolution_bitcast_fusion.10
  174.9 7.2 %multiply_reduce_fusion.4 = (f32[512]{0:T(512)S(1)}, f32[256]{0:T(256)S(1)}, f32[256,512]{1,0:T(8,128)S(1)}) fusion(f32[16,16,512]{2,1,0:T(8,128)S(1)} %copy-done.5, f32[256]{0:T(256)S(1)} %div.126, f32[256]{0:T(256)S(1)} %rsqrt.32, f32[512]{0:T(512)S(1)} %bitcast.289, f32[2,512,1536]{2,1,0:T(8,128)} %param.10, f32[192,8,2,128]{3,2,1,0:T(2,128)S(1)} %bitcast.256), kind=kOutput, calls=%fused_computation.84 | convolution fusion | flops 2416835840 | bytes 5774336 | tf_op jit(solution)/shard_map/transpose(jvp())/dot_general | solution.py:25
  185.5 11.9 %all_to_all.55 = f32[4,4,16,512]{3,2,1,0:T(8,128)} all-to-all(f32[4,4,16,512]{3,2,1,0:T(8,128)S(1)} %bitcast.270), channel_id=1, replica_groups=mesh['gx'=4,'gy'=8] {'gx'}, dimensions={0} | all-to-all | bytes 1048576 | tf_op jit(solution)/shard_map/all_to_all | solution.py:111
  206.6 5.9 convolution_bitcast_fusion.6
  214.9 5.7 all-to-all-done.7
  223.8 9.0 %convolution_bitcast_fusion.9 = f32[2,128,1,32,16]{1,4,3,0,2:T(8,128)S(1)} fusion(f32[2,32,128]{2,1,0:T(8,128)S(1)} %fusion.10, f32[2,32,128]{2,1,0:T(8,128)S(1)} %get-tuple-element.36, f32[2,32,128,128]{2,3,1,0:T(8,128)} %copy-done, f32[2,32,16,128]{3,1,2,0:T(8,128)S(1)} %convolution_bitcast_fusion.4), kind=kOutput, calls=%fused_computation.60 | convolution fusion | flops 204472320 | bytes 5308416 | tf_op jit(solution)/shard_map/transpose(jvp(phij,pjhd->pihd))/dot_general | solution.py:34
  232.9 7.0 %multiply_reduce_fusion = (f32[2,32,128]{2,1,0:T(8,128)S(1)}, f32[2,32,128,128]{2,3,1,0:T(8,128)S(1)}) fusion(f32[2,32,128]{2,1,0:T(8,128)S(1)} %multiply_divide_fusion, f32[2,32,128]{2,1,0:T(8,128)S(1)} %get-tuple-element.36, f32[2,32,128,128]{2,3,1,0:T(8,128)S(1)} %copy-done.1, f32[2,128,32,16]{1,2,3,0:T(8,128)S(1)} %copy-done.21, ...), kind=kOutput, calls=%fused_computation.18 | convolution fusion | flops 206561280 | bytes 9535488 | tf_op jit(solution)/shard_map/transpose(jvp(phij,pjhd->pihd))/dot_general | solution.py:34
  241.6 6.9 %convolution_bitcast_fusion.8 = f32[2,128,1,32,16]{1,4,3,0,2:T(8,128)S(1)} fusion(f32[2,32,128,128]{2,3,1,0:T(8,128)S(1)} %multiply_multiply_fusion, f32[2,128,32,16]{1,2,3,0:T(8,128)S(1)} %copy-done.15), kind=kOutput, calls=%fused_computation.59 | convolution fusion | flops 201326592 | bytes 5242880 | tf_op jit(solution)/shard_map/transpose(jvp(pihd,pjhd->phij))/dot_general | solution.py:30
  248.5 3.8 convolution_bitcast_fusion.7
  255.9 6.3 multiply_reduce_fusion.5
  266.5 6.4 convolution_bitcast_fusion
  272.9 5.2 convolution_bitcast_fusion.1
  289.7 107.6 %reduce-scatter.10.cloned.1.call-done = f32[16,2]{1,0:T(8,128)} async-done(((f32[512,2]{1,0:T(8,128)}), f32[16,2]{1,0:T(8,128)}) %reduce-scatter.10.cloned.1.call-update) | async-done | bytes 144
  400.0 136.0 %reduce-scatter.8.cloned.1.call-done = f32[2,16,512]{2,1,0:T(8,128)} async-done(((f32[2,512,512]{2,1,0:T(8,128)}), f32[2,16,512]{2,1,0:T(8,128)}) %reduce-scatter.8.cloned.1.call-update) | async-done | bytes 65552 | tf_op jit(solution)/shard_map/reduce_scatter | solution.py:119
  536.0 118.1 %reduce-scatter.6.cloned.1.call-done = f32[2,16,1536]{2,1,0:T(8,128)} async-done(((f32[2,512,1536]{2,1,0:T(8,128)}), f32[2,16,1536]{2,1,0:T(8,128)}) %reduce-scatter.6.cloned.1.call-update) | async-done | bytes 196624 | tf_op jit(solution)/shard_map/reduce_scatter | solution.py:118
  (167 shorter events, 106.7 us)
Async XLA Ops:
  10.8 18.3 %all-to-all-start = ((s32[8,1,2]{2,1,0:T(1,128)}), s32[8,1,2]{2,1,0:T(1,128)S(1)}, u32[]{:S(2)}, u32[]{:S(2)}) async-start(s32[8,1,2]{2,1,0:T(1,128)} %copy.107), calls=%async_computation | async-start | bytes 8192 | tf_op jit(solution)/shard_map/all_to_all | solution.py:83
  19.5 6.8 %copy-start.23 = (f32[256,512]{1,0:T(8,128)S(1)}, f32[256,512]{1,0:T(8,128)}, u32[]{:S(2)}) copy-start(f32[256,512]{1,0:T(8,128)} %param.7) | copy-start | bytes 1572868
  29.1 12.2 %copy-start.24 = (f32[2,512]{1,0:T(2,128)S(1)}, f32[2,512]{1,0:T(2,128)}, u32[]{:S(2)}) copy-start(f32[2,512]{1,0:T(2,128)} %param.9) | copy-start | bytes 12292
  29.1 20.2 %all-to-all-start.3 = ((f32[8,2,16,512]{3,2,1,0:T(8,128)}), f32[8,2,16,512]{3,2,1,0:T(8,128)}, u32[]{:S(2)}, u32[]{:S(2)}) async-start(f32[8,2,16,512]{3,2,1,0:T(8,128)} %scatter_fusion.3), calls=%async_computation.3 | async-start | bytes 1048576 | tf_op jit(solution)/shard_map/all_to_all | solution.py:82
  49.3 32.0 %all-to-all-start.1 = ((s32[4,1,4]{2,1,0:T(1,128)}), s32[4,1,4]{2,1,0:T(1,128)S(1)}, u32[]{:S(2)}, u32[]{:S(2)}) async-start(s32[4,1,4]{2,1,0:T(1,128)} %bitcast.14), calls=%async_computation.1 | async-start | bytes 4096 | tf_op jit(solution)/shard_map/all_to_all | solution.py:102
  58.7 4.3 copy-start.9
  63.1 7.5 %copy-start.14 = (f32[2,128,32,16]{1,2,3,0:T(8,128)}, f32[2,128,32,16]{1,2,3,0:T(8,128)S(1)}, u32[]{:S(2)}) copy-start(f32[2,128,32,16]{1,2,3,0:T(8,128)S(1)} %get-tuple-element.25) | copy-start | bytes 1572868
  63.1 8.8 %copy-start.20 = (f32[2,128,32,16]{1,2,3,0:T(8,128)}, f32[2,128,32,16]{1,2,3,0:T(8,128)S(1)}, u32[]{:S(2)}) copy-start(f32[2,128,32,16]{1,2,3,0:T(8,128)S(1)} %get-tuple-element.23) | copy-start | bytes 1572868
  70.6 5.6 copy-start
  71.9 4.7 copy-start.3
  71.9 4.7 copy-start.16
  81.3 19.5 %all-to-all-start.4 = ((f32[8,2,16,512]{3,2,1,0:T(8,128)}), f32[8,2,16,512]{3,2,1,0:T(8,128)}, u32[]{:S(2)}, u32[]{:S(2)}) async-start(f32[8,2,16,512]{3,2,1,0:T(8,128)} %bitcast.43), calls=%async_computation.4 | async-start | bytes 1048576 | tf_op jit(solution)/shard_map/all_to_all | solution.py:92
  100.8 14.6 %all-to-all-start.2 = ((f32[4,4,16,512]{3,2,1,0:T(8,128)}), f32[4,4,16,512]{3,2,1,0:T(8,128)}, u32[]{:S(2)}, u32[]{:S(2)}) async-start(f32[4,4,16,512]{3,2,1,0:T(8,128)} %scatter_fusion.2), calls=%async_computation.2 | async-start | bytes 1048576 | tf_op jit(solution)/shard_map/all_to_all | solution.py:101
  115.4 13.0 %all-to-all-start.5 = ((f32[4,4,16,512]{3,2,1,0:T(8,128)}), f32[4,4,16,512]{3,2,1,0:T(8,128)}, u32[]{:S(2)}, u32[]{:S(2)}) async-start(f32[4,4,16,512]{3,2,1,0:T(8,128)} %scatter_fusion.5), calls=%async_computation.5 | async-start | bytes 1048576 | tf_op jit(solution)/shard_map/all_to_all | solution.py:101
  134.4 4.3 copy-start.11
  138.8 8.0 %copy-start.22 = (f32[2,32,16,128]{3,1,2,0:T(8,128)S(1)}, f32[2,32,16,128]{3,1,2,0:T(8,128)}, u32[]{:S(2)}) copy-start(f32[2,32,16,128]{3,1,2,0:T(8,128)} %convolution_bitcast_fusion.5) | copy-start | bytes 1572868
  145.7 15.2 %copy-start.2 = (f32[2,32,128,128]{2,3,1,0:T(8,128)}, f32[2,32,128,128]{2,3,1,0:T(8,128)S(1)}, u32[]{:S(2)}) copy-start(f32[2,32,128,128]{2,3,1,0:T(8,128)S(1)} %get-tuple-element.39) | copy-start | bytes 12582916
  174.8 7.6 %copy-start.8 = (f32[16,16,512]{2,1,0:T(8,128)S(1)}, f32[16,16,512]{2,1,0:T(8,128)}, u32[]{:S(2)}) copy-start(f32[16,16,512]{2,1,0:T(8,128)} %gather_fusion) | copy-start | bytes 1572868
  202.7 17.8 %all-to-all-start.7 = ((f32[8,2,16,512]{3,2,1,0:T(8,128)}), f32[8,2,16,512]{3,2,1,0:T(8,128)S(1)}, u32[]{:S(2)}, u32[]{:S(2)}) async-start(f32[8,2,16,512]{3,2,1,0:T(8,128)} %scatter_fusion.7), calls=%async_computation.7 | async-start | bytes 1048576 | tf_op jit(solution)/shard_map/all_to_all | solution.py:82
  206.3 190.9 %reduce-scatter.10.cloned.1.call-start = ((), (), s32[]{:S(2)}) async-start(), calls=%async_computation.14 | async-start | bytes 270336
  223.8 9.0 %copy-start.1 = (f32[2,32,128,128]{2,3,1,0:T(8,128)S(1)}, f32[2,32,128,128]{2,3,1,0:T(8,128)}, u32[]{:S(2)}) copy-start(f32[2,32,128,128]{2,3,1,0:T(8,128)} %copy-done) | copy-start | bytes 12582916
  223.8 9.0 %copy-start.21 = (f32[2,128,32,16]{1,2,3,0:T(8,128)S(1)}, f32[2,128,32,16]{1,2,3,0:T(8,128)}, u32[]{:S(2)}) copy-start(f32[2,128,32,16]{1,2,3,0:T(8,128)} %copy-done.20) | copy-start | bytes 1572868
  241.6 6.9 %copy-start.13 = (f32[2,128,32,16]{1,2,3,0:T(8,128)S(1)}, f32[2,128,32,16]{1,2,3,0:T(8,128)}, u32[]{:S(2)}) copy-start(f32[2,128,32,16]{1,2,3,0:T(8,128)} %copy-done.12) | copy-start | bytes 1572868
  241.6 10.7 %copy-start.18 = (f32[2,128,32,16]{1,0,3,2:T(2,128)S(1)}, f32[2,128,32,16]{1,0,3,2:T(2,128)}, u32[]{:S(2)}) copy-start(f32[2,128,32,16]{1,0,3,2:T(2,128)} %copy-done.17) | copy-start | bytes 1572868
  248.5 7.3 %slice-start = ((s8[6291456]{0:T(1024)(128)(4,1)}), s8[2097152]{0:T(1024)(128)(4,1)S(1)}, s32[]{:S(2)}) async-start(s8[6291456]{0:T(1024)(128)(4,1)} %bitcast.254), calls=%async_computation.15 | async-start | bytes 4194304
  252.3 3.5 slice-start.1
  255.8 6.4 copy-start.6
  263.1 272.9 %reduce-scatter.8.cloned.1.call-start = ((), (), s32[]{:S(2)}) async-start(), calls=%async_computation.13 | async-start | bytes 2162688 | tf_op jit(solution)/shard_map/reduce_scatter | solution.py:119
  266.2 6.7 %copy-start.10 = (f32[16,16,512]{2,1,0:T(8,128)S(1)}, f32[16,16,512]{2,1,0:T(8,128)}, u32[]{:S(2)}) copy-start(f32[16,16,512]{2,1,0:T(8,128)} %copy-done.9) | copy-start | bytes 1572868
  266.2 387.9 %reduce-scatter.6.cloned.1.call-start = ((), (), s32[]{:S(2)}) async-start(), calls=%async_computation.12 | async-start | bytes 6488064 | tf_op jit(solution)/shard_map/reduce_scatter | solution.py:118
  266.5 6.4 copy-start.7
  286.1 112.5 %all-to-all-start.8 = ((f32[8,2,16,512]{3,2,1,0:T(8,128)}), f32[8,2,16,512]{3,2,1,0:T(8,128)S(1)}, u32[]{:S(2)}, u32[]{:S(2)}) async-start(f32[8,2,16,512]{3,2,1,0:T(8,128)} %bitcast.82), calls=%async_computation.8 | async-start | bytes 1048576 | tf_op jit(solution)/shard_map/all_to_all | solution.py:92
  (6 other events, 10.0 us)
Sparse Core Ops, SparseCore 0:
  263.2 134.0 reduce-scatter.9
  400.1 135.8 reduce-scatter.7
  542.2 111.8 reduce-scatter.5
where the time goes:
time: 666 us; the launch traced here: 661 us
  waiting for transfers between devices  385 us (58%)
  matrix products  120 us (18%)
  local copies, waits for them, and re-layouts  65.6 us (10%)
  starting transfers between devices  37.2 us (6%)
  other arithmetic  25.9 us (4%)
  between operations  14.8 us (2%)
  blocking collectives  11.9 us (2%)
    reduce_scatter x1, waiting for transfers between devices, reduce_grads(): lax.psum_scatter(proj_part, ('gx', 'gy'), scatter_dimension=1, tiled=True)  136 us
    reduce_scatter x1, waiting for transfers between devices, reduce_grads(): lax.psum_scatter(qkv_part, ('gx', 'gy'), scatter_dimension=1, tiled=True)  118 us
    unnamed x4, waiting for transfers between devices  108 us
    dot_general x6, matrix products, attend_block(): jnp.einsum('phij,pjhd->pihd', attention, value_rows, precision=exact_mode)  40.2 us
    dot_general x6, matrix products, attend_block(): jnp.einsum('pihd,pjhd->phij', queries, key_rows, precision=exact_mode)  34.9 us
    dot_general x6, matrix products, attend_block(): projected = jnp.dot(normed, qkv_weight, precision=exact_mode)  33.6 us
  transfers between devices with their start and end apart: 11, of which 7 were waited for; matrix products, arithmetic and copies ran while one was open for 15% of the time, Pallas kernels for 0%

commit v1 on v0

--- a/solution.py
+++ b/solution.py
@@ -12,6 +12,8 @@
 
 
 exact_mode = lax.Precision.HIGHEST
+fast_mode = lax.Precision.HIGH
+mesh_axes = ("gx", "gy")
 epsilon = 1e-05
 
 
@@ -31,8 +33,8 @@
         1.0 / math.sqrt(head_dim)
     )
     attention = jax.nn.softmax(scores, axis=-1)
-    mixed_rows = jnp.einsum("phij,pjhd->pihd", attention, value_rows, precision=exact_mode)
-    return rows_in + jnp.dot(mixed_rows.reshape(row_count, D), proj_weight, precision=exact_mode)
+    mixed_rows = jnp.einsum("phij,pjhd->pihd", attention, value_rows, precision=fast_mode)
+    return rows_in + jnp.dot(mixed_rows.reshape(row_count, D), proj_weight, precision=fast_mode)
 
 
 def occupancy(owner_index):
@@ -112,12 +114,45 @@
     return received[route[:, 0] // lax.axis_size("gy"), occur].reshape(-1, rows_in.shape[1])
 
 
+def halve_and_sum(part, bit_order, device_count):
+    bit_count = device_count.bit_length() - 1
+    me = lax.axis_index(mesh_axes)
+    shaped = part.reshape((2,) * bit_count + (part.shape[0] // device_count, part.shape[1]))
+    left = list(range(bit_count))
+    for bit in bit_order:
+        at = left.index(bit_count - 1 - bit)
+        left.pop(at)
+        mine = (me >> bit) & 1
+        sent = lax.dynamic_index_in_dim(shaped, 1 - mine, at, keepdims=False)
+        kept = lax.dynamic_index_in_dim(shaped, mine, at, keepdims=False)
+        swaps = [(i, i ^ (1 << bit)) for i in range(device_count)]
+        shaped = kept + lax.ppermute(sent, mesh_axes, swaps)
+    return shaped
+
+
+def bit_orders(mesh_gx, mesh_gy):
+    gy_bits = mesh_gy.bit_length() - 1
+    gx_bits = mesh_gx.bit_length() - 1
+    core = gy_bits
+    y_bits = list(range(gy_bits + 1, gy_bits + gx_bits))[::-1]
+    low = [0]
+    high = list(range(1, gy_bits))[::-1]
+    return ([core] + y_bits + low + high, [core] + low + high + y_bits, [core] + high + y_bits + low)
+
+
 def reduce_grads(gain_part, qkv_part, proj_part):
-    return (
-        lax.psum_scatter(gain_part, ("gx", "gy"), scatter_dimension=1, tiled=True),
-        lax.psum_scatter(qkv_part, ("gx", "gy"), scatter_dimension=1, tiled=True),
-        lax.psum_scatter(proj_part, ("gx", "gy"), scatter_dimension=1, tiled=True),
-    )
+    mesh_gx, mesh_gy = lax.axis_size("gx"), lax.axis_size("gy")
+    device_count = mesh_gx * mesh_gy
+    width = qkv_part.shape[1]
+    half = width // 2
+    orders = bit_orders(mesh_gx, mesh_gy)
+    gain_wide = jnp.broadcast_to(gain_part[:, None], (gain_part.shape[0], 128))
+    proj_wide = jnp.concatenate([proj_part, gain_wide], axis=1)
+    first = halve_and_sum(qkv_part[:, :half], orders[0], device_count)
+    second = halve_and_sum(qkv_part[:, half:], orders[1], device_count)
+    third = halve_and_sum(proj_wide, orders[2], device_count)
+    qkv_sum = jnp.concatenate([first, second], axis=1)
+    return (third[:, -1], qkv_sum, third[:, : proj_part.shape[1]])
 
 
 def per_device(points, upstream, gains, w_qkv, w_proj, z_route, h_route):
@@ -128,15 +163,13 @@
     grad_curve, unused_source, unused_occur = to_hilbert(upstream, h_route)
     second_out, pull_second = jax.vjp(attend_block, curve_second, gains[1], w_qkv[1], w_proj[1])
     grad_second, gain_second, qkv_second, proj_second = pull_second(grad_curve)
+    sums_second = reduce_grads(gain_second, qkv_second, proj_second)
     grad_middle = from_hilbert(grad_second, h_source, h_occur, h_route)
     middle_curve, unused_again, unused_spots = to_zorder(grad_middle, z_route)
     grad_first, gain_first, qkv_first, proj_first = pull_first(middle_curve)
     point_grad = from_zorder(grad_first, z_source, z_occur, z_route)
-    gain_grad, qkv_grad, proj_grad = reduce_grads(
-        jnp.stack([gain_first, gain_second]),
-        jnp.stack([qkv_first, qkv_second]),
-        jnp.stack([proj_first, proj_second]),
-    )
+    sums_first = reduce_grads(gain_first, qkv_first, proj_first)
+    gain_grad, qkv_grad, proj_grad = (jnp.stack(pair) for pair in zip(sums_first, sums_second))
     return (point_grad, gain_grad, qkv_grad, proj_grad)
 
 

time: 666 us -> 399 us (0.60)
  waiting for transfers between devices: 385 us -> 98.9 us
  starting transfers between devices: 37.2 us -> 70.5 us
  local copies, waits for them, and re-layouts: 65.6 us -> 88 us
  matrix products: 120 us -> 98.4 us
  between operations: 14.8 us -> 2.22 us
  blocking collectives: 11.9 us -> 0 us
  other arithmetic: 25.9 us -> 35.1 us
    reduce_scatter x2 -> x0, waiting for transfers between devices: 254 us -> none  [the longest x1 136 us: reduce_grads(): lax.psum_scatter(proj_part, ('gx', 'gy'), scatter_dimension=1, tiled=True)]
    unnamed x4 -> x0, waiting for transfers between devices: 108 us -> none
    ppermute x0 -> x30, waiting for transfers between devices: none -> 74.9 us  [halve_and_sum(): shaped = kept + lax.ppermute(sent, mesh_axes, swaps)]
    ppermute x0 -> x30, starting transfers between devices: none -> 31.6 us  [halve_and_sum(): shaped = kept + lax.ppermute(sent, mesh_axes, swaps)]
    dot_general x11, matrix products: 51.8 us -> 30.5 us  [the longest x6 24.1 us: attend_block(): jnp.einsum('phij,pjhd->pihd', attention, value_rows, precision=fast_mode)]
    all_to_all x1 -> x0, blocking collectives: 11.9 us -> none  [from_hilbert(): lax.all_to_all(buffer, 'gx', split_axis=0, concat_axis=0, tiled=True)]
    add x0 -> x30, other arithmetic: none -> 11.1 us  [halve_and_sum(): shaped = kept + lax.ppermute(sent, mesh_axes, swaps)]
    squeeze x0 -> x28, local copies, waits for them, and re-layouts: none -> 9.27 us  [halve_and_sum(): sent = lax.dynamic_index_in_dim(shaped, 1 - mine, at, keepdims=False)]
  transfers between devices with their start and end apart: 11 -> 39, of which waited for: 7 -> 20; matrix products, arithmetic and copies ran while one was open for 15% -> 33% of each run, Pallas kernels for 0% -> 0%
where the time goes in v1:
time: 399 us; the launch traced here: 393 us
  waiting for transfers between devices  98.9 us (25%)
  matrix products  98.4 us (25%)
  local copies, waits for them, and re-layouts  88 us (22%)
  starting transfers between devices  70.5 us (18%)
  other arithmetic  35.1 us (9%)
    ppermute x30, waiting for transfers between devices, halve_and_sum(): shaped = kept + lax.ppermute(sent, mesh_axes, swaps)  74.9 us
    dot_general x6, matrix products, attend_block(): jnp.einsum('pihd,pjhd->phij', queries, key_rows, precision=exact_mode)  35.3 us
    dot_general x6, matrix products, attend_block(): projected = jnp.dot(normed, qkv_weight, precision=exact_mode)  32.6 us
    ppermute x30, starting transfers between devices, halve_and_sum(): shaped = kept + lax.ppermute(sent, mesh_axes, swaps)  31.6 us
    dot_general x6, matrix products, attend_block(): jnp.einsum('phij,pjhd->pihd', attention, value_rows, precision=fast_mode)  24.1 us
    scatter x4, local copies, waits for them, and re-layouts, spread_out(): buffer = jnp.zeros((peer_count, per_peer) + segments.shape[1:], rows_in.d...  11.7 us
    add x30, other arithmetic, halve_and_sum(): shaped = kept + lax.ppermute(sent, mesh_axes, swaps)  11.1 us
    all_to_all x2, waiting for transfers between devices, from_zorder(): lax.all_to_all(buffer, 'gy', split_axis=0, concat_axis=0, tiled=True)  10.7 us
  transfers between devices with their start and end apart: 39, of which 20 were waited for; matrix products, arithmetic and copies ran while one was open for 33% of the time, Pallas kernels for 0%

profile of v1, /device:TPU:0, one launch (start us, length us, event | category | flops | bytes accessed | tf_op | source)
XLA Modules:
  0.0 393.0 jit_solution(8080548193078252769)
XLA Ops:
  5.8 4.3 %all-to-all-start.1 = ((s32[4,1,4]{2,1,0:T(1,128)}), s32[4,1,4]{2,1,0:T(1,128)S(1)}, u32[]{:S(2)}, u32[]{:S(2)}) async-start(s32[4,1,4]{2,1,0:T(1,128)} %bitcast.14), calls=%async_computation.1 | async-start | bytes 4096 | tf_op jit(solution)/shard_map/all_to_all | solution.py:104
  13.8 6.2 %all-to-all-start = ((s32[8,1,2]{2,1,0:T(1,128)}), s32[8,1,2]{2,1,0:T(1,128)S(1)}, u32[]{:S(2)}, u32[]{:S(2)}) async-start(s32[8,1,2]{2,1,0:T(1,128)} %copy.160), calls=%async_computation | async-start | bytes 8192 | tf_op jit(solution)/shard_map/all_to_all | solution.py:85
  26.4 4.1 %all-to-all-start.3 = ((f32[8,2,16,512]{3,2,1,0:T(8,128)}), f32[8,2,16,512]{3,2,1,0:T(8,128)}, u32[]{:S(2)}, u32[]{:S(2)}) async-start(f32[8,2,16,512]{3,2,1,0:T(8,128)} %scatter_fusion.3), calls=%async_computation.3 | async-start | bytes 1048576 | tf_op jit(solution)/shard_map/all_to_all | solution.py:84
  30.6 5.9 %fusion.78 = (f32[1,512,1536]{2,1,0:T(8,128)}, f32[1,512,1536]{2,1,0:T(8,128)}) fusion(f32[2,512,1536]{2,1,0:T(8,128)} %param.10), kind=kLoop, calls=%fused_computation.258 | loop fusion | bytes 12582912 | tf_op jit(solution)/shard_map/slice | solution.py:164
  50.6 4.2 %fusion.6 = f32[2,128,3,32,16]{1,3,4,2,0:T(8,128)S(1)} fusion(f32[2,128,512,1,1]{2,1,4,3,0:T(8,128)S(1)} %bitcast.400, f32[3,32,16,512]{3,2,1,0:T(8,128)S(1)} %bitcast.378), kind=kOutput, calls=%fused_computation.30 | convolution fusion | flops 2415919104 | bytes 5242880 | tf_op jit(solution)/shard_map/jvp()/dot_general | solution.py:27
  55.8 6.7 %multiply_reduce_fusion.3 = (f32[2,32,128]{2,1,0:T(8,128)S(1)}, f32[2,32,128,128]{2,3,1,0:T(8,128)S(1)}) fusion(f32[2,128,32,16]{1,2,3,0:T(8,128)S(1)} %get-tuple-element.32, f32[2,128,32,16]{1,2,3,0:T(8,128)S(1)} %get-tuple-element.33), kind=kOutput, calls=%fused_computation.23 | convolution fusion | flops 203415552 | bytes 5275648 | tf_op jit(solution)/shard_map/jvp(pihd,pjhd->phij)/dot_general | solution.py:32
  70.8 3.7 all-to-all-start.4
  78.0 10.7 %all-to-all-done.4 = f32[8,2,16,512]{3,2,1,0:T(8,128)S(1)} async-done(((f32[8,2,16,512]{3,2,1,0:T(8,128)}), f32[8,2,16,512]{3,2,1,0:T(8,128)S(1)}, u32[]{:S(2)}, u32[]{:S(2)}) %all-to-all-start.4) | async-done | bytes 524320 | tf_op jit(solution)/shard_map/all_to_all | solution.py:94
  88.8 4.1 %all-to-all-start.2 = ((f32[4,4,16,512]{3,2,1,0:T(8,128)}), f32[4,4,16,512]{3,2,1,0:T(8,128)}, u32[]{:S(2)}, u32[]{:S(2)}) async-start(f32[4,4,16,512]{3,2,1,0:T(8,128)} %scatter_fusion.2), calls=%async_computation.2 | async-start | bytes 1048576 | tf_op jit(solution)/shard_map/all_to_all | solution.py:103
  104.9 4.6 %all-to-all-start.5 = ((f32[4,4,16,512]{3,2,1,0:T(8,128)}), f32[4,4,16,512]{3,2,1,0:T(8,128)}, u32[]{:S(2)}, u32[]{:S(2)}) async-start(f32[4,4,16,512]{3,2,1,0:T(8,128)} %scatter_fusion.5), calls=%async_computation.5 | async-start | bytes 1048576 | tf_op jit(solution)/shard_map/all_to_all | solution.py:103
  124.0 4.2 %fusion.4 = f32[2,128,3,32,16]{1,3,4,2,0:T(8,128)S(1)} fusion(f32[2,128,512,1,1]{2,1,4,3,0:T(8,128)S(1)} %bitcast.402, f32[3,32,16,512]{3,2,1,0:T(8,128)S(1)} %bitcast.377), kind=kOutput, calls=%fused_computation.28 | convolution fusion | flops 2415919104 | bytes 5242880 | tf_op jit(solution)/shard_map/jvp()/dot_general | solution.py:27
  128.4 6.9 %multiply_reduce_fusion.2 = (f32[2,32,128]{2,1,0:T(8,128)S(1)}, f32[2,32,128,128]{2,3,1,0:T(8,128)S(1)}) fusion(f32[2,128,32,16]{1,2,3,0:T(8,128)S(1)} %get-tuple-element.30, f32[2,128,32,16]{1,2,3,0:T(8,128)S(1)} %get-tuple-element.28), kind=kOutput, calls=%fused_computation.22 | convolution fusion | flops 203415552 | bytes 5275648 | tf_op jit(solution)/shard_map/jvp(pihd,pjhd->phij)/dot_general | solution.py:32
  139.7 3.7 multiply_reduce_fusion.1
  145.2 7.1 %convolution_bitcast_fusion.7 = f32[2,128,1,32,16]{1,4,3,0,2:T(8,128)S(1)} fusion(f32[2,32,128,128]{2,3,1,0:T(8,128)S(1)} %multiply_multiply_fusion.1, f32[2,128,32,16]{1,2,3,0:T(8,128)S(1)} %get-tuple-element.28), kind=kOutput, calls=%fused_computation.60 | convolution fusion | flops 201326592 | bytes 5242880 | tf_op jit(solution)/shard_map/transpose(jvp(pihd,pjhd->phij))/dot_general | solution.py:32
  152.3 3.8 convolution_bitcast_fusion.6
  156.2 5.3 %convolution_bitcast_fusion.2 = f32[2,128,32,16]{1,3,2,0:T(8,128)} fusion(f32[2,32,128]{2,1,0:T(8,128)S(1)} %fusion.11, f32[2,32,128]{2,1,0:T(8,128)S(1)} %get-tuple-element.46, f32[2,32,128,128]{2,3,1,0:T(8,128)} %copy-done.2, f32[2,128,32,16]{1,2,3,0:T(8,128)S(1)} %get-tuple-element.29), kind=kOutput, calls=%fused_computation.55 | convolution fusion | flops 103809024 | bytes 5308416 | tf_op jit(solution)/shard_map/jvp(phij,pjhd->pihd)/dot_general | solution.py:36
  163.0 7.4 %multiply_reduce_fusion.4 = (f32[512]{0:T(512)S(1)}, f32[256]{0:T(256)S(1)}, f32[256,512]{1,0:T(8,128)S(1)}) fusion(f32[16,16,512]{2,1,0:T(8,128)S(1)} %copy-done.5, f32[256]{0:T(256)S(1)} %div.126, f32[256]{0:T(256)S(1)} %rsqrt.32, f32[512]{0:T(512)S(1)} %bitcast.424, f32[2,512,1536]{2,1,0:T(8,128)} %param.10, f32[192,8,2,128]{3,2,1,0:T(2,128)S(1)} %bitcast.382), kind=kOutput, calls=%fused_computation.96 | convolution fusion | flops 2416835840 | bytes 5774336 | tf_op jit(solution)/shard_map/transpose(jvp())/dot_general | solution.py:27
  178.9 5.2 %fusion.15 = f32[512,1536]{1,0:T(8,128)S(1)} fusion(f32[256,512]{1,0:T(8,128)S(1)} %bitcast.403, f32[192,8,2,128]{3,2,1,0:T(2,128)S(1)} %bitcast.383), kind=kOutput, calls=%fused_computation.41 | convolution fusion | flops 2415919104 | bytes 5242880 | tf_op jit(solution)/shard_map/transpose(jvp())/dot_general | solution.py:27
  191.7 4.2 %all-to-all-start.6 = ((f32[4,4,16,512]{3,2,1,0:T(8,128)}), f32[4,4,16,512]{3,2,1,0:T(8,128)}, u32[]{:S(2)}, u32[]{:S(2)}) async-start(f32[4,4,16,512]{3,2,1,0:T(8,128)} %bitcast.406), calls=%async_computation.6 | async-start | bytes 1048576 | tf_op jit(solution)/shard_map/all_to_all | solution.py:113
  200.1 4.6 %all-to-all-done.6 = f32[4,4,16,512]{3,2,1,0:T(8,128)} async-done(((f32[4,4,16,512]{3,2,1,0:T(8,128)}), f32[4,4,16,512]{3,2,1,0:T(8,128)}, u32[]{:S(2)}, u32[]{:S(2)}) %all-to-all-start.6) | async-done | bytes 524320 | tf_op jit(solution)/shard_map/all_to_all | solution.py:113
  219.7 22.3 %collective-permute-done.6 = f32[2,2,2,16,640]{4,3,2,1,0:T(8,128)S(1)} collective-permute-done((f32[2,2,2,16,640]{4,3,2,1,0:T(8,128)S(1)}, f32[2,2,2,16,640]{4,3,2,1,0:T(8,128)S(1)}, u32[]{:S(2)}, u32[]{:S(2)}) %collective-permute-start.6) | collective-permute-done | bytes 327712 | tf_op jit(solution)/shard_map/ppermute | solution.py:129
  250.6 5.0 %collective-permute-done.26 = f32[2,2,2,16,768]{4,3,2,1,0:T(8,128)S(1)} collective-permute-done((f32[2,2,2,16,768]{4,3,2,1,0:T(8,128)S(1)}, f32[2,2,2,16,768]{4,3,2,1,0:T(8,128)S(1)}, u32[]{:S(2)}, u32[]{:S(2)}) %collective-permute-start.26) | collective-permute-done | bytes 393248 | tf_op jit(solution)/shard_map/ppermute | solution.py:129
  262.0 5.7 %convolution_bitcast_fusion.5 = f32[2,128,1,32,16]{1,4,3,0,2:T(8,128)S(1)} fusion(f32[2,32,128]{2,1,0:T(8,128)S(1)} %fusion.10, f32[2,32,128]{2,1,0:T(8,128)S(1)} %get-tuple-element.44, f32[2,32,128,128]{2,3,1,0:T(8,128)} %copy-done, f32[2,32,16,128]{3,1,2,0:T(8,128)S(1)} %convolution_bitcast_fusion), kind=kOutput, calls=%fused_computation.58 | convolution fusion | flops 103809024 | bytes 5308416 | tf_op jit(solution)/shard_map/transpose(jvp(phij,pjhd->pihd))/dot_general | solution.py:36
  267.7 3.7 multiply_reduce_fusion
  273.2 6.7 %convolution_bitcast_fusion.4 = f32[2,128,1,32,16]{1,4,3,0,2:T(8,128)S(1)} fusion(f32[2,32,128,128]{2,3,1,0:T(8,128)S(1)} %multiply_multiply_fusion, f32[2,128,32,16]{1,2,3,0:T(8,128)S(1)} %copy-done.16), kind=kOutput, calls=%fused_computation.57 | convolution fusion | flops 201326592 | bytes 5242880 | tf_op jit(solution)/shard_map/transpose(jvp(pihd,pjhd->phij))/dot_general | solution.py:32
  279.9 4.0 %convolution_bitcast_fusion.3 = f32[2,128,1,32,16]{1,4,3,0,2:T(8,128)S(1)} fusion(f32[2,32,128,128]{2,3,1,0:T(8,128)S(1)} %multiply_multiply_fusion, f32[2,128,32,16]{1,2,3,0:T(8,128)S(1)} %copy-done.14), kind=kOutput, calls=%fused_computation.56 | convolution fusion | flops 201326592 | bytes 5242880 | tf_op jit(solution)/shard_map/transpose(jvp(pihd,pjhd->phij))/dot_general | solution.py:32
  286.3 6.1 %multiply_reduce_fusion.5 = (f32[512]{0:T(512)S(1)}, f32[256]{0:T(256)S(1)}, f32[256,512]{1,0:T(8,128)}) fusion(f32[16,16,512]{2,1,0:T(8,128)S(1)} %copy-done.4, f32[256]{0:T(256)S(1)} %copy-done.31, f32[256]{0:T(256)S(1)} %copy-done.32, f32[512]{0:T(512)S(1)} %bitcast.421, f32[2,512,1536]{2,1,0:T(8,128)S(1)} %bitcast.381, f32[192,8,2,128]{3,2,1,0:T(2,128)S(1)} %bitcast.384), kind=kOutput, calls=%fused_computation.97 | convolution fusion | flops 2416835840 | bytes 5774336 | tf_op jit(solution)/shard_map/transpose(jvp())/dot_general | solution.py:27
  298.3 5.4 %fusion.12 = f32[512,1536]{1,0:T(8,128)S(1)} fusion(f32[256,512]{1,0:T(8,128)S(1)} %bitcast.401, f32[192,8,2,128]{3,2,1,0:T(2,128)S(1)} %bitcast.385), kind=kOutput, calls=%fused_computation.38 | convolution fusion | flops 2415919104 | bytes 5242880 | tf_op jit(solution)/shard_map/transpose(jvp())/dot_general | solution.py:27
  311.3 4.0 %all-to-all-start.8 = ((f32[8,2,16,512]{3,2,1,0:T(8,128)}), f32[8,2,16,512]{3,2,1,0:T(8,128)S(1)}, u32[]{:S(2)}, u32[]{:S(2)}) async-start(f32[8,2,16,512]{3,2,1,0:T(8,128)} %bitcast.82), calls=%async_computation.8 | async-start | bytes 1048576 | tf_op jit(solution)/shard_map/all_to_all | solution.py:94
  322.1 12.7 %collective-permute-done.23 = f32[2,16,768]{2,1,0:T(8,128)S(1)} collective-permute-done((f32[2,16,768]{2,1,0:T(8,128)S(1)}, f32[2,16,768]{2,1,0:T(8,128)S(1)}, u32[]{:S(2)}, u32[]{:S(2)}) %collective-permute-start.23) | collective-permute-done | bytes 98336 | tf_op jit(solution)/shard_map/ppermute | solution.py:129
  345.1 11.3 %collective-permute-done.1 = f32[2,2,2,16,640]{4,3,2,1,0:T(8,128)S(1)} collective-permute-done((f32[2,2,2,16,640]{4,3,2,1,0:T(8,128)S(1)}, f32[2,2,2,16,640]{4,3,2,1,0:T(8,128)S(1)}, u32[]{:S(2)}, u32[]{:S(2)}) %collective-permute-start.1) | collective-permute-done | bytes 327712 | tf_op jit(solution)/shard_map/ppermute | solution.py:129
  364.3 6.5 %collective-permute-done.16 = f32[2,2,2,16,768]{4,3,2,1,0:T(8,128)} collective-permute-done((f32[2,2,2,16,768]{4,3,2,1,0:T(8,128)}, f32[2,2,2,16,768]{4,3,2,1,0:T(8,128)}, u32[]{:S(2)}, u32[]{:S(2)}) %collective-permute-start.16) | collective-permute-done | bytes 393248 | tf_op jit(solution)/shard_map/ppermute | solution.py:129
  (320 shorter events, 190.3 us)
Async XLA Ops:
  5.8 8.0 %all-to-all-start.1 = ((s32[4,1,4]{2,1,0:T(1,128)}), s32[4,1,4]{2,1,0:T(1,128)S(1)}, u32[]{:S(2)}, u32[]{:S(2)}) async-start(s32[4,1,4]{2,1,0:T(1,128)} %bitcast.14), calls=%async_computation.1 | async-start | bytes 4096 | tf_op jit(solution)/shard_map/all_to_all | solution.py:104
  13.8 12.6 %all-to-all-start = ((s32[8,1,2]{2,1,0:T(1,128)}), s32[8,1,2]{2,1,0:T(1,128)S(1)}, u32[]{:S(2)}, u32[]{:S(2)}) async-start(s32[8,1,2]{2,1,0:T(1,128)} %copy.160), calls=%async_computation | async-start | bytes 8192 | tf_op jit(solution)/shard_map/all_to_all | solution.py:85
  26.4 18.2 %all-to-all-start.3 = ((f32[8,2,16,512]{3,2,1,0:T(8,128)}), f32[8,2,16,512]{3,2,1,0:T(8,128)}, u32[]{:S(2)}, u32[]{:S(2)}) async-start(f32[8,2,16,512]{3,2,1,0:T(8,128)} %scatter_fusion.3), calls=%async_computation.3 | async-start | bytes 1048576 | tf_op jit(solution)/shard_map/all_to_all | solution.py:84
  70.8 18.0 %all-to-all-start.4 = ((f32[8,2,16,512]{3,2,1,0:T(8,128)}), f32[8,2,16,512]{3,2,1,0:T(8,128)S(1)}, u32[]{:S(2)}, u32[]{:S(2)}) async-start(f32[8,2,16,512]{3,2,1,0:T(8,128)} %bitcast.43), calls=%async_computation.4 | async-start | bytes 1048576 | tf_op jit(solution)/shard_map/all_to_all | solution.py:94
  88.8 16.1 %all-to-all-start.2 = ((f32[4,4,16,512]{3,2,1,0:T(8,128)}), f32[4,4,16,512]{3,2,1,0:T(8,128)}, u32[]{:S(2)}, u32[]{:S(2)}) async-start(f32[4,4,16,512]{3,2,1,0:T(8,128)} %scatter_fusion.2), calls=%async_computation.2 | async-start | bytes 1048576 | tf_op jit(solution)/shard_map/all_to_all | solution.py:103
  104.9 13.0 %all-to-all-start.5 = ((f32[4,4,16,512]{3,2,1,0:T(8,128)}), f32[4,4,16,512]{3,2,1,0:T(8,128)}, u32[]{:S(2)}, u32[]{:S(2)}) async-start(f32[4,4,16,512]{3,2,1,0:T(8,128)} %scatter_fusion.5), calls=%async_computation.5 | async-start | bytes 1048576 | tf_op jit(solution)/shard_map/all_to_all | solution.py:103
  178.9 34.9 %collective-permute-start.5 = (f32[2,2,2,2,16,640]{5,4,3,2,1,0:T(8,128)}, f32[2,2,2,2,16,640]{5,4,3,2,1,0:T(8,128)}, u32[]{:S(2)}, u32[]{:S(2)}) collective-permute-start(f32[2,2,2,2,16,640]{5,4,3,2,1,0:T(8,128)} %dynamic-slice_bitcast_fusion.2), channel_id=1, source_target_pairs={{0,8},{1,9},{2,10},{3,11},{4,12},{5,13},{6,14},{7,15},{8,0},{9,1},... | collective-permute-start | bytes 1966088 | tf_op jit(solution)/shard_map/ppermute | solution.py:129
  186.5 31.5 %collective-permute-start.20 = (f32[2,2,2,2,16,768]{5,4,3,2,1,0:T(8,128)}, f32[2,2,2,2,16,768]{5,4,3,2,1,0:T(8,128)}, u32[]{:S(2)}, u32[]{:S(2)}) collective-permute-start(f32[2,2,2,2,16,768]{5,4,3,2,1,0:T(8,128)} %dynamic-slice_bitcast_fusion), channel_id=1, source_target_pairs={{0,8},{1,9},{2,10},{3,11},{4,12},{5,13},{6,14},{7,15},{8,0},{9,1},... | collective-permute-start | bytes 2359304 | tf_op jit(solution)/shard_map/ppermute | solution.py:129
  191.7 13.0 %all-to-all-start.6 = ((f32[4,4,16,512]{3,2,1,0:T(8,128)}), f32[4,4,16,512]{3,2,1,0:T(8,128)}, u32[]{:S(2)}, u32[]{:S(2)}) async-start(f32[4,4,16,512]{3,2,1,0:T(8,128)} %bitcast.406), calls=%async_computation.6 | async-start | bytes 1048576 | tf_op jit(solution)/shard_map/all_to_all | solution.py:113
  199.7 42.5 %collective-permute-start.25 = (f32[2,2,2,2,16,768]{5,4,2,1,0,3:T(8,128)}, f32[2,2,2,2,16,768]{5,4,2,1,0,3:T(8,128)}, u32[]{:S(2)}, u32[]{:S(2)}) collective-permute-start(f32[2,2,2,2,16,768]{5,4,2,1,0,3:T(8,128)} %bitcast.374), channel_id=1, source_target_pairs={{0,8},{1,9},{2,10},{3,11},{4,12},{5,13},{6,14},{7,15},{8,0},{9,1},... | collective-permute-start | bytes 2359304 | tf_op jit(solution)/shard_map/ppermute | solution.py:129
  210.1 50.0 %all-to-all-start.7 = ((f32[8,2,16,512]{3,2,1,0:T(8,128)}), f32[8,2,16,512]{3,2,1,0:T(8,128)S(1)}, u32[]{:S(2)}, u32[]{:S(2)}) async-start(f32[8,2,16,512]{3,2,1,0:T(8,128)} %scatter_fusion.7), calls=%async_computation.7 | async-start | bytes 1048576 | tf_op jit(solution)/shard_map/all_to_all | solution.py:84
  215.0 27.0 %collective-permute-start.6 = (f32[2,2,2,16,640]{4,3,2,1,0:T(8,128)S(1)}, f32[2,2,2,16,640]{4,3,2,1,0:T(8,128)S(1)}, u32[]{:S(2)}, u32[]{:S(2)}) collective-permute-start(f32[2,2,2,16,640]{4,3,2,1,0:T(8,128)S(1)} %dynamic-slice_bitcast_fusion.8), channel_id=1, source_target_pairs={{0,4},{1,5},{2,6},{3,7},{4,0},{5,1},{6,2},{7,3},{8,12},{9,13},{10,... | collective-permute-start | bytes 983048 | tf_op jit(solution)/shard_map/ppermute | solution.py:129
  219.3 29.1 %collective-permute-start.21 = (f32[2,2,2,16,768]{4,3,2,1,0:T(8,128)S(1)}, f32[2,2,2,16,768]{4,3,2,1,0:T(8,128)S(1)}, u32[]{:S(2)}, u32[]{:S(2)}) collective-permute-start(f32[2,2,2,16,768]{4,3,2,1,0:T(8,128)S(1)} %dynamic-slice_bitcast_fusion.5), channel_id=1, source_target_pairs={{0,16},{1,17},{2,18},{3,19},{4,20},{5,21},{6,22},{7,23},{8,24},{9,... | collective-permute-start | bytes 1179656 | tf_op jit(solution)/shard_map/ppermute | solution.py:129
  242.1 5.4 %collective-permute-start.7 = (f32[2,2,16,640]{3,2,1,0:T(8,128)S(1)}, f32[2,2,16,640]{3,2,1,0:T(8,128)S(1)}, u32[]{:S(2)}, u32[]{:S(2)}) collective-permute-start(f32[2,2,16,640]{3,2,1,0:T(8,128)S(1)} %dynamic-slice_bitcast_fusion.14), channel_id=1, source_target_pairs={{0,2},{1,3},{2,0},{3,1},{4,6},{5,7},{6,4},{7,5},{8,10},{9,11},{10,... | collective-permute-start | bytes 491528 | tf_op jit(solution)/shard_map/ppermute | solution.py:129
  243.6 12.1 %collective-permute-start.26 = (f32[2,2,2,16,768]{4,3,2,1,0:T(8,128)S(1)}, f32[2,2,2,16,768]{4,3,2,1,0:T(8,128)S(1)}, u32[]{:S(2)}, u32[]{:S(2)}) collective-permute-start(f32[2,2,2,16,768]{4,3,2,1,0:T(8,128)S(1)} %dynamic-slice_bitcast_fusion.4), channel_id=1, source_target_pairs={{0,1},{1,0},{2,3},{3,2},{4,5},{5,4},{6,7},{7,6},{8,9},{9,8},{10,11... | collective-permute-start | bytes 1179656 | tf_op jit(solution)/shard_map/ppermute | solution.py:129
  247.5 8.2 %collective-permute-start.8 = (f32[2,16,640]{2,1,0:T(8,128)S(1)}, f32[2,16,640]{2,1,0:T(8,128)S(1)}, u32[]{:S(2)}, u32[]{:S(2)}) collective-permute-start(f32[2,16,640]{2,1,0:T(8,128)S(1)} %dynamic-slice_bitcast_fusion.20), channel_id=1, source_target_pairs={{0,16},{1,17},{2,18},{3,19},{4,20},{5,21},{6,22},{7,23},{8,24},{9,... | collective-permute-start | bytes 245768 | tf_op jit(solution)/shard_map/ppermute | solution.py:129
  249.1 66.2 %collective-permute-start.22 = (f32[2,2,16,768]{3,2,1,0:T(8,128)}, f32[2,2,16,768]{3,2,1,0:T(8,128)}, u32[]{:S(2)}, u32[]{:S(2)}) collective-permute-start(f32[2,2,16,768]{3,2,1,0:T(8,128)} %dynamic-slice_bitcast_fusion.11), channel_id=1, source_target_pairs={{0,1},{1,0},{2,3},{3,2},{4,5},{5,4},{6,7},{7,6},{8,9},{9,8},{10,11... | collective-permute-start | bytes 589832 | tf_op jit(solution)/shard_map/ppermute | solution.py:129
  257.9 61.5 %collective-permute-start.27 = (f32[2,2,16,768]{3,2,1,0:T(8,128)}, f32[2,2,16,768]{3,2,1,0:T(8,128)}, u32[]{:S(2)}, u32[]{:S(2)}) collective-permute-start(f32[2,2,16,768]{3,2,1,0:T(8,128)} %dynamic-slice_bitcast_fusion.10), channel_id=1, source_target_pairs={{0,4},{1,5},{2,6},{3,7},{4,0},{5,1},{6,2},{7,3},{8,12},{9,13},{10,... | collective-permute-start | bytes 589832 | tf_op jit(solution)/shard_map/ppermute | solution.py:129
  298.3 40.8 %collective-permute-start = (f32[2,2,2,2,16,640]{5,4,3,2,1,0:T(8,128)}, f32[2,2,2,2,16,640]{5,4,3,2,1,0:T(8,128)}, u32[]{:S(2)}, u32[]{:S(2)}) collective-permute-start(f32[2,2,2,2,16,640]{5,4,3,2,1,0:T(8,128)} %dynamic-slice_bitcast_fusion.3), channel_id=1, source_target_pairs={{0,8},{1,9},{2,10},{3,11},{4,12},{5,13},{6,14},{7,15},{8,0},{9,1},... | collective-permute-start | bytes 1966088 | tf_op jit(solution)/shard_map/ppermute | solution.py:129
  305.0 37.3 %collective-permute-start.10 = (f32[2,2,2,2,16,768]{5,4,3,2,1,0:T(8,128)}, f32[2,2,2,2,16,768]{5,4,3,2,1,0:T(8,128)}, u32[]{:S(2)}, u32[]{:S(2)}) collective-permute-start(f32[2,2,2,2,16,768]{5,4,3,2,1,0:T(8,128)} %dynamic-slice_bitcast_fusion.1), channel_id=1, source_target_pairs={{0,8},{1,9},{2,10},{3,11},{4,12},{5,13},{6,14},{7,15},{8,0},{9,1},... | collective-permute-start | bytes 2359304 | tf_op jit(solution)/shard_map/ppermute | solution.py:129
  307.5 49.0 %collective-permute-start.15 = (f32[2,2,2,2,16,768]{5,4,2,1,0,3:T(8,128)}, f32[2,2,2,2,16,768]{5,4,2,1,0,3:T(8,128)}, u32[]{:S(2)}, u32[]{:S(2)}) collective-permute-start(f32[2,2,2,2,16,768]{5,4,2,1,0,3:T(8,128)} %bitcast.375), channel_id=1, source_target_pairs={{0,8},{1,9},{2,10},{3,11},{4,12},{5,13},{6,14},{7,15},{8,0},{9,1},... | collective-permute-start | bytes 2359304 | tf_op jit(solution)/shard_map/ppermute | solution.py:129
  311.3 48.6 %all-to-all-start.8 = ((f32[8,2,16,512]{3,2,1,0:T(8,128)}), f32[8,2,16,512]{3,2,1,0:T(8,128)S(1)}, u32[]{:S(2)}, u32[]{:S(2)}) async-start(f32[8,2,16,512]{3,2,1,0:T(8,128)} %bitcast.82), calls=%async_computation.8 | async-start | bytes 1048576 | tf_op jit(solution)/shard_map/all_to_all | solution.py:94
  316.5 18.3 %collective-permute-start.23 = (f32[2,16,768]{2,1,0:T(8,128)S(1)}, f32[2,16,768]{2,1,0:T(8,128)S(1)}, u32[]{:S(2)}, u32[]{:S(2)}) collective-permute-start(f32[2,16,768]{2,1,0:T(8,128)S(1)} %dynamic-slice_bitcast_fusion.17), channel_id=1, source_target_pairs={{0,4},{1,5},{2,6},{3,7},{4,0},{5,1},{6,2},{7,3},{8,12},{9,13},{10,... | collective-permute-start | bytes 294920 | tf_op jit(solution)/shard_map/ppermute | solution.py:129
  320.5 14.3 %collective-permute-start.28 = (f32[2,16,768]{2,1,0:T(8,128)S(1)}, f32[2,16,768]{2,1,0:T(8,128)S(1)}, u32[]{:S(2)}, u32[]{:S(2)}) collective-permute-start(f32[2,16,768]{2,1,0:T(8,128)S(1)} %dynamic-slice_bitcast_fusion.16), channel_id=1, source_target_pairs={{0,2},{1,3},{2,0},{3,1},{4,6},{5,7},{6,4},{7,5},{8,10},{9,11},{10,... | collective-permute-start | bytes 294920 | tf_op jit(solution)/shard_map/ppermute | solution.py:129
  340.5 15.8 %collective-permute-start.1 = (f32[2,2,2,16,640]{4,3,2,1,0:T(8,128)S(1)}, f32[2,2,2,16,640]{4,3,2,1,0:T(8,128)S(1)}, u32[]{:S(2)}, u32[]{:S(2)}) collective-permute-start(f32[2,2,2,16,640]{4,3,2,1,0:T(8,128)S(1)} %dynamic-slice_bitcast_fusion.9), channel_id=1, source_target_pairs={{0,4},{1,5},{2,6},{3,7},{4,0},{5,1},{6,2},{7,3},{8,12},{9,13},{10,... | collective-permute-start | bytes 983048 | tf_op jit(solution)/shard_map/ppermute | solution.py:129
  344.3 18.4 %collective-permute-start.11 = (f32[2,2,2,16,768]{4,3,2,1,0:T(8,128)}, f32[2,2,2,16,768]{4,3,2,1,0:T(8,128)S(1)}, u32[]{:S(2)}, u32[]{:S(2)}) collective-permute-start(f32[2,2,2,16,768]{4,3,2,1,0:T(8,128)} %dynamic-slice_bitcast_fusion.7), channel_id=1, source_target_pairs={{0,16},{1,17},{2,18},{3,19},{4,20},{5,21},{6,22},{7,23},{8,24},{9,... | collective-permute-start | bytes 1179656 | tf_op jit(solution)/shard_map/ppermute | solution.py:129
  356.4 5.4 %collective-permute-start.2 = (f32[2,2,16,640]{3,2,1,0:T(8,128)S(1)}, f32[2,2,16,640]{3,2,1,0:T(8,128)S(1)}, u32[]{:S(2)}, u32[]{:S(2)}) collective-permute-start(f32[2,2,16,640]{3,2,1,0:T(8,128)S(1)} %dynamic-slice_bitcast_fusion.15), channel_id=1, source_target_pairs={{0,2},{1,3},{2,0},{3,1},{4,6},{5,7},{6,4},{7,5},{8,10},{9,11},{10,... | collective-permute-start | bytes 491528 | tf_op jit(solution)/shard_map/ppermute | solution.py:129
  358.5 12.3 %collective-permute-start.16 = (f32[2,2,2,16,768]{4,3,2,1,0:T(8,128)}, f32[2,2,2,16,768]{4,3,2,1,0:T(8,128)}, u32[]{:S(2)}, u32[]{:S(2)}) collective-permute-start(f32[2,2,2,16,768]{4,3,2,1,0:T(8,128)} %dynamic-slice_bitcast_fusion.6), channel_id=1, source_target_pairs={{0,1},{1,0},{2,3},{3,2},{4,5},{5,4},{6,7},{7,6},{8,9},{9,8},{10,11... | collective-permute-start | bytes 1179656 | tf_op jit(solution)/shard_map/ppermute | solution.py:129
  361.8 10.0 %collective-permute-start.3 = (f32[2,16,640]{2,1,0:T(8,128)S(1)}, f32[2,16,640]{2,1,0:T(8,128)S(1)}, u32[]{:S(2)}, u32[]{:S(2)}) collective-permute-start(f32[2,16,640]{2,1,0:T(8,128)S(1)} %dynamic-slice_bitcast_fusion.21), channel_id=1, source_target_pairs={{0,16},{1,17},{2,18},{3,19},{4,20},{5,21},{6,22},{7,23},{8,24},{9,... | collective-permute-start | bytes 245768 | tf_op jit(solution)/shard_map/ppermute | solution.py:129
  362.7 14.9 %collective-permute-start.12 = (f32[2,2,16,768]{3,2,1,0:T(8,128)S(1)}, f32[2,2,16,768]{3,2,1,0:T(8,128)S(1)}, u32[]{:S(2)}, u32[]{:S(2)}) collective-permute-start(f32[2,2,16,768]{3,2,1,0:T(8,128)S(1)} %dynamic-slice_bitcast_fusion.13), channel_id=1, source_target_pairs={{0,1},{1,0},{2,3},{3,2},{4,5},{5,4},{6,7},{7,6},{8,9},{9,8},{10,11... | collective-permute-start | bytes 589832 | tf_op jit(solution)/shard_map/ppermute | solution.py:129
  373.5 9.6 %collective-permute-start.17 = (f32[2,2,16,768]{3,2,1,0:T(8,128)S(1)}, f32[2,2,16,768]{3,2,1,0:T(8,128)S(1)}, u32[]{:S(2)}, u32[]{:S(2)}) collective-permute-start(f32[2,2,16,768]{3,2,1,0:T(8,128)S(1)} %dynamic-slice_bitcast_fusion.12), channel_id=1, source_target_pairs={{0,4},{1,5},{2,6},{3,7},{4,0},{5,1},{6,2},{7,3},{8,12},{9,13},{10,... | collective-permute-start | bytes 589832 | tf_op jit(solution)/shard_map/ppermute | solution.py:129
  377.7 7.5 %collective-permute-start.13 = (f32[2,16,768]{2,1,0:T(8,128)S(1)}, f32[2,16,768]{2,1,0:T(8,128)S(1)}, u32[]{:S(2)}, u32[]{:S(2)}) collective-permute-start(f32[2,16,768]{2,1,0:T(8,128)S(1)} %dynamic-slice_bitcast_fusion.19), channel_id=1, source_target_pairs={{0,4},{1,5},{2,6},{3,7},{4,0},{5,1},{6,2},{7,3},{8,12},{9,13},{10,... | collective-permute-start | bytes 294920 | tf_op jit(solution)/shard_map/ppermute | solution.py:129
  (48 other events, 334.2 us)

commit v2 on v0

--- a/solution.py
+++ b/solution.py
@@ -12,27 +12,41 @@
 
 
 exact_mode = lax.Precision.HIGHEST
+fast_mode = lax.Precision.HIGH
+mesh_axes = ("gx", "gy")
 epsilon = 1e-05
 
 
-def attend_block(rows_in, gain_row, qkv_weight, proj_weight):
+def project_rows(rows_in, gain_row, qkv_weight):
     row_count = rows_in.shape[0]
-    head_dim = D // HEADS
     row_mean = jnp.mean(rows_in, axis=-1, keepdims=True)
     centered = rows_in - row_mean
     row_var = jnp.mean(centered * centered, axis=-1, keepdims=True)
     normed = centered * lax.rsqrt(row_var + epsilon) * gain_row
     projected = jnp.dot(normed, qkv_weight, precision=exact_mode)
-    projected = projected.reshape(row_count // PATCH, PATCH, 3, HEADS, head_dim)
+    return projected.reshape(row_count // PATCH, PATCH, 3, HEADS, D // HEADS)
+
+
+def attend(projected):
     queries = projected[:, :, 0]
     key_rows = projected[:, :, 1]
     value_rows = projected[:, :, 2]
     scores = jnp.einsum("pihd,pjhd->phij", queries, key_rows, precision=exact_mode) * (
-        1.0 / math.sqrt(head_dim)
+        1.0 / math.sqrt(D // HEADS)
     )
     attention = jax.nn.softmax(scores, axis=-1)
-    mixed_rows = jnp.einsum("phij,pjhd->pihd", attention, value_rows, precision=exact_mode)
-    return rows_in + jnp.dot(mixed_rows.reshape(row_count, D), proj_weight, precision=exact_mode)
+    return jnp.einsum("phij,pjhd->pihd", attention, value_rows, precision=fast_mode)
+
+
+def leave_block(rows_in, mixed_rows, proj_weight):
+    return rows_in + jnp.dot(mixed_rows.reshape(rows_in.shape), proj_weight, precision=fast_mode)
+
+
+def block_forward(rows_in, gain_row, qkv_weight, proj_weight):
+    projected, pull_project = jax.vjp(project_rows, rows_in, gain_row, qkv_weight)
+    mixed_rows, pull_attend = jax.vjp(attend, projected)
+    rows_out, pull_leave = jax.vjp(leave_block, rows_in, mixed_rows, proj_weight)
+    return (rows_out, pull_project, pull_attend, pull_leave)
 
 
 def occupancy(owner_index):
@@ -112,32 +126,116 @@
     return received[route[:, 0] // lax.axis_size("gy"), occur].reshape(-1, rows_in.shape[1])
 
 
-def reduce_grads(gain_part, qkv_part, proj_part):
-    return (
-        lax.psum_scatter(gain_part, ("gx", "gy"), scatter_dimension=1, tiled=True),
-        lax.psum_scatter(qkv_part, ("gx", "gy"), scatter_dimension=1, tiled=True),
-        lax.psum_scatter(proj_part, ("gx", "gy"), scatter_dimension=1, tiled=True),
-    )
+def pick_bits(shaped, left, bits, values, bit_count):
+    left = list(left)
+    for bit, value in zip(bits, values):
+        at = left.index(bit_count - 1 - bit)
+        left.pop(at)
+        shaped = lax.dynamic_index_in_dim(shaped, value, at, keepdims=False)
+    return (shaped, left)
+
+
+class ScatterSum:
+    def __init__(self, part, groups):
+        self.device_count = lax.axis_size("gx") * lax.axis_size("gy")
+        self.bit_count = self.device_count.bit_length() - 1
+        self.groups = list(groups)
+        self.left = list(range(self.bit_count))
+        self.shaped = part.reshape(
+            (2,) * self.bit_count + (part.shape[0] // self.device_count, part.shape[1])
+        )
+        self.kept, self.received = None, []
+        self.send_next()
+
+    def send_next(self):
+        if self.received:
+            self.shaped = sum(self.received, self.kept)
+            self.received = []
+        if not self.groups:
+            return
+        bits = self.groups.pop(0)
+        me = lax.axis_index(mesh_axes)
+        mine = [(me >> bit) & 1 for bit in bits]
+        self.kept, left = pick_bits(self.shaped, self.left, bits, mine, self.bit_count)
+        for flips in range(1, 1 << len(bits)):
+            flip = [(flips >> i) & 1 for i in range(len(bits))]
+            mask = sum(value << bit for value, bit in zip(flip, bits))
+            theirs = [own ^ value for own, value in zip(mine, flip)]
+            sent, unused = pick_bits(self.shaped, self.left, bits, theirs, self.bit_count)
+            swaps = [(i, i ^ mask) for i in range(self.device_count)]
+            self.received.append(lax.ppermute(sent, mesh_axes, swaps))
+        self.left = left
+
+    def meet(self, value):
+        value, self.received = lax.optimization_barrier((value, self.received))
+        self.send_next()
+        return value
+
+    def finish(self):
+        while self.received:
+            self.send_next()
+        return self.shaped
+
+
+def bit_groups(mesh_gx, mesh_gy):
+    gy_bits = mesh_gy.bit_length() - 1
+    gx_bits = mesh_gx.bit_length() - 1
+    groups = [[gy_bits]]
+    low = list(range(gy_bits // 2))
+    high = list(range(gy_bits // 2, gy_bits))
+    y_bits = list(range(gy_bits + 1, gy_bits + gx_bits))
+    return groups + ([y_bits + low] if len(y_bits + low) < 3 else [y_bits, low]) + [high]
+
+
+def with_gain(proj_part, gain_part):
+    gain_wide = jnp.broadcast_to(gain_part[:, None], (gain_part.shape[0], 128))
+    return jnp.concatenate([proj_part, gain_wide], axis=1)
 
 
 def per_device(points, upstream, gains, w_qkv, w_proj, z_route, h_route):
+    groups = bit_groups(lax.axis_size("gx"), lax.axis_size("gy"))
+    wide = w_qkv.shape[2]
+    tall = w_proj.shape[2]
     curve_first, z_source, z_occur = to_zorder(points, z_route)
-    first_out, pull_first = jax.vjp(attend_block, curve_first, gains[0], w_qkv[0], w_proj[0])
+    grad_curve, unused_source, unused_occur = to_hilbert(upstream, h_route)
+    first_out, project_first, attend_first, leave_first = block_forward(
+        curve_first, gains[0], w_qkv[0], w_proj[0]
+    )
     middle = from_zorder(first_out, z_source, z_occur, z_route)
     curve_second, h_source, h_occur = to_hilbert(middle, h_route)
-    grad_curve, unused_source, unused_occur = to_hilbert(upstream, h_route)
-    second_out, pull_second = jax.vjp(attend_block, curve_second, gains[1], w_qkv[1], w_proj[1])
-    grad_second, gain_second, qkv_second, proj_second = pull_second(grad_curve)
-    grad_middle = from_hilbert(grad_second, h_source, h_occur, h_route)
+    second_out, project_second, attend_second, leave_second = block_forward(
+        curve_second, gains[1], w_qkv[1], w_proj[1]
+    )
+    straight, grad_mixed, proj_second = leave_second(grad_curve)
+    proj_sum = ScatterSum(proj_second, groups)
+    (grad_projected,) = attend_second(grad_mixed)
+    grad_projected = proj_sum.meet(grad_projected)
+    around, gain_second, qkv_second = project_second(grad_projected)
+    around = proj_sum.meet(around)
+    qkv_sum = ScatterSum(with_gain(qkv_second, gain_second), groups)
+    grad_middle = from_hilbert(straight + around, h_source, h_occur, h_route)
+    grad_middle = proj_sum.meet(grad_middle)
+    proj_second = proj_sum.finish()
+    grad_middle = qkv_sum.meet(grad_middle)
     middle_curve, unused_again, unused_spots = to_zorder(grad_middle, z_route)
-    grad_first, gain_first, qkv_first, proj_first = pull_first(middle_curve)
-    point_grad = from_zorder(grad_first, z_source, z_occur, z_route)
-    gain_grad, qkv_grad, proj_grad = reduce_grads(
-        jnp.stack([gain_first, gain_second]),
-        jnp.stack([qkv_first, qkv_second]),
+    straight, grad_mixed, proj_first = leave_first(middle_curve)
+    grad_mixed = qkv_sum.meet(grad_mixed)
+    proj_sum = ScatterSum(proj_first, groups)
+    (grad_projected,) = attend_first(grad_mixed)
+    grad_projected = qkv_sum.meet(grad_projected)
+    grad_projected = proj_sum.meet(grad_projected)
+    second_sum = qkv_sum.finish()
+    around, gain_first, qkv_first = project_first(grad_projected)
+    qkv_sum = ScatterSum(with_gain(qkv_first, gain_first), groups)
+    point_grad = from_zorder(straight + around, z_source, z_occur, z_route)
+    proj_first = proj_sum.finish()
+    first_sum = qkv_sum.finish()
+    return (
+        point_grad,
+        jnp.stack([first_sum[:, wide], second_sum[:, wide]]),
+        jnp.stack([first_sum[:, :wide], second_sum[:, :wide]]),
         jnp.stack([proj_first, proj_second]),
     )
-    return (point_grad, gain_grad, qkv_grad, proj_grad)
 
 
 def solution(mesh):

time: 666 us -> 357 us (0.54)
  waiting for transfers between devices: 385 us -> 73.2 us
  starting transfers between devices: 37.2 us -> 71.9 us
  matrix products: 120 us -> 94.7 us
  local copies, waits for them, and re-layouts: 65.6 us -> 80.4 us
  between operations: 14.8 us -> 2.38 us
  blocking collectives: 11.9 us -> 0 us
    reduce_scatter x2 -> x0, waiting for transfers between devices: 254 us -> none  [the longest x1 136 us: reduce_grads(): lax.psum_scatter(proj_part, ('gx', 'gy'), scatter_dimension=1, tiled=True)]
    unnamed x4 -> x0, waiting for transfers between devices: 108 us -> none
    ppermute x0 -> x28, waiting for transfers between devices: none -> 48 us  [send_next(): self.received.append(lax.ppermute(sent, mesh_axes, swaps))]
    ppermute x0 -> x28, starting transfers between devices: none -> 32.9 us  [send_next(): self.received.append(lax.ppermute(sent, mesh_axes, swaps))]
    dot_general x23, matrix products: 120 us -> 94.7 us  [the longest x6 37.1 us: attend(): jnp.einsum('pihd,pjhd->phij', queries, key_rows, precision=exact_mode)]
    all_to_all x1 -> x0, blocking collectives: 11.9 us -> none  [from_hilbert(): lax.all_to_all(buffer, 'gx', split_axis=0, concat_axis=0, tiled=True)]
  transfers between devices with their start and end apart: 11 -> 37, of which waited for: 7 -> 23; matrix products, arithmetic and copies ran while one was open for 15% -> 26% of each run, Pallas kernels for 0% -> 0%
where the time goes in v2:
time: 357 us; the launch traced here: 352 us
  matrix products  94.7 us (27%)
  local copies, waits for them, and re-layouts  80.4 us (23%)
  waiting for transfers between devices  73.2 us (21%)
  starting transfers between devices  71.9 us (20%)
  other arithmetic  29.6 us (8%)
    ppermute x28, waiting for transfers between devices, send_next(): self.received.append(lax.ppermute(sent, mesh_axes, swaps))  48 us
    dot_general x6, matrix products, attend(): jnp.einsum('pihd,pjhd->phij', queries, key_rows, precision=exact_mode)  37.1 us
    ppermute x28, starting transfers between devices, send_next(): self.received.append(lax.ppermute(sent, mesh_axes, swaps))  32.9 us
    dot_general x6, matrix products, project_rows(): projected = jnp.dot(normed, qkv_weight, precision=exact_mode)  30.5 us
    dot_general x6, matrix products, attend(): jnp.einsum('phij,pjhd->pihd', attention, value_rows, precision=fast_mode)  20.8 us
    unnamed x100, local copies, waits for them, and re-layouts  12.8 us
    scatter x4, local copies, waits for them, and re-layouts, spread_out(): buffer = jnp.zeros((peer_count, per_peer) + segments.shape[1:], rows_in.d...  12.1 us
    all_to_all x2, waiting for transfers between devices, from_zorder(): lax.all_to_all(buffer, 'gy', split_axis=0, concat_axis=0, tiled=True)  10.6 us
  transfers between devices with their start and end apart: 37, of which 23 were waited for; matrix products, arithmetic and copies ran while one was open for 26% of the time, Pallas kernels for 0%

profile of v2, /device:TPU:0, one launch (start us, length us, event | category | flops | bytes accessed | tf_op | source)
XLA Modules:
  0.0 352.1 jit_solution(17182346351994880249)
XLA Ops:
  5.8 4.3 %all-to-all-start.1 = ((s32[4,1,4]{2,1,0:T(1,128)}), s32[4,1,4]{2,1,0:T(1,128)S(1)}, u32[]{:S(2)}, u32[]{:S(2)}) async-start(s32[4,1,4]{2,1,0:T(1,128)} %bitcast.14), calls=%async_computation.1 | async-start | bytes 4096 | tf_op jit(solution)/shard_map/all_to_all | solution.py:116
  13.8 6.2 %all-to-all-start = ((s32[8,1,2]{2,1,0:T(1,128)}), s32[8,1,2]{2,1,0:T(1,128)S(1)}, u32[]{:S(2)}, u32[]{:S(2)}) async-start(s32[8,1,2]{2,1,0:T(1,128)} %copy.107), calls=%async_computation | async-start | bytes 8192 | tf_op jit(solution)/shard_map/all_to_all | solution.py:97
  26.4 4.1 %all-to-all-start.3 = ((f32[8,2,16,512]{3,2,1,0:T(8,128)}), f32[8,2,16,512]{3,2,1,0:T(8,128)}, u32[]{:S(2)}, u32[]{:S(2)}) async-start(f32[8,2,16,512]{3,2,1,0:T(8,128)} %scatter_fusion.3), calls=%async_computation.3 | async-start | bytes 1048576 | tf_op jit(solution)/shard_map/all_to_all | solution.py:96
  30.6 5.9 %fusion.89 = (f32[1,512,1536]{2,1,0:T(8,128)}, f32[1,512,1536]{2,1,0:T(8,128)}) fusion(f32[2,512,1536]{2,1,0:T(8,128)} %param.10), kind=kLoop, calls=%fused_computation.245 | loop fusion | bytes 12582912 | tf_op jit(solution)/shard_map/slice | solution.py:207
  50.6 4.2 %fusion.6 = f32[2,128,3,32,16]{1,3,4,2,0:T(8,128)S(1)} fusion(f32[2,128,512,1,1]{2,1,4,3,0:T(8,128)S(1)} %bitcast.402, f32[3,32,16,512]{3,2,1,0:T(8,128)S(1)} %bitcast.384), kind=kOutput, calls=%fused_computation.32 | convolution fusion | flops 2415919104 | bytes 5242880 | tf_op jit(solution)/shard_map/jvp()/dot_general | solution.py:26
  55.8 6.7 %multiply_reduce_fusion.3 = (f32[2,32,128]{2,1,0:T(8,128)S(1)}, f32[2,32,128,128]{2,3,1,0:T(8,128)S(1)}) fusion(f32[2,128,32,16]{1,2,3,0:T(8,128)S(1)} %get-tuple-element.74, f32[2,128,32,16]{1,2,3,0:T(8,128)S(1)} %get-tuple-element.75), kind=kOutput, calls=%fused_computation.23 | convolution fusion | flops 203415552 | bytes 5275648 | tf_op jit(solution)/shard_map/jvp(pihd,pjhd->phij)/dot_general | solution.py:34
  70.8 3.6 %all-to-all-start.4 = ((f32[8,2,16,512]{3,2,1,0:T(8,128)}), f32[8,2,16,512]{3,2,1,0:T(8,128)S(1)}, u32[]{:S(2)}, u32[]{:S(2)}) async-start(f32[8,2,16,512]{3,2,1,0:T(8,128)} %bitcast.43), calls=%async_computation.4 | async-start | bytes 1048576 | tf_op jit(solution)/shard_map/all_to_all | solution.py:106
  78.2 10.6 %all-to-all-done.4 = f32[8,2,16,512]{3,2,1,0:T(8,128)S(1)} async-done(((f32[8,2,16,512]{3,2,1,0:T(8,128)}), f32[8,2,16,512]{3,2,1,0:T(8,128)S(1)}, u32[]{:S(2)}, u32[]{:S(2)}) %all-to-all-start.4) | async-done | bytes 524320 | tf_op jit(solution)/shard_map/all_to_all | solution.py:106
  88.8 4.1 %all-to-all-start.2 = ((f32[4,4,16,512]{3,2,1,0:T(8,128)}), f32[4,4,16,512]{3,2,1,0:T(8,128)}, u32[]{:S(2)}, u32[]{:S(2)}) async-start(f32[4,4,16,512]{3,2,1,0:T(8,128)} %scatter_fusion.2), calls=%async_computation.2 | async-start | bytes 1048576 | tf_op jit(solution)/shard_map/all_to_all | solution.py:115
  104.9 4.6 %all-to-all-start.5 = ((f32[4,4,16,512]{3,2,1,0:T(8,128)}), f32[4,4,16,512]{3,2,1,0:T(8,128)}, u32[]{:S(2)}, u32[]{:S(2)}) async-start(f32[4,4,16,512]{3,2,1,0:T(8,128)} %scatter_fusion.5), calls=%async_computation.5 | async-start | bytes 1048576 | tf_op jit(solution)/shard_map/all_to_all | solution.py:115
  124.0 4.2 %fusion.4 = f32[2,128,3,32,16]{1,3,4,2,0:T(8,128)S(1)} fusion(f32[2,128,512,1,1]{2,1,4,3,0:T(8,128)S(1)} %bitcast.404, f32[3,32,16,512]{3,2,1,0:T(8,128)S(1)} %bitcast.383), kind=kOutput, calls=%fused_computation.30 | convolution fusion | flops 2415919104 | bytes 5242880 | tf_op jit(solution)/shard_map/jvp()/dot_general | solution.py:26
  128.3 6.9 %multiply_reduce_fusion.2 = (f32[2,32,128]{2,1,0:T(8,128)S(1)}, f32[2,32,128,128]{2,3,1,0:T(8,128)S(1)}) fusion(f32[2,128,32,16]{1,2,3,0:T(8,128)S(1)} %get-tuple-element.72, f32[2,128,32,16]{1,2,3,0:T(8,128)S(1)} %get-tuple-element.70), kind=kOutput, calls=%fused_computation.22 | convolution fusion | flops 203415552 | bytes 5275648 | tf_op jit(solution)/shard_map/jvp(pihd,pjhd->phij)/dot_general | solution.py:34
  140.8 3.4 convolution_bitcast_fusion.7
  144.2 3.7 %multiply_reduce_fusion.1 = (f32[2,32,128]{2,1,0:T(8,128)S(1)}, f32[2,32,128,128]{2,3,1,0:T(8,128)S(1)}) fusion(f32[2,32,128]{2,1,0:T(8,128)S(1)} %multiply_divide_fusion.1, f32[2,32,128]{2,1,0:T(8,128)S(1)} %get-tuple-element.106, f32[2,32,128,128]{2,3,1,0:T(8,128)S(1)} %get-tuple-element.107, f32[2,128,32,16]{1,2,3,0:T(8,128)S(1)} %get-tuple-element.71, ...), kind=kOutput, calls=%fused_computation.19 | convolution fusion | flops 105897984 | bytes 9535488 | tf_op jit(solution)/shard_map/transpose(jvp(phij,pjhd->pihd))/dot_general | solution.py:38
  151.9 6.7 %convolution_bitcast_fusion.6 = f32[2,128,1,32,16]{1,4,3,0,2:T(8,128)S(1)} fusion(f32[2,32,128,128]{2,3,1,0:T(8,128)S(1)} %multiply_multiply_fusion.1, f32[2,128,32,16]{1,2,3,0:T(8,128)S(1)} %get-tuple-element.70), kind=kOutput, calls=%fused_computation.63 | convolution fusion | flops 201326592 | bytes 5242880 | tf_op jit(solution)/shard_map/transpose(jvp(pihd,pjhd->phij))/dot_general | solution.py:34
  158.8 6.0 %convolution_bitcast_fusion.5 = f32[2,128,1,32,16]{1,4,3,0,2:T(8,128)S(1)} fusion(f32[2,32,128,128]{2,3,1,0:T(8,128)} %copy-done.2, f32[2,128,32,16]{1,2,3,0:T(8,128)S(1)} %get-tuple-element.72), kind=kOutput, calls=%fused_computation.62 | convolution fusion | flops 201326592 | bytes 5242880 | tf_op jit(solution)/shard_map/transpose(jvp(pihd,pjhd->phij))/dot_general | solution.py:34
  166.3 5.3 %fusion.15 = f32[512,1536]{1,0:T(8,128)S(1)} fusion(f32[256,512]{1,0:T(8,128)S(1)} %bitcast.405, f32[192,8,2,128]{3,2,1,0:T(2,128)S(1)} %bitcast.390), kind=kOutput, calls=%fused_computation.47 | convolution fusion | flops 2415919104 | bytes 5242880 | tf_op jit(solution)/shard_map/transpose(jvp())/dot_general | solution.py:26
  171.6 5.6 %multiply_reduce_fusion.6 = (f32[512]{0:T(512)S(1)}, f32[256]{0:T(256)S(1)}, f32[256,512]{1,0:T(8,128)S(1)}) fusion(f32[16,16,512]{2,1,0:T(8,128)S(1)} %copy-done.5, f32[256]{0:T(256)S(1)} %div.126, f32[256]{0:T(256)S(1)} %rsqrt.32, f32[512]{0:T(512)S(1)} %bitcast.429, f32[2,512,1536]{2,1,0:T(8,128)S(1)} %bitcast.387, f32[192,8,2,128]{3,2,1,0:T(2,128)S(1)} %bitcast.391), kind=kOutput, calls=%fused_computation.91 | convolution fusion | flops 2416835840 | bytes 5774336 | tf_op jit(solution)/shard_map/transpose(jvp())/dot_general | solution.py:26
  193.9 4.1 %all-to-all-start.6 = ((f32[4,4,16,512]{3,2,1,0:T(8,128)}), f32[4,4,16,512]{3,2,1,0:T(8,128)}, u32[]{:S(2)}, u32[]{:S(2)}) async-start(f32[4,4,16,512]{3,2,1,0:T(8,128)} %bitcast.408), calls=%async_computation.6 | async-start | bytes 1048576 | tf_op jit(solution)/shard_map/all_to_all | solution.py:125
  214.5 4.1 %all-to-all-start.7 = ((f32[8,2,16,512]{3,2,1,0:T(8,128)}), f32[8,2,16,512]{3,2,1,0:T(8,128)}, u32[]{:S(2)}, u32[]{:S(2)}) async-start(f32[8,2,16,512]{3,2,1,0:T(8,128)} %scatter_fusion.7), calls=%async_computation.7 | async-start | bytes 1048576 | tf_op jit(solution)/shard_map/all_to_all | solution.py:96
  227.2 6.0 %all-to-all-done.7 = f32[8,2,16,512]{3,2,1,0:T(8,128)} async-done(((f32[8,2,16,512]{3,2,1,0:T(8,128)}), f32[8,2,16,512]{3,2,1,0:T(8,128)}, u32[]{:S(2)}, u32[]{:S(2)}) %all-to-all-start.7) | async-done | bytes 524320 | tf_op jit(solution)/shard_map/all_to_all | solution.py:96
  238.4 6.4 %collective-permute-done.8 = f32[2,2,16,1664]{3,2,1,0:T(8,128)S(1)} collective-permute-done((f32[2,2,16,1664]{3,2,1,0:T(8,128)}, f32[2,2,16,1664]{3,2,1,0:T(8,128)S(1)}, u32[]{:S(2)}, u32[]{:S(2)}) %collective-permute-start.8) | collective-permute-done | bytes 426016 | tf_op jit(solution)/shard_map/ppermute | solution.py:166
  246.2 5.3 %convolution_bitcast_fusion.3 = f32[2,128,1,32,16]{1,4,3,0,2:T(8,128)S(1)} fusion(f32[2,32,128]{2,1,0:T(8,128)S(1)} %fusion.10, f32[2,32,128]{2,1,0:T(8,128)S(1)} %get-tuple-element.104, f32[2,32,128,128]{2,3,1,0:T(8,128)} %copy-done, f32[2,32,16,128]{3,1,2,0:T(8,128)S(1)} %bitcast.413), kind=kOutput, calls=%fused_computation.60 | convolution fusion | flops 103809024 | bytes 5308416 | tf_op jit(solution)/shard_map/transpose(jvp(phij,pjhd->pihd))/dot_general | solution.py:38
  251.5 3.7 %multiply_reduce_fusion = (f32[2,32,128]{2,1,0:T(8,128)S(1)}, f32[2,32,128,128]{2,3,1,0:T(8,128)S(1)}) fusion(f32[2,32,128]{2,1,0:T(8,128)S(1)} %multiply_divide_fusion, f32[2,32,128]{2,1,0:T(8,128)S(1)} %get-tuple-element.104, f32[2,32,128,128]{2,3,1,0:T(8,128)S(1)} %copy-done.1, f32[2,128,32,16]{1,2,3,0:T(8,128)S(1)} %copy-done.24, ...), kind=kOutput, calls=%fused_computation.17 | convolution fusion | flops 105897984 | bytes 9535488 | tf_op jit(solution)/shard_map/transpose(jvp(phij,pjhd->pihd))/dot_general | solution.py:38
  257.0 6.7 %convolution_bitcast_fusion.2 = f32[2,128,1,32,16]{1,4,3,0,2:T(8,128)S(1)} fusion(f32[2,32,128,128]{2,3,1,0:T(8,128)S(1)} %multiply_multiply_fusion, f32[2,128,32,16]{1,2,3,0:T(8,128)S(1)} %copy-done.16), kind=kOutput, calls=%fused_computation.59 | convolution fusion | flops 201326592 | bytes 5242880 | tf_op jit(solution)/shard_map/transpose(jvp(pihd,pjhd->phij))/dot_general | solution.py:34
  263.7 4.1 %convolution_bitcast_fusion.1 = f32[2,128,1,32,16]{1,4,3,0,2:T(8,128)S(1)} fusion(f32[2,32,128,128]{2,3,1,0:T(8,128)S(1)} %multiply_multiply_fusion, f32[2,128,32,16]{1,2,3,0:T(8,128)S(1)} %copy-done.14), kind=kOutput, calls=%fused_computation.58 | convolution fusion | flops 201326592 | bytes 5242880 | tf_op jit(solution)/shard_map/transpose(jvp(pihd,pjhd->phij))/dot_general | solution.py:34
  275.2 7.7 %collective-permute-done.12 = f32[16,1664]{1,0:T(8,128)S(1)} collective-permute-done((f32[16,1664]{1,0:T(8,128)S(1)}, f32[16,1664]{1,0:T(8,128)S(1)}, u32[]{:S(2)}, u32[]{:S(2)}) %collective-permute-start.12) | collective-permute-done | bytes 106528 | tf_op jit(solution)/shard_map/ppermute | solution.py:166
  284.2 5.3 %fusion.12 = f32[512,1536]{1,0:T(8,128)S(1)} fusion(f32[256,512]{1,0:T(8,128)S(1)} %bitcast.403, f32[192,8,2,128]{3,2,1,0:T(2,128)S(1)} %bitcast.392), kind=kOutput, calls=%fused_computation.44 | convolution fusion | flops 2415919104 | bytes 5242880 | tf_op jit(solution)/shard_map/transpose(jvp())/dot_general | solution.py:26
  289.6 5.9 %multiply_reduce_fusion.4 = (f32[512]{0:T(512)S(1)}, f32[256]{0:T(256)S(1)}, f32[256,512]{1,0:T(8,128)S(1)}) fusion(f32[16,16,512]{2,1,0:T(8,128)S(1)} %copy-done.4, f32[256]{0:T(256)S(1)} %copy-done.35, f32[256]{0:T(256)S(1)} %copy-done.36, f32[512]{0:T(512)S(1)} %bitcast.426, f32[2,512,1536]{2,1,0:T(8,128)S(1)} %bitcast.389, ...), kind=kOutput, calls=%fused_computation.88 | convolution fusion | flops 2416835840 | bytes 5774336 | tf_op jit(solution)/shard_map/transpose(jvp())/dot_general | solution.py:26
  320.4 3.6 %all-to-all-start.8 = ((f32[8,2,16,512]{3,2,1,0:T(8,128)}), f32[8,2,16,512]{3,2,1,0:T(8,128)S(1)}, u32[]{:S(2)}, u32[]{:S(2)}) async-start(f32[8,2,16,512]{3,2,1,0:T(8,128)} %bitcast.114), calls=%async_computation.8 | async-start | bytes 1048576 | tf_op jit(solution)/shard_map/all_to_all | solution.py:106
  325.3 3.9 %collective-permute-done.17 = f32[2,2,16,1664]{3,2,1,0:T(8,128)} collective-permute-done((f32[2,2,16,1664]{3,2,1,0:T(8,128)}, f32[2,2,16,1664]{3,2,1,0:T(8,128)}, u32[]{:S(2)}, u32[]{:S(2)}) %collective-permute-start.17) | collective-permute-done | bytes 426016 | tf_op jit(solution)/shard_map/ppermute | solution.py:166
  329.3 10.1 %collective-permute-done.18 = f32[2,2,16,1664]{3,2,1,0:T(8,128)} collective-permute-done((f32[2,2,16,1664]{3,2,1,0:T(8,128)}, f32[2,2,16,1664]{3,2,1,0:T(8,128)}, u32[]{:S(2)}, u32[]{:S(2)}) %collective-permute-start.18) | collective-permute-done | bytes 426016 | tf_op jit(solution)/shard_map/ppermute | solution.py:166
  (290 shorter events, 176.4 us)
Async XLA Ops:
  5.8 8.0 %all-to-all-start.1 = ((s32[4,1,4]{2,1,0:T(1,128)}), s32[4,1,4]{2,1,0:T(1,128)S(1)}, u32[]{:S(2)}, u32[]{:S(2)}) async-start(s32[4,1,4]{2,1,0:T(1,128)} %bitcast.14), calls=%async_computation.1 | async-start | bytes 4096 | tf_op jit(solution)/shard_map/all_to_all | solution.py:116
  13.8 12.6 %all-to-all-start = ((s32[8,1,2]{2,1,0:T(1,128)}), s32[8,1,2]{2,1,0:T(1,128)S(1)}, u32[]{:S(2)}, u32[]{:S(2)}) async-start(s32[8,1,2]{2,1,0:T(1,128)} %copy.107), calls=%async_computation | async-start | bytes 8192 | tf_op jit(solution)/shard_map/all_to_all | solution.py:97
  26.4 18.2 %all-to-all-start.3 = ((f32[8,2,16,512]{3,2,1,0:T(8,128)}), f32[8,2,16,512]{3,2,1,0:T(8,128)}, u32[]{:S(2)}, u32[]{:S(2)}) async-start(f32[8,2,16,512]{3,2,1,0:T(8,128)} %scatter_fusion.3), calls=%async_computation.3 | async-start | bytes 1048576 | tf_op jit(solution)/shard_map/all_to_all | solution.py:96
  70.8 18.0 %all-to-all-start.4 = ((f32[8,2,16,512]{3,2,1,0:T(8,128)}), f32[8,2,16,512]{3,2,1,0:T(8,128)S(1)}, u32[]{:S(2)}, u32[]{:S(2)}) async-start(f32[8,2,16,512]{3,2,1,0:T(8,128)} %bitcast.43), calls=%async_computation.4 | async-start | bytes 1048576 | tf_op jit(solution)/shard_map/all_to_all | solution.py:106
  88.8 16.1 %all-to-all-start.2 = ((f32[4,4,16,512]{3,2,1,0:T(8,128)}), f32[4,4,16,512]{3,2,1,0:T(8,128)}, u32[]{:S(2)}, u32[]{:S(2)}) async-start(f32[4,4,16,512]{3,2,1,0:T(8,128)} %scatter_fusion.2), calls=%async_computation.2 | async-start | bytes 1048576 | tf_op jit(solution)/shard_map/all_to_all | solution.py:115
  104.9 13.0 %all-to-all-start.5 = ((f32[4,4,16,512]{3,2,1,0:T(8,128)}), f32[4,4,16,512]{3,2,1,0:T(8,128)}, u32[]{:S(2)}, u32[]{:S(2)}) async-start(f32[4,4,16,512]{3,2,1,0:T(8,128)} %scatter_fusion.5), calls=%async_computation.5 | async-start | bytes 1048576 | tf_op jit(solution)/shard_map/all_to_all | solution.py:115
  140.7 24.3 %collective-permute-start = (f32[2,2,2,2,16,512]{5,4,3,2,1,0:T(8,128)S(1)}, f32[2,2,2,2,16,512]{5,4,3,2,1,0:T(8,128)S(1)}, u32[]{:S(2)}, u32[]{:S(2)}) collective-permute-start(f32[2,2,2,2,16,512]{5,4,3,2,1,0:T(8,128)S(1)} %dynamic-slice_bitcast_fusion.3), channel_id=1, source_target_pairs={{0,8},{1,9},{2,10},{3,11},{4,12},{5,13},{6,14},{7,15},{8,0},{9,1},... | collective-permute-start | bytes 1572872 | tf_op jit(solution)/shard_map/ppermute | solution.py:166
  179.1 31.4 %collective-permute-start.7 = (f32[2,2,2,2,16,1664]{5,4,3,2,1,0:T(8,128)}, f32[2,2,2,2,16,1664]{5,4,3,2,1,0:T(8,128)}, u32[]{:S(2)}, u32[]{:S(2)}) collective-permute-start(f32[2,2,2,2,16,1664]{5,4,3,2,1,0:T(8,128)} %dynamic-slice_bitcast_fusion.1), channel_id=1, source_target_pairs={{0,8},{1,9},{2,10},{3,11},{4,12},{5,13},{6,14},{7,15},{8,0},{9,1},... | collective-permute-start | bytes 5111816 | tf_op jit(solution)/shard_map/ppermute | solution.py:166
  181.7 7.6 %collective-permute-start.3 = (f32[2,2,16,512]{3,2,1,0:T(8,128)S(1)}, f32[2,2,16,512]{3,2,1,0:T(8,128)S(1)}, u32[]{:S(2)}, u32[]{:S(2)}) collective-permute-start(f32[2,2,16,512]{3,2,1,0:T(8,128)S(1)} %get-tuple-element.79), channel_id=1, source_target_pairs={{0,17},{1,16},{2,19},{3,18},{4,21},{5,20},{6,23},{7,22},{8,25},{9,... | collective-permute-start | bytes 393224 | tf_op jit(solution)/shard_map/ppermute | solution.py:166
  193.9 14.2 %all-to-all-start.6 = ((f32[4,4,16,512]{3,2,1,0:T(8,128)}), f32[4,4,16,512]{3,2,1,0:T(8,128)}, u32[]{:S(2)}, u32[]{:S(2)}) async-start(f32[4,4,16,512]{3,2,1,0:T(8,128)} %bitcast.408), calls=%async_computation.6 | async-start | bytes 1048576 | tf_op jit(solution)/shard_map/all_to_all | solution.py:125
  200.4 10.1 %collective-permute-start.4 = (f32[16,512]{1,0:T(8,128)}, f32[16,512]{1,0:T(8,128)}, u32[]{:S(2)}, u32[]{:S(2)}) collective-permute-start(f32[16,512]{1,0:T(8,128)} %get-tuple-element.93), channel_id=1, source_target_pairs={{0,2},{1,3},{2,0},{3,1},{4,6},{5,7},{6,4},{7,5},{8,10},{9,11},{10,... | collective-permute-start | bytes 98312 | tf_op jit(solution)/shard_map/ppermute | solution.py:166
  201.2 9.3 %collective-permute-start.5 = (f32[16,512]{1,0:T(8,128)}, f32[16,512]{1,0:T(8,128)}, u32[]{:S(2)}, u32[]{:S(2)}) collective-permute-start(f32[16,512]{1,0:T(8,128)} %get-tuple-element.92), channel_id=1, source_target_pairs={{0,4},{1,5},{2,6},{3,7},{4,0},{5,1},{6,2},{7,3},{8,12},{9,13},{10,... | collective-permute-start | bytes 98312 | tf_op jit(solution)/shard_map/ppermute | solution.py:166
  202.2 8.3 %collective-permute-start.6 = (f32[16,512]{1,0:T(8,128)}, f32[16,512]{1,0:T(8,128)}, u32[]{:S(2)}, u32[]{:S(2)}) collective-permute-start(f32[16,512]{1,0:T(8,128)} %get-tuple-element.91), channel_id=1, source_target_pairs={{0,6},{1,7},{2,4},{3,5},{4,2},{5,3},{6,0},{7,1},{8,14},{9,15},{10,... | collective-permute-start | bytes 98312 | tf_op jit(solution)/shard_map/ppermute | solution.py:166
  214.5 18.7 %all-to-all-start.7 = ((f32[8,2,16,512]{3,2,1,0:T(8,128)}), f32[8,2,16,512]{3,2,1,0:T(8,128)}, u32[]{:S(2)}, u32[]{:S(2)}) async-start(f32[8,2,16,512]{3,2,1,0:T(8,128)} %scatter_fusion.7), calls=%async_computation.7 | async-start | bytes 1048576 | tf_op jit(solution)/shard_map/all_to_all | solution.py:96
  222.5 15.9 %collective-permute-start.10 = (f32[2,2,16,1664]{3,2,1,0:T(8,128)}, f32[2,2,16,1664]{3,2,1,0:T(8,128)S(1)}, u32[]{:S(2)}, u32[]{:S(2)}) collective-permute-start(f32[2,2,16,1664]{3,2,1,0:T(8,128)} %get-tuple-element.67), channel_id=1, source_target_pairs={{0,17},{1,16},{2,19},{3,18},{4,21},{5,20},{6,23},{7,22},{8,25},{9,... | collective-permute-start | bytes 1277960 | tf_op jit(solution)/shard_map/ppermute | solution.py:166
  225.8 19.1 %collective-permute-start.8 = (f32[2,2,16,1664]{3,2,1,0:T(8,128)}, f32[2,2,16,1664]{3,2,1,0:T(8,128)S(1)}, u32[]{:S(2)}, u32[]{:S(2)}) collective-permute-start(f32[2,2,16,1664]{3,2,1,0:T(8,128)} %get-tuple-element.69), channel_id=1, source_target_pairs={{0,16},{1,17},{2,18},{3,19},{4,20},{5,21},{6,22},{7,23},{8,24},{9,... | collective-permute-start | bytes 1277960 | tf_op jit(solution)/shard_map/ppermute | solution.py:166
  225.9 20.3 %collective-permute-start.9 = (f32[2,2,16,1664]{3,2,1,0:T(8,128)S(1)}, f32[2,2,16,1664]{3,2,1,0:T(8,128)S(1)}, u32[]{:S(2)}, u32[]{:S(2)}) collective-permute-start(f32[2,2,16,1664]{3,2,1,0:T(8,128)S(1)} %get-tuple-element.68), channel_id=1, source_target_pairs={{0,1},{1,0},{2,3},{3,2},{4,5},{5,4},{6,7},{7,6},{8,9},{9,8},{10,11... | collective-permute-start | bytes 1277960 | tf_op jit(solution)/shard_map/ppermute | solution.py:166
  268.4 14.5 %collective-permute-start.14 = (f32[2,2,2,2,16,512]{5,4,3,2,1,0:T(8,128)S(1)}, f32[2,2,2,2,16,512]{5,4,3,2,1,0:T(8,128)S(1)}, u32[]{:S(2)}, u32[]{:S(2)}) collective-permute-start(f32[2,2,2,2,16,512]{5,4,3,2,1,0:T(8,128)S(1)} %dynamic-slice_bitcast_fusion.2), channel_id=1, source_target_pairs={{0,8},{1,9},{2,10},{3,11},{4,12},{5,13},{6,14},{7,15},{8,0},{9,1},... | collective-permute-start | bytes 1572872 | tf_op jit(solution)/shard_map/ppermute | solution.py:166
  271.6 11.3 %collective-permute-start.12 = (f32[16,1664]{1,0:T(8,128)S(1)}, f32[16,1664]{1,0:T(8,128)S(1)}, u32[]{:S(2)}, u32[]{:S(2)}) collective-permute-start(f32[16,1664]{1,0:T(8,128)S(1)} %get-tuple-element.86), channel_id=1, source_target_pairs={{0,4},{1,5},{2,6},{3,7},{4,0},{5,1},{6,2},{7,3},{8,12},{9,13},{10,... | collective-permute-start | bytes 319496 | tf_op jit(solution)/shard_map/ppermute | solution.py:166
  273.4 9.4 %collective-permute-start.13 = (f32[16,1664]{1,0:T(8,128)S(1)}, f32[16,1664]{1,0:T(8,128)S(1)}, u32[]{:S(2)}, u32[]{:S(2)}) collective-permute-start(f32[16,1664]{1,0:T(8,128)S(1)} %get-tuple-element.85), channel_id=1, source_target_pairs={{0,6},{1,7},{2,4},{3,5},{4,2},{5,3},{6,0},{7,1},{8,14},{9,15},{10,... | collective-permute-start | bytes 319496 | tf_op jit(solution)/shard_map/ppermute | solution.py:166
  296.0 16.0 %collective-permute-start.15 = (f32[2,2,2,2,16,1664]{5,4,3,2,1,0:T(8,128)S(1)}, f32[2,2,2,2,16,1664]{5,4,3,2,1,0:T(8,128)S(1)}, u32[]{:S(2)}, u32[]{:S(2)}) collective-permute-start(f32[2,2,2,2,16,1664]{5,4,3,2,1,0:T(8,128)S(1)} %dynamic-slice_bitcast_fusion), channel_id=1, source_target_pairs={{0,8},{1,9},{2,10},{3,11},{4,12},{5,13},{6,14},{7,15},{8,0},{9,1},... | collective-permute-start | bytes 5111816 | tf_op jit(solution)/shard_map/ppermute | solution.py:166
  298.5 8.3 %collective-permute-start.24 = (f32[2,2,16,512]{3,2,1,0:T(8,128)S(1)}, f32[2,2,16,512]{3,2,1,0:T(8,128)S(1)}, u32[]{:S(2)}, u32[]{:S(2)}) collective-permute-start(f32[2,2,16,512]{3,2,1,0:T(8,128)S(1)} %get-tuple-element.77), channel_id=1, source_target_pairs={{0,17},{1,16},{2,19},{3,18},{4,21},{5,20},{6,23},{7,22},{8,25},{9,... | collective-permute-start | bytes 393224 | tf_op jit(solution)/shard_map/ppermute | solution.py:166
  307.5 7.7 %collective-permute-start.25 = (f32[16,512]{1,0:T(8,128)S(1)}, f32[16,512]{1,0:T(8,128)S(1)}, u32[]{:S(2)}, u32[]{:S(2)}) collective-permute-start(f32[16,512]{1,0:T(8,128)S(1)} %get-tuple-element.88), channel_id=1, source_target_pairs={{0,2},{1,3},{2,0},{3,1},{4,6},{5,7},{6,4},{7,5},{8,10},{9,11},{10,... | collective-permute-start | bytes 98312 | tf_op jit(solution)/shard_map/ppermute | solution.py:166
  309.6 14.5 %collective-permute-start.26 = (f32[16,512]{1,0:T(8,128)}, f32[16,512]{1,0:T(8,128)S(1)}, u32[]{:S(2)}, u32[]{:S(2)}) collective-permute-start(f32[16,512]{1,0:T(8,128)} %get-tuple-element.90), channel_id=1, source_target_pairs={{0,4},{1,5},{2,6},{3,7},{4,0},{5,1},{6,2},{7,3},{8,12},{9,13},{10,... | collective-permute-start | bytes 98312 | tf_op jit(solution)/shard_map/ppermute | solution.py:166
  310.5 13.5 %collective-permute-start.27 = (f32[16,512]{1,0:T(8,128)S(1)}, f32[16,512]{1,0:T(8,128)}, u32[]{:S(2)}, u32[]{:S(2)}) collective-permute-start(f32[16,512]{1,0:T(8,128)S(1)} %get-tuple-element.89), channel_id=1, source_target_pairs={{0,6},{1,7},{2,4},{3,5},{4,2},{5,3},{6,0},{7,1},{8,14},{9,15},{10,... | collective-permute-start | bytes 98312 | tf_op jit(solution)/shard_map/ppermute | solution.py:166
  313.4 12.0 %collective-permute-start.16 = (f32[2,2,16,1664]{3,2,1,0:T(8,128)}, f32[2,2,16,1664]{3,2,1,0:T(8,128)S(1)}, u32[]{:S(2)}, u32[]{:S(2)}) collective-permute-start(f32[2,2,16,1664]{3,2,1,0:T(8,128)} %get-tuple-element.64), channel_id=1, source_target_pairs={{0,16},{1,17},{2,18},{3,19},{4,20},{5,21},{6,22},{7,23},{8,24},{9,... | collective-permute-start | bytes 1277960 | tf_op jit(solution)/shard_map/ppermute | solution.py:166
  314.9 14.4 %collective-permute-start.17 = (f32[2,2,16,1664]{3,2,1,0:T(8,128)}, f32[2,2,16,1664]{3,2,1,0:T(8,128)}, u32[]{:S(2)}, u32[]{:S(2)}) collective-permute-start(f32[2,2,16,1664]{3,2,1,0:T(8,128)} %get-tuple-element.66), channel_id=1, source_target_pairs={{0,1},{1,0},{2,3},{3,2},{4,5},{5,4},{6,7},{7,6},{8,9},{9,8},{10,11... | collective-permute-start | bytes 1277960 | tf_op jit(solution)/shard_map/ppermute | solution.py:166
  315.2 24.2 %collective-permute-start.18 = (f32[2,2,16,1664]{3,2,1,0:T(8,128)}, f32[2,2,16,1664]{3,2,1,0:T(8,128)}, u32[]{:S(2)}, u32[]{:S(2)}) collective-permute-start(f32[2,2,16,1664]{3,2,1,0:T(8,128)} %get-tuple-element.65), channel_id=1, source_target_pairs={{0,17},{1,16},{2,19},{3,18},{4,21},{5,20},{6,23},{7,22},{8,25},{9,... | collective-permute-start | bytes 1277960 | tf_op jit(solution)/shard_map/ppermute | solution.py:166
  320.4 25.3 %all-to-all-start.8 = ((f32[8,2,16,512]{3,2,1,0:T(8,128)}), f32[8,2,16,512]{3,2,1,0:T(8,128)S(1)}, u32[]{:S(2)}, u32[]{:S(2)}) async-start(f32[8,2,16,512]{3,2,1,0:T(8,128)} %bitcast.114), calls=%async_computation.8 | async-start | bytes 1048576 | tf_op jit(solution)/shard_map/all_to_all | solution.py:106
  340.7 6.8 %collective-permute-start.19 = (f32[16,1664]{1,0:T(8,128)S(1)}, f32[16,1664]{1,0:T(8,128)S(1)}, u32[]{:S(2)}, u32[]{:S(2)}) collective-permute-start(f32[16,1664]{1,0:T(8,128)S(1)} %get-tuple-element.82), channel_id=1, source_target_pairs={{0,2},{1,3},{2,0},{3,1},{4,6},{5,7},{6,4},{7,5},{8,10},{9,11},{10,... | collective-permute-start | bytes 319496 | tf_op jit(solution)/shard_map/ppermute | solution.py:166
  341.5 6.7 %collective-permute-start.20 = (f32[16,1664]{1,0:T(8,128)S(1)}, f32[16,1664]{1,0:T(8,128)S(1)}, u32[]{:S(2)}, u32[]{:S(2)}) collective-permute-start(f32[16,1664]{1,0:T(8,128)S(1)} %get-tuple-element.84), channel_id=1, source_target_pairs={{0,4},{1,5},{2,6},{3,7},{4,0},{5,1},{6,2},{7,3},{8,12},{9,13},{10,... | collective-permute-start | bytes 319496 | tf_op jit(solution)/shard_map/ppermute | solution.py:166
  343.7 6.6 %collective-permute-start.21 = (f32[16,1664]{1,0:T(8,128)S(1)}, f32[16,1664]{1,0:T(8,128)S(1)}, u32[]{:S(2)}, u32[]{:S(2)}) collective-permute-start(f32[16,1664]{1,0:T(8,128)S(1)} %get-tuple-element.83), channel_id=1, source_target_pairs={{0,6},{1,7},{2,4},{3,5},{4,2},{5,3},{6,0},{7,1},{8,14},{9,15},{10,... | collective-permute-start | bytes 319496 | tf_op jit(solution)/shard_map/ppermute | solution.py:166
  (53 other events, 348.1 us)

commit v3 on v2

--- a/solution.py
+++ b/solution.py
@@ -17,36 +17,59 @@
 epsilon = 1e-05
 
 
-def project_rows(rows_in, gain_row, qkv_weight):
-    row_count = rows_in.shape[0]
+def normalize(rows_in, gain_row):
     row_mean = jnp.mean(rows_in, axis=-1, keepdims=True)
     centered = rows_in - row_mean
     row_var = jnp.mean(centered * centered, axis=-1, keepdims=True)
-    normed = centered * lax.rsqrt(row_var + epsilon) * gain_row
+    return centered * lax.rsqrt(row_var + epsilon) * gain_row
+
+
+def block_forward(rows_in, gain_row, qkv_weight, proj_weight):
+    row_count = rows_in.shape[0]
+    normed, pull_normalize = jax.vjp(normalize, rows_in, gain_row)
     projected = jnp.dot(normed, qkv_weight, precision=exact_mode)
-    return projected.reshape(row_count // PATCH, PATCH, 3, HEADS, D // HEADS)
-
-
-def attend(projected):
-    queries = projected[:, :, 0]
-    key_rows = projected[:, :, 1]
-    value_rows = projected[:, :, 2]
+    heads = projected.reshape(row_count // PATCH, PATCH, 3, HEADS, D // HEADS)
+    queries, key_rows, value_rows = heads[:, :, 0], heads[:, :, 1], heads[:, :, 2]
     scores = jnp.einsum("pihd,pjhd->phij", queries, key_rows, precision=exact_mode) * (
         1.0 / math.sqrt(D // HEADS)
     )
     attention = jax.nn.softmax(scores, axis=-1)
-    return jnp.einsum("phij,pjhd->pihd", attention, value_rows, precision=fast_mode)
-
-
-def leave_block(rows_in, mixed_rows, proj_weight):
-    return rows_in + jnp.dot(mixed_rows.reshape(rows_in.shape), proj_weight, precision=fast_mode)
-
-
-def block_forward(rows_in, gain_row, qkv_weight, proj_weight):
-    projected, pull_project = jax.vjp(project_rows, rows_in, gain_row, qkv_weight)
-    mixed_rows, pull_attend = jax.vjp(attend, projected)
-    rows_out, pull_leave = jax.vjp(leave_block, rows_in, mixed_rows, proj_weight)
-    return (rows_out, pull_project, pull_attend, pull_leave)
+    mixed_heads = jnp.einsum("phij,pjhd->pihd", attention, value_rows, precision=fast_mode)
+    mixed_rows = mixed_heads.reshape(row_count, D)
+    saved = (normed, queries, key_rows, value_rows, attention, mixed_rows, pull_normalize)
+    return (mixed_rows, saved)
+
+
+def mixed_grads(grad_out, saved, proj_weight):
+    mixed_rows = saved[5]
+    grad_mixed = jnp.dot(grad_out, proj_weight.T, precision=fast_mode)
+    proj_grad = jnp.dot(mixed_rows.T, grad_out, precision=fast_mode)
+    return (grad_mixed, proj_grad)
+
+
+def value_grads(grad_mixed, saved):
+    attention = saved[4]
+    grad_heads = grad_mixed.reshape(-1, PATCH, HEADS, D // HEADS)
+    grad_value = jnp.einsum("phij,pihd->pjhd", attention, grad_heads, precision=fast_mode)
+    return (grad_heads, grad_value.reshape(grad_mixed.shape))
+
+
+def score_grads(grad_heads, saved):
+    normed, queries, key_rows, value_rows, attention = saved[:5]
+    grad_attention = jnp.einsum("pihd,pjhd->phij", grad_heads, value_rows, precision=fast_mode)
+    along = jnp.sum(attention * grad_attention, axis=-1, keepdims=True)
+    grad_scores = attention * (grad_attention - along) * (1.0 / math.sqrt(D // HEADS))
+    grad_query = jnp.einsum("phij,pjhd->pihd", grad_scores, key_rows, precision=fast_mode)
+    grad_key = jnp.einsum("phij,pihd->pjhd", grad_scores, queries, precision=fast_mode)
+    return (grad_query.reshape(normed.shape), grad_key.reshape(normed.shape))
+
+
+def weight_grad(saved, grad_projected):
+    return jnp.dot(saved[0].T, grad_projected, precision=fast_mode)
+
+
+def normed_grad(grad_projected, qkv_weight):
+    return jnp.dot(grad_projected, qkv_weight.T, precision=fast_mode)
 
 
 def occupancy(owner_index):
@@ -187,9 +210,9 @@
     return groups + ([y_bits + low] if len(y_bits + low) < 3 else [y_bits, low]) + [high]
 
 
-def with_gain(proj_part, gain_part):
+def with_gain(parts, gain_part):
     gain_wide = jnp.broadcast_to(gain_part[:, None], (gain_part.shape[0], 128))
-    return jnp.concatenate([proj_part, gain_wide], axis=1)
+    return jnp.concatenate(list(parts) + [gain_wide], axis=1)
 
 
 def per_device(points, upstream, gains, w_qkv, w_proj, z_route, h_route):
@@ -198,43 +221,48 @@
     tall = w_proj.shape[2]
     curve_first, z_source, z_occur = to_zorder(points, z_route)
     grad_curve, unused_source, unused_occur = to_hilbert(upstream, h_route)
-    first_out, project_first, attend_first, leave_first = block_forward(
-        curve_first, gains[0], w_qkv[0], w_proj[0]
-    )
+    mixed_first, saved_first = block_forward(curve_first, gains[0], w_qkv[0], w_proj[0])
+    mixed_out, grad_curve = lax.optimization_barrier((mixed_first, grad_curve))
+    first_out = curve_first + jnp.dot(mixed_out, w_proj[0], precision=fast_mode)
     middle = from_zorder(first_out, z_source, z_occur, z_route)
     curve_second, h_source, h_occur = to_hilbert(middle, h_route)
-    second_out, project_second, attend_second, leave_second = block_forward(
-        curve_second, gains[1], w_qkv[1], w_proj[1]
-    )
-    straight, grad_mixed, proj_second = leave_second(grad_curve)
-    proj_sum = ScatterSum(proj_second, groups)
-    (grad_projected,) = attend_second(grad_mixed)
-    grad_projected = proj_sum.meet(grad_projected)
-    around, gain_second, qkv_second = project_second(grad_projected)
-    around = proj_sum.meet(around)
-    qkv_sum = ScatterSum(with_gain(qkv_second, gain_second), groups)
-    grad_middle = from_hilbert(straight + around, h_source, h_occur, h_route)
-    grad_middle = proj_sum.meet(grad_middle)
-    proj_second = proj_sum.finish()
-    grad_middle = qkv_sum.meet(grad_middle)
+    unused_mixed, saved_second = block_forward(curve_second, gains[1], w_qkv[1], w_proj[1])
+
+    grad_mixed, proj_second = mixed_grads(grad_curve, saved_second, w_proj[1])
+    grad_heads, grad_value = value_grads(grad_mixed, saved_second)
+    grad_projected = jnp.concatenate(
+        [*score_grads(grad_heads, saved_second), grad_value], axis=1
+    )
+    qkv_second = weight_grad(saved_second, grad_projected)
+    around, gain_second = saved_second[6](normed_grad(grad_projected, w_qkv[1]))
+    second_sum = ScatterSum(with_gain([qkv_second, proj_second], gain_second), groups)
+
+    grad_middle = from_hilbert(grad_curve + around, h_source, h_occur, h_route)
+    grad_middle = second_sum.meet(grad_middle)
     middle_curve, unused_again, unused_spots = to_zorder(grad_middle, z_route)
-    straight, grad_mixed, proj_first = leave_first(middle_curve)
-    grad_mixed = qkv_sum.meet(grad_mixed)
-    proj_sum = ScatterSum(proj_first, groups)
-    (grad_projected,) = attend_first(grad_mixed)
-    grad_projected = qkv_sum.meet(grad_projected)
-    grad_projected = proj_sum.meet(grad_projected)
-    second_sum = qkv_sum.finish()
-    around, gain_first, qkv_first = project_first(grad_projected)
-    qkv_sum = ScatterSum(with_gain(qkv_first, gain_first), groups)
-    point_grad = from_zorder(straight + around, z_source, z_occur, z_route)
-    proj_first = proj_sum.finish()
-    first_sum = qkv_sum.finish()
+    grad_mixed, proj_first = mixed_grads(middle_curve, saved_first, w_proj[0])
+    grad_heads, grad_value = value_grads(grad_mixed, saved_first)
+    grad_heads = second_sum.meet(grad_heads)
+    value_first = weight_grad(saved_first, grad_value)
+    early_sum = ScatterSum(jnp.concatenate([value_first, proj_first], axis=1), groups)
+    grad_query, grad_key = score_grads(grad_heads, saved_first)
+    grad_pair = jnp.concatenate([grad_query, grad_key], axis=1)
+    grad_pair = second_sum.meet(grad_pair)
+    grad_pair = early_sum.meet(grad_pair)
+    second = second_sum.finish()
+    grad_normed = normed_grad(jnp.concatenate([grad_pair, grad_value], axis=1), w_qkv[0])
+    around, gain_first = saved_first[6](grad_normed)
+    late_sum = ScatterSum(with_gain([weight_grad(saved_first, grad_pair)], gain_first), groups)
+    point_grad = from_zorder(middle_curve + around, z_source, z_occur, z_route)
+    early = early_sum.finish()
+    late = late_sum.finish()
+    pair_wide = wide - tall
+    qkv_first = jnp.concatenate([late[:, :pair_wide], early[:, :tall]], axis=1)
     return (
         point_grad,
-        jnp.stack([first_sum[:, wide], second_sum[:, wide]]),
-        jnp.stack([first_sum[:, :wide], second_sum[:, :wide]]),
-        jnp.stack([proj_first, proj_second]),
+        jnp.stack([late[:, pair_wide], second[:, wide + tall]]),
+        jnp.stack([qkv_first, second[:, :wide]]),
+        jnp.stack([early[:, tall:], second[:, wide : wide + tall]]),
     )
 
 

time: 357 us -> 336 us (0.941)
  blocking collectives: 0 us -> 18.1 us
  matrix products: 94.7 us -> 79.8 us
  starting transfers between devices: 71.9 us -> 59.7 us
  local copies, waits for them, and re-layouts: 80.4 us -> 72.3 us
    all_to_all x0 -> x1, blocking collectives: none -> 18.1 us  [from_zorder(): lax.all_to_all(buffer, 'gy', split_axis=0, concat_axis=0, tiled=True)]
    dot_general x23 -> x24, matrix products: 94.7 us -> 79.8 us  [the longest x2 13.6 us: block_forward(): jnp.einsum('pihd,pjhd->phij', queries, key_rows, precision=exact_mode)]
    all_to_all x2 -> x1, waiting for transfers between devices: 10.6 us -> 0.01 us  [from_zorder(): lax.all_to_all(buffer, 'gy', split_axis=0, concat_axis=0, tiled=True)]
    all_to_all x1, waiting for transfers between devices: 0.01 us -> 8.57 us  [from_hilbert(): lax.all_to_all(buffer, 'gx', split_axis=0, concat_axis=0, tiled=True)]
    ppermute x28 -> x21, starting transfers between devices: 32.9 us -> 25.1 us  [send_next(): self.received.append(lax.ppermute(sent, mesh_axes, swaps))]
    all_to_all x2, waiting for transfers between devices: 9.31 us -> 16.1 us  [to_zorder(): lax.all_to_all(buffer, 'gy', split_axis=0, concat_axis=0, tiled=True)]
    ppermute x28 -> x21, waiting for transfers between devices: 48 us -> 42.2 us  [send_next(): self.received.append(lax.ppermute(sent, mesh_axes, swaps))]
    transpose x2 -> x8, local copies, waits for them, and re-layouts: 0.82 us -> 5.1 us  [the longest x2 1.86 us: block_forward(): jnp.einsum('phij,pjhd->pihd', attention, value_rows, precision=fast_mode)]
  transfers between devices with their start and end apart: 37 -> 29, of which waited for: 23 -> 16; matrix products, arithmetic and copies ran while one was open for 26% -> 17% of each run, Pallas kernels for 0% -> 0%
where the time goes in v3:
time: 336 us; the launch traced here: 330 us
  matrix products  79.8 us (24%)
  local copies, waits for them, and re-layouts  72.3 us (22%)
  waiting for transfers between devices  71.6 us (21%)
  starting transfers between devices  59.7 us (18%)
  other arithmetic  26.9 us (8%)
  blocking collectives  18.1 us (5%)
    ppermute x21, waiting for transfers between devices, send_next(): self.received.append(lax.ppermute(sent, mesh_axes, swaps))  42.2 us
    ppermute x21, starting transfers between devices, send_next(): self.received.append(lax.ppermute(sent, mesh_axes, swaps))  25.1 us
    all_to_all x1, blocking collectives, from_zorder(): lax.all_to_all(buffer, 'gy', split_axis=0, concat_axis=0, tiled=True)  18.1 us
    all_to_all x2, waiting for transfers between devices, to_zorder(): lax.all_to_all(buffer, 'gy', split_axis=0, concat_axis=0, tiled=True)  16.1 us
    dot_general x2, matrix products, block_forward(): jnp.einsum('pihd,pjhd->phij', queries, key_rows, precision=exact_mode)  13.6 us
    scatter x4, local copies, waits for them, and re-layouts, spread_out(): buffer = jnp.zeros((peer_count, per_peer) + segments.shape[1:], rows_in.d...  11.7 us
    unnamed x68, local copies, waits for them, and re-layouts  10.4 us
    dot_general x2, matrix products, value_grads(): jnp.einsum('phij,pihd->pjhd', attention, grad_heads, precision=fast_mode)  8.64 us
  transfers between devices with their start and end apart: 29, of which 16 were waited for; matrix products, arithmetic and copies ran while one was open for 17% of the time, Pallas kernels for 0%

profile of v3, /device:TPU:0, one launch (start us, length us, event | category | flops | bytes accessed | tf_op | source)
XLA Modules:
  0.0 330.3 jit_solution(13005874960607411715)
XLA Ops:
  5.8 4.3 %all-to-all-start.1 = ((s32[4,1,4]{2,1,0:T(1,128)}), s32[4,1,4]{2,1,0:T(1,128)S(1)}, u32[]{:S(2)}, u32[]{:S(2)}) async-start(s32[4,1,4]{2,1,0:T(1,128)} %bitcast.14), calls=%async_computation.1 | async-start | bytes 4096 | tf_op jit(solution)/shard_map/all_to_all | solution.py:139
  13.8 6.2 %all-to-all-start = ((s32[8,1,2]{2,1,0:T(1,128)}), s32[8,1,2]{2,1,0:T(1,128)S(1)}, u32[]{:S(2)}, u32[]{:S(2)}) async-start(s32[8,1,2]{2,1,0:T(1,128)} %copy.124), calls=%async_computation | async-start | bytes 8192 | tf_op jit(solution)/shard_map/all_to_all | solution.py:120
  26.4 4.2 %all-to-all-start.3 = ((f32[4,4,16,512]{3,2,1,0:T(8,128)}), f32[4,4,16,512]{3,2,1,0:T(8,128)}, u32[]{:S(2)}, u32[]{:S(2)}) async-start(f32[4,4,16,512]{3,2,1,0:T(8,128)} %scatter_fusion.3), calls=%async_computation.3 | async-start | bytes 1048576 | tf_op jit(solution)/shard_map/all_to_all | solution.py:138
  30.6 6.0 %fusion.106 = (f32[1,512,1536]{2,1,0:T(8,128)}, f32[1,512,1536]{2,1,0:T(8,128)}) fusion(f32[2,512,1536]{2,1,0:T(8,128)} %param.10), kind=kLoop, calls=%fused_computation.241 | loop fusion | bytes 12582912 | tf_op jit(solution)/shard_map/slice | solution.py:229
  42.9 4.3 %all-to-all-start.2 = ((f32[8,2,16,512]{3,2,1,0:T(8,128)}), f32[8,2,16,512]{3,2,1,0:T(8,128)}, u32[]{:S(2)}, u32[]{:S(2)}) async-start(f32[8,2,16,512]{3,2,1,0:T(8,128)} %scatter_fusion.2), calls=%async_computation.2 | async-start | bytes 1048576 | tf_op jit(solution)/shard_map/all_to_all | solution.py:119
  51.9 10.5 %all-to-all-done.2 = f32[8,2,16,512]{3,2,1,0:T(8,128)} async-done(((f32[8,2,16,512]{3,2,1,0:T(8,128)}), f32[8,2,16,512]{3,2,1,0:T(8,128)}, u32[]{:S(2)}, u32[]{:S(2)}) %all-to-all-start.2) | async-done | bytes 524320 | tf_op jit(solution)/shard_map/all_to_all | solution.py:119
  68.5 4.2 %fusion.10 = f32[2,128,3,32,16]{1,3,4,2,0:T(8,128)S(1)} fusion(f32[2,128,512,1,1]{2,1,4,3,0:T(8,128)S(1)} %bitcast.343, f32[3,32,16,512]{3,2,1,0:T(8,128)S(1)} %bitcast.326), kind=kOutput, calls=%fused_computation.35 | convolution fusion | flops 2415919104 | bytes 5242880 | tf_op jit(solution)/shard_map/dot_general | solution.py:30
  73.7 6.7 %multiply_reduce_fusion.3 = (f32[2,32,128]{2,1,0:T(8,128)S(1)}, f32[2,32,128,128]{2,3,1,0:T(8,128)S(1)}) fusion(f32[2,128,32,16]{1,2,3,0:T(8,128)S(1)} %get-tuple-element.55, f32[2,128,32,16]{1,2,3,0:T(8,128)S(1)} %get-tuple-element.54), kind=kOutput, calls=%fused_computation.24 | convolution fusion | flops 203415552 | bytes 5275648 | tf_op jit(solution)/shard_map/pihd,pjhd->phij/dot_general | solution.py:33
  86.6 18.1 %all_to_all.55 = f32[8,2,16,512]{3,2,1,0:T(8,128)S(1)} all-to-all(f32[8,2,16,512]{3,2,1,0:T(8,128)S(1)} %bitcast.345), channel_id=1, replica_groups=mesh['gx'=4,'gy'=8] {'gy'}, dimensions={0} | all-to-all | bytes 1048576 | tf_op jit(solution)/shard_map/all_to_all | solution.py:129
  108.9 4.2 %all-to-all-start.5 = ((f32[4,4,16,512]{3,2,1,0:T(8,128)}), f32[4,4,16,512]{3,2,1,0:T(8,128)}, u32[]{:S(2)}, u32[]{:S(2)}) async-start(f32[4,4,16,512]{3,2,1,0:T(8,128)} %scatter_fusion.5), calls=%async_computation.5 | async-start | bytes 1048576 | tf_op jit(solution)/shard_map/all_to_all | solution.py:138
  128.0 4.2 %fusion.8 = f32[2,128,3,32,16]{1,3,4,2,0:T(8,128)S(1)} fusion(f32[2,128,512,1,1]{2,1,4,3,0:T(8,128)S(1)} %bitcast.352, f32[3,32,16,512]{3,2,1,0:T(8,128)S(1)} %bitcast.327), kind=kOutput, calls=%fused_computation.33 | convolution fusion | flops 2415919104 | bytes 5242880 | tf_op jit(solution)/shard_map/dot_general | solution.py:30
  132.4 6.9 %multiply_reduce_fusion.2 = (f32[2,32,128]{2,1,0:T(8,128)S(1)}, f32[2,32,128,128]{2,3,1,0:T(8,128)S(1)}) fusion(f32[2,128,32,16]{1,2,3,0:T(8,128)S(1)} %get-tuple-element.53, f32[2,128,32,16]{1,2,3,0:T(8,128)S(1)} %get-tuple-element.51), kind=kOutput, calls=%fused_computation.23 | convolution fusion | flops 203415552 | bytes 5275648 | tf_op jit(solution)/shard_map/pihd,pjhd->phij/dot_general | solution.py:33
  140.4 3.4 %convolution_bitcast_fusion.2 = f32[2,128,32,16]{1,3,2,0:T(8,128)S(1)} fusion(f32[2,128,32,16]{1,3,2,0:T(8,128)S(1)} %copy-done.21, f32[2,32,128,128]{2,3,1,0:T(8,128)S(1)} %get-tuple-element.91, f32[2,32,128]{2,1,0:T(8,128)S(1)} %fusion.3, f32[2,32,128]{2,1,0:T(8,128)S(1)} %get-tuple-element.90), kind=kOutput, calls=%fused_computation.57 | convolution fusion | flops 103809024 | bytes 5308416 | tf_op jit(solution)/shard_map/phij,pihd->pjhd/dot_general | solution.py:53
  143.7 3.8 %multiply_reduce_fusion.1 = (f32[2,32,128]{2,1,0:T(8,128)S(1)}, f32[2,32,128,128]{2,3,1,0:T(8,128)S(1)}) fusion(f32[2,32,128]{2,1,0:T(8,128)S(1)} %fusion.3, f32[2,32,128]{2,1,0:T(8,128)S(1)} %get-tuple-element.90, f32[2,32,128,128]{2,3,1,0:T(8,128)S(1)} %get-tuple-element.91, f32[2,128,32,16]{1,3,2,0:T(8,128)S(1)} %copy-done.21, ...), kind=kOutput, calls=%fused_computation.20 | convolution fusion | flops 105897984 | bytes 9535488 | tf_op jit(solution)/shard_map/pihd,pjhd->phij/dot_general | solution.py:59
  147.5 3.8 %fusion.24 = f32[2,128,32,16]{1,3,2,0:T(8,128)S(1)} fusion(f32[2,32,128,128]{2,3,1,0:T(8,128)S(1)} %get-tuple-element.93, f32[2,32,128]{2,1,0:T(8,128)S(1)} %get-tuple-element.92, f32[2,128,32,16]{1,2,3,0:T(8,128)S(1)} %get-tuple-element.51, f32[2,32,128,128]{2,3,1,0:T(8,128)S(1)} %get-tuple-element.91, f32[2,32,128]{2,1,0:T(8,128)S(1)} %fusion.3, ...), kind=kOutput, calls=%fused_computation.54 | convolution fusion | flops 106954752 | bytes 9535488 | tf_op jit(solution)/shard_map/phij,pihd->pjhd/dot_general | solution.py:63
  154.6 5.3 %convolution_bitcast_fusion.1 = f32[2,128,32,16]{1,3,2,0:T(8,128)} fusion(f32[2,128,32,16]{1,2,3,0:T(8,128)S(1)} %get-tuple-element.52, f32[2,32,128,128]{2,3,1,0:T(8,128)} %copy-done.5, f32[2,32,128]{2,1,0:T(8,128)S(1)} %fusion.3, f32[2,32,128]{2,1,0:T(8,128)S(1)} %get-tuple-element.90), kind=kOutput, calls=%fused_computation.56 | convolution fusion | flops 103809024 | bytes 5308416 | tf_op jit(solution)/shard_map/phij,pjhd->pihd/dot_general | solution.py:37
  165.2 4.6 %multiply_reduce_fusion.7 = (f32[256]{0:T(256)S(1)}, f32[256,512]{1,0:T(8,128)S(1)}, f32[256,512]{1,0:T(8,128)S(1)}) fusion(f32[512]{0:T(512)S(1)} %bitcast.378, f32[256]{0:T(256)S(1)} %div.96, f32[16,16,512]{2,1,0:T(8,128)S(1)} %copy-done.6, f32[256,1536]{0,1:T(8,128)S(1)} %bitcast_dynamic-update-slice_fusion, f32[2,512,1536]{2,1,0:T(8,128)} %param.10), kind=kOutput, calls=%fused_computation.106 | convolution fusion | flops 1208483584 | bytes 6295552 | tf_op jit(solution)/shard_map/dot_general | solution.py:72
  180.9 3.5 %all-to-all-start.6 = ((f32[4,4,16,512]{3,2,1,0:T(8,128)}), f32[4,4,16,512]{3,2,1,0:T(8,128)S(1)}, u32[]{:S(2)}, u32[]{:S(2)}) async-start(f32[4,4,16,512]{3,2,1,0:T(8,128)} %bitcast.61), calls=%async_computation.6 | async-start | bytes 1048576 | tf_op jit(solution)/shard_map/all_to_all | solution.py:148
  184.6 8.6 %all-to-all-done.6 = f32[4,4,16,512]{3,2,1,0:T(8,128)S(1)} async-done(((f32[4,4,16,512]{3,2,1,0:T(8,128)}), f32[4,4,16,512]{3,2,1,0:T(8,128)S(1)}, u32[]{:S(2)}, u32[]{:S(2)}) %all-to-all-start.6) | async-done | bytes 524320 | tf_op jit(solution)/shard_map/all_to_all | solution.py:148
  197.4 3.6 %all-to-all-start.7 = ((f32[8,2,16,512]{3,2,1,0:T(8,128)}), f32[8,2,16,512]{3,2,1,0:T(8,128)S(1)}, u32[]{:S(2)}, u32[]{:S(2)}) async-start(f32[8,2,16,512]{3,2,1,0:T(8,128)} %scatter_fusion.7), calls=%async_computation.7 | async-start | bytes 1048576 | tf_op jit(solution)/shard_map/all_to_all | solution.py:119
  209.8 5.5 %all-to-all-done.7 = f32[8,2,16,512]{3,2,1,0:T(8,128)S(1)} async-done(((f32[8,2,16,512]{3,2,1,0:T(8,128)}), f32[8,2,16,512]{3,2,1,0:T(8,128)S(1)}, u32[]{:S(2)}, u32[]{:S(2)}) %all-to-all-start.7) | async-done | bytes 524320 | tf_op jit(solution)/shard_map/all_to_all | solution.py:119
  217.1 5.3 %convolution_bitcast_fusion = f32[2,128,32,16]{1,3,2,0:T(8,128)S(1)} fusion(f32[2,128,32,16]{1,2,3,0:T(8,128)S(1)} %fusion.25, f32[2,32,128,128]{2,3,1,0:T(8,128)} %copy-done.3, f32[2,32,128]{2,1,0:T(8,128)S(1)} %fusion.1, f32[2,32,128]{2,1,0:T(8,128)S(1)} %get-tuple-element.88), kind=kOutput, calls=%fused_computation.55 | convolution fusion | flops 103809024 | bytes 5308416 | tf_op jit(solution)/shard_map/phij,pihd->pjhd/dot_general | solution.py:53
  223.7 11.4 %collective-permute-done.3 = f32[2,2,16,2176]{3,2,1,0:T(8,128)} collective-permute-done((f32[2,2,16,2176]{3,2,1,0:T(8,128)}, f32[2,2,16,2176]{3,2,1,0:T(8,128)}, u32[]{:S(2)}, u32[]{:S(2)}) %collective-permute-start.3) | collective-permute-done | bytes 557088 | tf_op jit(solution)/shard_map/ppermute | solution.py:189
  235.1 3.8 %multiply_reduce_fusion = (f32[2,32,128]{2,1,0:T(8,128)S(1)}, f32[2,32,128,128]{2,3,1,0:T(8,128)S(1)}) fusion(f32[2,32,128]{2,1,0:T(8,128)S(1)} %fusion.1, f32[2,32,128]{2,1,0:T(8,128)S(1)} %get-tuple-element.88, f32[2,32,128,128]{2,3,1,0:T(8,128)S(1)} %copy-done.4, f32[2,128,32,16]{1,2,3,0:T(8,128)S(1)} %copy-done.26, f32[2,128,32,16]{1,2,3,0:T(8,128)S(1)} %fusion.25), kind=kOutput, calls=%fused_computation.18 | convolution fusion | flops 105897984 | bytes 9535488 | tf_op jit(solution)/shard_map/pihd,pjhd->phij/dot_general | solution.py:59
  238.9 3.6 %fusion.21 = f32[2,128,32,16]{1,3,2,0:T(8,128)} fusion(f32[2,32,128,128]{2,3,1,0:T(8,128)S(1)} %get-tuple-element.96, f32[2,32,128]{2,1,0:T(8,128)S(1)} %get-tuple-element.95, f32[2,128,32,16]{1,2,3,0:T(8,128)S(1)} %copy-done.20, f32[2,32,128,128]{2,3,1,0:T(8,128)S(1)} %copy-done.4, f32[2,32,128]{2,1,0:T(8,128)S(1)} %fusion.1, ...), kind=kOutput, calls=%fused_computation.51 | convolution fusion | flops 106954752 | bytes 9535488 | tf_op jit(solution)/shard_map/phij,pjhd->pihd/dot_general | solution.py:62
  242.5 4.6 %fusion.22 = f32[2,128,32,16]{1,3,2,0:T(8,128)} fusion(f32[2,32,128,128]{2,3,1,0:T(8,128)S(1)} %get-tuple-element.96, f32[2,32,128]{2,1,0:T(8,128)S(1)} %get-tuple-element.95, f32[2,128,32,16]{1,2,3,0:T(8,128)S(1)} %copy-done.18, f32[2,32,128,128]{2,3,1,0:T(8,128)S(1)} %copy-done.4, f32[2,32,128]{2,1,0:T(8,128)S(1)} %fusion.1, ...), kind=kOutput, calls=%fused_computation.52 | convolution fusion | flops 106954752 | bytes 9535488 | tf_op jit(solution)/shard_map/phij,pihd->pjhd/dot_general | solution.py:63
  250.3 3.2 copy.165
  261.9 8.0 %collective-permute-done.5 = f32[16,2176]{1,0:T(8,128)S(1)} collective-permute-done((f32[16,2176]{1,0:T(8,128)S(1)}, f32[16,2176]{1,0:T(8,128)S(1)}, u32[]{:S(2)}, u32[]{:S(2)}) %collective-permute-start.5) | collective-permute-done | bytes 139296 | tf_op jit(solution)/shard_map/ppermute | solution.py:189
  285.0 4.4 %all-to-all-start.8 = ((f32[8,2,16,512]{3,2,1,0:T(8,128)}), f32[8,2,16,512]{3,2,1,0:T(8,128)S(1)}, u32[]{:S(2)}, u32[]{:S(2)}) async-start(f32[8,2,16,512]{3,2,1,0:T(8,128)} %bitcast.90), calls=%async_computation.8 | async-start | bytes 1048576 | tf_op jit(solution)/shard_map/all_to_all | solution.py:129
  289.4 6.4 %collective-permute-done.17 = f32[2,2,16,1024]{3,2,1,0:T(8,128)} collective-permute-done((f32[2,2,16,1024]{3,2,1,0:T(8,128)}, f32[2,2,16,1024]{3,2,1,0:T(8,128)}, u32[]{:S(2)}, u32[]{:S(2)}) %collective-permute-start.17) | collective-permute-done | bytes 262176 | tf_op jit(solution)/shard_map/ppermute | solution.py:189
  308.6 5.1 %collective-permute-done.10 = f32[2,2,16,1152]{3,2,1,0:T(8,128)S(1)} collective-permute-done((f32[2,2,16,1152]{3,2,1,0:T(8,128)S(1)}, f32[2,2,16,1152]{3,2,1,0:T(8,128)S(1)}, u32[]{:S(2)}, u32[]{:S(2)}) %collective-permute-start.10) | collective-permute-done | bytes 294944 | tf_op jit(solution)/shard_map/ppermute | solution.py:189
  313.7 4.2 %collective-permute-done.11 = f32[2,2,16,1152]{3,2,1,0:T(8,128)S(1)} collective-permute-done((f32[2,2,16,1152]{3,2,1,0:T(8,128)S(1)}, f32[2,2,16,1152]{3,2,1,0:T(8,128)S(1)}, u32[]{:S(2)}, u32[]{:S(2)}) %collective-permute-start.11) | collective-permute-done | bytes 294944 | tf_op jit(solution)/shard_map/ppermute | solution.py:189
  (237 shorter events, 146.5 us)
Async XLA Ops:
  5.8 8.0 %all-to-all-start.1 = ((s32[4,1,4]{2,1,0:T(1,128)}), s32[4,1,4]{2,1,0:T(1,128)S(1)}, u32[]{:S(2)}, u32[]{:S(2)}) async-start(s32[4,1,4]{2,1,0:T(1,128)} %bitcast.14), calls=%async_computation.1 | async-start | bytes 4096 | tf_op jit(solution)/shard_map/all_to_all | solution.py:139
  13.8 12.6 %all-to-all-start = ((s32[8,1,2]{2,1,0:T(1,128)}), s32[8,1,2]{2,1,0:T(1,128)S(1)}, u32[]{:S(2)}, u32[]{:S(2)}) async-start(s32[8,1,2]{2,1,0:T(1,128)} %copy.124), calls=%async_computation | async-start | bytes 8192 | tf_op jit(solution)/shard_map/all_to_all | solution.py:120
  26.4 16.5 %all-to-all-start.3 = ((f32[4,4,16,512]{3,2,1,0:T(8,128)}), f32[4,4,16,512]{3,2,1,0:T(8,128)}, u32[]{:S(2)}, u32[]{:S(2)}) async-start(f32[4,4,16,512]{3,2,1,0:T(8,128)} %scatter_fusion.3), calls=%async_computation.3 | async-start | bytes 1048576 | tf_op jit(solution)/shard_map/all_to_all | solution.py:138
  42.9 19.6 %all-to-all-start.2 = ((f32[8,2,16,512]{3,2,1,0:T(8,128)}), f32[8,2,16,512]{3,2,1,0:T(8,128)}, u32[]{:S(2)}, u32[]{:S(2)}) async-start(f32[8,2,16,512]{3,2,1,0:T(8,128)} %scatter_fusion.2), calls=%async_computation.2 | async-start | bytes 1048576 | tf_op jit(solution)/shard_map/all_to_all | solution.py:119
  108.9 13.0 %all-to-all-start.5 = ((f32[4,4,16,512]{3,2,1,0:T(8,128)}), f32[4,4,16,512]{3,2,1,0:T(8,128)}, u32[]{:S(2)}, u32[]{:S(2)}) async-start(f32[4,4,16,512]{3,2,1,0:T(8,128)} %scatter_fusion.5), calls=%async_computation.5 | async-start | bytes 1048576 | tf_op jit(solution)/shard_map/all_to_all | solution.py:138
  177.2 16.5 %collective-permute-start = (f32[2,2,2,2,16,2176]{5,4,3,2,1,0:T(8,128)}, f32[2,2,2,2,16,2176]{5,4,3,2,1,0:T(8,128)}, u32[]{:S(2)}, u32[]{:S(2)}) collective-permute-start(f32[2,2,2,2,16,2176]{5,4,3,2,1,0:T(8,128)} %dynamic-slice_bitcast_fusion), channel_id=1, source_target_pairs={{0,8},{1,9},{2,10},{3,11},{4,12},{5,13},{6,14},{7,15},{8,0},{9,1},... | collective-permute-start | bytes 6684680 | tf_op jit(solution)/shard_map/ppermute | solution.py:189
  180.9 12.3 %all-to-all-start.6 = ((f32[4,4,16,512]{3,2,1,0:T(8,128)}), f32[4,4,16,512]{3,2,1,0:T(8,128)S(1)}, u32[]{:S(2)}, u32[]{:S(2)}) async-start(f32[4,4,16,512]{3,2,1,0:T(8,128)} %bitcast.61), calls=%async_computation.6 | async-start | bytes 1048576 | tf_op jit(solution)/shard_map/all_to_all | solution.py:148
  197.4 17.9 %all-to-all-start.7 = ((f32[8,2,16,512]{3,2,1,0:T(8,128)}), f32[8,2,16,512]{3,2,1,0:T(8,128)S(1)}, u32[]{:S(2)}, u32[]{:S(2)}) async-start(f32[8,2,16,512]{3,2,1,0:T(8,128)} %scatter_fusion.7), calls=%async_computation.7 | async-start | bytes 1048576 | tf_op jit(solution)/shard_map/all_to_all | solution.py:119
  206.3 16.1 %collective-permute-start.1 = (f32[2,2,16,2176]{3,2,1,0:T(8,128)}, f32[2,2,16,2176]{3,2,1,0:T(8,128)S(1)}, u32[]{:S(2)}, u32[]{:S(2)}) collective-permute-start(f32[2,2,16,2176]{3,2,1,0:T(8,128)} %get-tuple-element.48), channel_id=1, source_target_pairs={{0,16},{1,17},{2,18},{3,19},{4,20},{5,21},{6,22},{7,23},{8,24},{9,... | collective-permute-start | bytes 1671176 | tf_op jit(solution)/shard_map/ppermute | solution.py:189
  206.7 17.0 %collective-permute-start.2 = (f32[2,2,16,2176]{3,2,1,0:T(8,128)}, f32[2,2,16,2176]{3,2,1,0:T(8,128)}, u32[]{:S(2)}, u32[]{:S(2)}) collective-permute-start(f32[2,2,16,2176]{3,2,1,0:T(8,128)} %get-tuple-element.47), channel_id=1, source_target_pairs={{0,1},{1,0},{2,3},{3,2},{4,5},{5,4},{6,7},{7,6},{8,9},{9,8},{10,11... | collective-permute-start | bytes 1671176 | tf_op jit(solution)/shard_map/ppermute | solution.py:189
  208.7 26.4 %collective-permute-start.3 = (f32[2,2,16,2176]{3,2,1,0:T(8,128)}, f32[2,2,16,2176]{3,2,1,0:T(8,128)}, u32[]{:S(2)}, u32[]{:S(2)}) collective-permute-start(f32[2,2,16,2176]{3,2,1,0:T(8,128)} %get-tuple-element.46), channel_id=1, source_target_pairs={{0,17},{1,16},{2,19},{3,18},{4,21},{5,20},{6,23},{7,22},{8,25},{9,... | collective-permute-start | bytes 1671176 | tf_op jit(solution)/shard_map/ppermute | solution.py:189
  217.0 18.0 %copy-start.4 = (f32[2,32,128,128]{2,3,1,0:T(8,128)S(1)}, f32[2,32,128,128]{2,3,1,0:T(8,128)}, u32[]{:S(2)}) copy-start(f32[2,32,128,128]{2,3,1,0:T(8,128)} %copy-done.3) | copy-start | bytes 12582916
  217.1 18.0 %copy-start.26 = (f32[2,128,32,16]{1,2,3,0:T(8,128)S(1)}, f32[2,128,32,16]{1,2,3,0:T(8,128)}, u32[]{:S(2)}) copy-start(f32[2,128,32,16]{1,2,3,0:T(8,128)} %copy-done.25) | copy-start | bytes 1572868
  250.3 19.7 %slice-start = ((s8[6291456]{0:T(1024)(128)(4,1)}), s8[2097152]{0:T(1024)(128)(4,1)S(1)}, s32[]{:S(2)}) async-start(s8[6291456]{0:T(1024)(128)(4,1)} %bitcast.328), calls=%async_computation.9 | async-start | bytes 4194304
  255.4 6.5 %collective-permute-start.4 = (f32[16,2176]{1,0:T(8,128)S(1)}, f32[16,2176]{1,0:T(8,128)S(1)}, u32[]{:S(2)}, u32[]{:S(2)}) collective-permute-start(f32[16,2176]{1,0:T(8,128)S(1)} %get-tuple-element.65), channel_id=1, source_target_pairs={{0,2},{1,3},{2,0},{3,1},{4,6},{5,7},{6,4},{7,5},{8,10},{9,11},{10,... | collective-permute-start | bytes 417800 | tf_op jit(solution)/shard_map/ppermute | solution.py:189
  257.1 12.8 %collective-permute-start.5 = (f32[16,2176]{1,0:T(8,128)S(1)}, f32[16,2176]{1,0:T(8,128)S(1)}, u32[]{:S(2)}, u32[]{:S(2)}) collective-permute-start(f32[16,2176]{1,0:T(8,128)S(1)} %get-tuple-element.64), channel_id=1, source_target_pairs={{0,4},{1,5},{2,6},{3,7},{4,0},{5,1},{6,2},{7,3},{8,12},{9,13},{10,... | collective-permute-start | bytes 417800 | tf_op jit(solution)/shard_map/ppermute | solution.py:189
  258.7 11.1 %collective-permute-start.6 = (f32[16,2176]{1,0:T(8,128)S(1)}, f32[16,2176]{1,0:T(8,128)S(1)}, u32[]{:S(2)}, u32[]{:S(2)}) collective-permute-start(f32[16,2176]{1,0:T(8,128)S(1)} %get-tuple-element.63), channel_id=1, source_target_pairs={{0,6},{1,7},{2,4},{3,5},{4,2},{5,3},{6,0},{7,1},{8,14},{9,15},{10,... | collective-permute-start | bytes 417800 | tf_op jit(solution)/shard_map/ppermute | solution.py:189
  260.3 9.7 %collective-permute-start.7 = (f32[2,2,2,2,16,1024]{5,4,3,2,1,0:T(8,128)S(1)}, f32[2,2,2,2,16,1024]{5,4,3,2,1,0:T(8,128)S(1)}, u32[]{:S(2)}, u32[]{:S(2)}) collective-permute-start(f32[2,2,2,2,16,1024]{5,4,3,2,1,0:T(8,128)S(1)} %dynamic-slice_bitcast_fusion.2), channel_id=1, source_target_pairs={{0,8},{1,9},{2,10},{3,11},{4,12},{5,13},{6,14},{7,15},{8,0},{9,1},... | collective-permute-start | bytes 3145736 | tf_op jit(solution)/shard_map/ppermute | solution.py:189
  276.7 25.6 %collective-permute-start.8 = (f32[2,2,2,2,16,1152]{5,4,3,2,1,0:T(8,128)}, f32[2,2,2,2,16,1152]{5,4,3,2,1,0:T(8,128)}, u32[]{:S(2)}, u32[]{:S(2)}) collective-permute-start(f32[2,2,2,2,16,1152]{5,4,3,2,1,0:T(8,128)} %dynamic-slice_bitcast_fusion.1), channel_id=1, source_target_pairs={{0,8},{1,9},{2,10},{3,11},{4,12},{5,13},{6,14},{7,15},{8,0},{9,1},... | collective-permute-start | bytes 3538952 | tf_op jit(solution)/shard_map/ppermute | solution.py:189
  277.8 11.5 %collective-permute-start.15 = (f32[2,2,16,1024]{3,2,1,0:T(8,128)}, f32[2,2,16,1024]{3,2,1,0:T(8,128)}, u32[]{:S(2)}, u32[]{:S(2)}) collective-permute-start(f32[2,2,16,1024]{3,2,1,0:T(8,128)} %get-tuple-element.60), channel_id=1, source_target_pairs={{0,16},{1,17},{2,18},{3,19},{4,20},{5,21},{6,22},{7,23},{8,24},{9,... | collective-permute-start | bytes 786440 | tf_op jit(solution)/shard_map/ppermute | solution.py:189
  278.9 10.5 %collective-permute-start.16 = (f32[2,2,16,1024]{3,2,1,0:T(8,128)}, f32[2,2,16,1024]{3,2,1,0:T(8,128)}, u32[]{:S(2)}, u32[]{:S(2)}) collective-permute-start(f32[2,2,16,1024]{3,2,1,0:T(8,128)} %get-tuple-element.62), channel_id=1, source_target_pairs={{0,1},{1,0},{2,3},{3,2},{4,5},{5,4},{6,7},{7,6},{8,9},{9,8},{10,11... | collective-permute-start | bytes 786440 | tf_op jit(solution)/shard_map/ppermute | solution.py:189
  278.9 16.9 %collective-permute-start.17 = (f32[2,2,16,1024]{3,2,1,0:T(8,128)}, f32[2,2,16,1024]{3,2,1,0:T(8,128)}, u32[]{:S(2)}, u32[]{:S(2)}) collective-permute-start(f32[2,2,16,1024]{3,2,1,0:T(8,128)} %get-tuple-element.61), channel_id=1, source_target_pairs={{0,17},{1,16},{2,19},{3,18},{4,21},{5,20},{6,23},{7,22},{8,25},{9,... | collective-permute-start | bytes 786440 | tf_op jit(solution)/shard_map/ppermute | solution.py:189
  285.0 39.6 %all-to-all-start.8 = ((f32[8,2,16,512]{3,2,1,0:T(8,128)}), f32[8,2,16,512]{3,2,1,0:T(8,128)S(1)}, u32[]{:S(2)}, u32[]{:S(2)}) async-start(f32[8,2,16,512]{3,2,1,0:T(8,128)} %bitcast.90), calls=%async_computation.8 | async-start | bytes 1048576 | tf_op jit(solution)/shard_map/all_to_all | solution.py:129
  297.1 9.5 %collective-permute-start.18 = (f32[16,1024]{1,0:T(8,128)S(1)}, f32[16,1024]{1,0:T(8,128)S(1)}, u32[]{:S(2)}, u32[]{:S(2)}) collective-permute-start(f32[16,1024]{1,0:T(8,128)S(1)} %get-tuple-element.69), channel_id=1, source_target_pairs={{0,2},{1,3},{2,0},{3,1},{4,6},{5,7},{6,4},{7,5},{8,10},{9,11},{10,... | collective-permute-start | bytes 196616 | tf_op jit(solution)/shard_map/ppermute | solution.py:189
  298.5 10.1 %collective-permute-start.19 = (f32[16,1024]{1,0:T(8,128)S(1)}, f32[16,1024]{1,0:T(8,128)S(1)}, u32[]{:S(2)}, u32[]{:S(2)}) collective-permute-start(f32[16,1024]{1,0:T(8,128)S(1)} %get-tuple-element.71), channel_id=1, source_target_pairs={{0,4},{1,5},{2,6},{3,7},{4,0},{5,1},{6,2},{7,3},{8,12},{9,13},{10,... | collective-permute-start | bytes 196616 | tf_op jit(solution)/shard_map/ppermute | solution.py:189
  300.9 7.7 %collective-permute-start.20 = (f32[16,1024]{1,0:T(8,128)S(1)}, f32[16,1024]{1,0:T(8,128)S(1)}, u32[]{:S(2)}, u32[]{:S(2)}) collective-permute-start(f32[16,1024]{1,0:T(8,128)S(1)} %get-tuple-element.70), channel_id=1, source_target_pairs={{0,6},{1,7},{2,4},{3,5},{4,2},{5,3},{6,0},{7,1},{8,14},{9,15},{10,... | collective-permute-start | bytes 196616 | tf_op jit(solution)/shard_map/ppermute | solution.py:189
  303.8 9.9 %collective-permute-start.10 = (f32[2,2,16,1152]{3,2,1,0:T(8,128)S(1)}, f32[2,2,16,1152]{3,2,1,0:T(8,128)S(1)}, u32[]{:S(2)}, u32[]{:S(2)}) collective-permute-start(f32[2,2,16,1152]{3,2,1,0:T(8,128)S(1)} %get-tuple-element.59), channel_id=1, source_target_pairs={{0,1},{1,0},{2,3},{3,2},{4,5},{5,4},{6,7},{7,6},{8,9},{9,8},{10,11... | collective-permute-start | bytes 884744 | tf_op jit(solution)/shard_map/ppermute | solution.py:189
  305.9 12.0 %collective-permute-start.11 = (f32[2,2,16,1152]{3,2,1,0:T(8,128)S(1)}, f32[2,2,16,1152]{3,2,1,0:T(8,128)S(1)}, u32[]{:S(2)}, u32[]{:S(2)}) collective-permute-start(f32[2,2,16,1152]{3,2,1,0:T(8,128)S(1)} %get-tuple-element.58), channel_id=1, source_target_pairs={{0,17},{1,16},{2,19},{3,18},{4,21},{5,20},{6,23},{7,22},{8,25},{9,... | collective-permute-start | bytes 884744 | tf_op jit(solution)/shard_map/ppermute | solution.py:189
  306.6 12.8 %collective-permute-start.9 = (f32[2,2,16,1152]{3,2,1,0:T(8,128)S(1)}, f32[2,2,16,1152]{3,2,1,0:T(8,128)S(1)}, u32[]{:S(2)}, u32[]{:S(2)}) collective-permute-start(f32[2,2,16,1152]{3,2,1,0:T(8,128)S(1)} %get-tuple-element.57), channel_id=1, source_target_pairs={{0,16},{1,17},{2,18},{3,19},{4,20},{5,21},{6,22},{7,23},{8,24},{9,... | collective-permute-start | bytes 884744 | tf_op jit(solution)/shard_map/ppermute | solution.py:189
  319.4 6.5 %collective-permute-start.12 = (f32[16,1152]{1,0:T(8,128)S(1)}, f32[16,1152]{1,0:T(8,128)S(1)}, u32[]{:S(2)}, u32[]{:S(2)}) collective-permute-start(f32[16,1152]{1,0:T(8,128)S(1)} %get-tuple-element.66), channel_id=1, source_target_pairs={{0,2},{1,3},{2,0},{3,1},{4,6},{5,7},{6,4},{7,5},{8,10},{9,11},{10,... | collective-permute-start | bytes 221192 | tf_op jit(solution)/shard_map/ppermute | solution.py:189
  320.1 5.9 %collective-permute-start.13 = (f32[16,1152]{1,0:T(8,128)S(1)}, f32[16,1152]{1,0:T(8,128)S(1)}, u32[]{:S(2)}, u32[]{:S(2)}) collective-permute-start(f32[16,1152]{1,0:T(8,128)S(1)} %get-tuple-element.68), channel_id=1, source_target_pairs={{0,4},{1,5},{2,6},{3,7},{4,0},{5,1},{6,2},{7,3},{8,12},{9,13},{10,... | collective-permute-start | bytes 221192 | tf_op jit(solution)/shard_map/ppermute | solution.py:189
  322.5 6.2 %collective-permute-start.14 = (f32[16,1152]{1,0:T(8,128)S(1)}, f32[16,1152]{1,0:T(8,128)S(1)}, u32[]{:S(2)}, u32[]{:S(2)}) collective-permute-start(f32[16,1152]{1,0:T(8,128)S(1)} %get-tuple-element.67), channel_id=1, source_target_pairs={{0,6},{1,7},{2,4},{3,5},{4,2},{5,3},{6,0},{7,1},{8,14},{9,15},{10,... | collective-permute-start | bytes 221192 | tf_op jit(solution)/shard_map/ppermute | solution.py:189
  (27 other events, 181.5 us)

commit v4 on v3

--- a/solution.py
+++ b/solution.py
@@ -222,8 +222,7 @@
     curve_first, z_source, z_occur = to_zorder(points, z_route)
     grad_curve, unused_source, unused_occur = to_hilbert(upstream, h_route)
     mixed_first, saved_first = block_forward(curve_first, gains[0], w_qkv[0], w_proj[0])
-    mixed_out, grad_curve = lax.optimization_barrier((mixed_first, grad_curve))
-    first_out = curve_first + jnp.dot(mixed_out, w_proj[0], precision=fast_mode)
+    first_out = curve_first + jnp.dot(mixed_first, w_proj[0], precision=fast_mode)
     middle = from_zorder(first_out, z_source, z_occur, z_route)
     curve_second, h_source, h_occur = to_hilbert(middle, h_route)
     unused_mixed, saved_second = block_forward(curve_second, gains[1], w_qkv[1], w_proj[1])
@@ -242,15 +241,15 @@
     middle_curve, unused_again, unused_spots = to_zorder(grad_middle, z_route)
     grad_mixed, proj_first = mixed_grads(middle_curve, saved_first, w_proj[0])
     grad_heads, grad_value = value_grads(grad_mixed, saved_first)
-    grad_heads = second_sum.meet(grad_heads)
     value_first = weight_grad(saved_first, grad_value)
     early_sum = ScatterSum(jnp.concatenate([value_first, proj_first], axis=1), groups)
     grad_query, grad_key = score_grads(grad_heads, saved_first)
     grad_pair = jnp.concatenate([grad_query, grad_key], axis=1)
     grad_pair = second_sum.meet(grad_pair)
     grad_pair = early_sum.meet(grad_pair)
+    grad_normed = normed_grad(jnp.concatenate([grad_pair, grad_value], axis=1), w_qkv[0])
+    grad_normed = second_sum.meet(grad_normed)
     second = second_sum.finish()
-    grad_normed = normed_grad(jnp.concatenate([grad_pair, grad_value], axis=1), w_qkv[0])
     around, gain_first = saved_first[6](grad_normed)
     late_sum = ScatterSum(with_gain([weight_grad(saved_first, grad_pair)], gain_first), groups)
     point_grad = from_zorder(middle_curve + around, z_source, z_occur, z_route)

time: 336 us -> 310 us (0.923)
  blocking collectives: 18.1 us -> 0 us
  waiting for transfers between devices: 71.6 us -> 55.6 us
  local copies, waits for them, and re-layouts: 72.3 us -> 76.4 us
  starting transfers between devices: 59.7 us -> 63.6 us
    ppermute x21, waiting for transfers between devices: 42.2 us -> 20.4 us  [send_next(): self.received.append(lax.ppermute(sent, mesh_axes, swaps))]
    all_to_all x1 -> x0, blocking collectives: 18.1 us -> none  [from_zorder(): lax.all_to_all(buffer, 'gy', split_axis=0, concat_axis=0, tiled=True)]
    all_to_all x1 -> x2, waiting for transfers between devices: 0.01 us -> 10.7 us  [from_zorder(): lax.all_to_all(buffer, 'gy', split_axis=0, concat_axis=0, tiled=True)]
    all_to_all x2, waiting for transfers between devices: 16.1 us -> 10.3 us  [to_zorder(): lax.all_to_all(buffer, 'gy', split_axis=0, concat_axis=0, tiled=True)]
    all_to_all x1 -> x2, starting transfers between devices: 4.38 us -> 8.2 us  [from_zorder(): lax.all_to_all(buffer, 'gy', split_axis=0, concat_axis=0, tiled=True)]
    unnamed x68 -> x67, local copies, waits for them, and re-layouts: 10.4 us -> 8.19 us
  transfers between devices with their start and end apart: 29 -> 30, of which waited for: 16 -> 14; matrix products, arithmetic and copies ran while one was open for 17% -> 31% of each run, Pallas kernels for 0% -> 0%
where the time goes in v4:
time: 310 us; the launch traced here: 305 us
  matrix products  80.7 us (26%)
  local copies, waits for them, and re-layouts  76.4 us (25%)
  starting transfers between devices  63.6 us (21%)
  waiting for transfers between devices  55.6 us (18%)
  other arithmetic  26.6 us (9%)
    ppermute x21, starting transfers between devices, send_next(): self.received.append(lax.ppermute(sent, mesh_axes, swaps))  25 us
    ppermute x21, waiting for transfers between devices, send_next(): self.received.append(lax.ppermute(sent, mesh_axes, swaps))  20.4 us
    dot_general x2, matrix products, block_forward(): jnp.einsum('pihd,pjhd->phij', queries, key_rows, precision=exact_mode)  13.6 us
    scatter x4, local copies, waits for them, and re-layouts, spread_out(): buffer = jnp.zeros((peer_count, per_peer) + segments.shape[1:], rows_in.d...  11.7 us
    all_to_all x2, waiting for transfers between devices, from_zorder(): lax.all_to_all(buffer, 'gy', split_axis=0, concat_axis=0, tiled=True)  10.7 us
    all_to_all x2, waiting for transfers between devices, to_zorder(): lax.all_to_all(buffer, 'gy', split_axis=0, concat_axis=0, tiled=True)  10.3 us
    all_to_all x2, starting transfers between devices, to_hilbert(): lax.all_to_all(buffer, 'gx', split_axis=0, concat_axis=0, tiled=True)  8.71 us
    dot_general x2, matrix products, value_grads(): jnp.einsum('phij,pihd->pjhd', attention, grad_heads, precision=fast_mode)  8.69 us
  transfers between devices with their start and end apart: 30, of which 14 were waited for; matrix products, arithmetic and copies ran while one was open for 31% of the time, Pallas kernels for 0%

profile of v4, /device:TPU:0, one launch (start us, length us, event | category | flops | bytes accessed | tf_op | source)
XLA Modules:
  0.0 304.9 jit_solution(6355170555999196656)
XLA Ops:
  5.8 4.3 %all-to-all-start.1 = ((s32[4,1,4]{2,1,0:T(1,128)}), s32[4,1,4]{2,1,0:T(1,128)S(1)}, u32[]{:S(2)}, u32[]{:S(2)}) async-start(s32[4,1,4]{2,1,0:T(1,128)} %bitcast.14), calls=%async_computation.1 | async-start | bytes 4096 | tf_op jit(solution)/shard_map/all_to_all | solution.py:139
  13.8 6.2 %all-to-all-start = ((s32[8,1,2]{2,1,0:T(1,128)}), s32[8,1,2]{2,1,0:T(1,128)S(1)}, u32[]{:S(2)}, u32[]{:S(2)}) async-start(s32[8,1,2]{2,1,0:T(1,128)} %copy.124), calls=%async_computation | async-start | bytes 8192 | tf_op jit(solution)/shard_map/all_to_all | solution.py:120
  26.4 4.1 %all-to-all-start.3 = ((f32[8,2,16,512]{3,2,1,0:T(8,128)}), f32[8,2,16,512]{3,2,1,0:T(8,128)}, u32[]{:S(2)}, u32[]{:S(2)}) async-start(f32[8,2,16,512]{3,2,1,0:T(8,128)} %scatter_fusion.3), calls=%async_computation.3 | async-start | bytes 1048576 | tf_op jit(solution)/shard_map/all_to_all | solution.py:119
  30.6 6.0 %fusion.105 = (f32[1,512,1536]{2,1,0:T(8,128)}, f32[1,512,1536]{2,1,0:T(8,128)}) fusion(f32[2,512,1536]{2,1,0:T(8,128)} %param.10), kind=kLoop, calls=%fused_computation.239 | loop fusion | bytes 12582912 | tf_op jit(solution)/shard_map/slice | solution.py:228
  41.3 3.3 %all-to-all-done.3 = f32[8,2,16,512]{3,2,1,0:T(8,128)} async-done(((f32[8,2,16,512]{3,2,1,0:T(8,128)}), f32[8,2,16,512]{3,2,1,0:T(8,128)}, u32[]{:S(2)}, u32[]{:S(2)}) %all-to-all-start.3) | async-done | bytes 524320 | tf_op jit(solution)/shard_map/all_to_all | solution.py:119
  50.6 4.2 %fusion.10 = f32[2,128,3,32,16]{1,3,4,2,0:T(8,128)S(1)} fusion(f32[2,128,512,1,1]{2,1,4,3,0:T(8,128)S(1)} %bitcast.344, f32[3,32,16,512]{3,2,1,0:T(8,128)S(1)} %bitcast.328), kind=kOutput, calls=%fused_computation.35 | convolution fusion | flops 2415919104 | bytes 5242880 | tf_op jit(solution)/shard_map/dot_general | solution.py:30
  55.9 6.7 %multiply_reduce_fusion.3 = (f32[2,32,128]{2,1,0:T(8,128)S(1)}, f32[2,32,128,128]{2,3,1,0:T(8,128)S(1)}) fusion(f32[2,128,32,16]{1,2,3,0:T(8,128)S(1)} %get-tuple-element.51, f32[2,128,32,16]{1,2,3,0:T(8,128)S(1)} %get-tuple-element.50), kind=kOutput, calls=%fused_computation.24 | convolution fusion | flops 203415552 | bytes 5275648 | tf_op jit(solution)/shard_map/pihd,pjhd->phij/dot_general | solution.py:33
  70.9 3.6 %all-to-all-start.4 = ((f32[8,2,16,512]{3,2,1,0:T(8,128)}), f32[8,2,16,512]{3,2,1,0:T(8,128)S(1)}, u32[]{:S(2)}, u32[]{:S(2)}) async-start(f32[8,2,16,512]{3,2,1,0:T(8,128)} %bitcast.37), calls=%async_computation.4 | async-start | bytes 1048576 | tf_op jit(solution)/shard_map/all_to_all | solution.py:129
  78.2 10.7 %all-to-all-done.4 = f32[8,2,16,512]{3,2,1,0:T(8,128)S(1)} async-done(((f32[8,2,16,512]{3,2,1,0:T(8,128)}), f32[8,2,16,512]{3,2,1,0:T(8,128)S(1)}, u32[]{:S(2)}, u32[]{:S(2)}) %all-to-all-start.4) | async-done | bytes 524320 | tf_op jit(solution)/shard_map/all_to_all | solution.py:129
  88.8 4.2 %all-to-all-start.2 = ((f32[4,4,16,512]{3,2,1,0:T(8,128)}), f32[4,4,16,512]{3,2,1,0:T(8,128)}, u32[]{:S(2)}, u32[]{:S(2)}) async-start(f32[4,4,16,512]{3,2,1,0:T(8,128)} %scatter_fusion.2), calls=%async_computation.2 | async-start | bytes 1048576 | tf_op jit(solution)/shard_map/all_to_all | solution.py:138
  104.9 4.5 %all-to-all-start.5 = ((f32[4,4,16,512]{3,2,1,0:T(8,128)}), f32[4,4,16,512]{3,2,1,0:T(8,128)}, u32[]{:S(2)}, u32[]{:S(2)}) async-start(f32[4,4,16,512]{3,2,1,0:T(8,128)} %scatter_fusion.5), calls=%async_computation.5 | async-start | bytes 1048576 | tf_op jit(solution)/shard_map/all_to_all | solution.py:138
  114.7 3.2 %all-to-all-done.5 = f32[4,4,16,512]{3,2,1,0:T(8,128)} async-done(((f32[4,4,16,512]{3,2,1,0:T(8,128)}), f32[4,4,16,512]{3,2,1,0:T(8,128)}, u32[]{:S(2)}, u32[]{:S(2)}) %all-to-all-start.5) | async-done | bytes 524320 | tf_op jit(solution)/shard_map/all_to_all | solution.py:138
  123.9 4.2 %fusion.8 = f32[2,128,3,32,16]{1,3,4,2,0:T(8,128)S(1)} fusion(f32[2,128,512,1,1]{2,1,4,3,0:T(8,128)S(1)} %bitcast.351, f32[3,32,16,512]{3,2,1,0:T(8,128)S(1)} %bitcast.327), kind=kOutput, calls=%fused_computation.33 | convolution fusion | flops 2415919104 | bytes 5242880 | tf_op jit(solution)/shard_map/dot_general | solution.py:30
  128.3 6.9 %multiply_reduce_fusion.2 = (f32[2,32,128]{2,1,0:T(8,128)S(1)}, f32[2,32,128,128]{2,3,1,0:T(8,128)S(1)}) fusion(f32[2,128,32,16]{1,2,3,0:T(8,128)S(1)} %get-tuple-element.49, f32[2,128,32,16]{1,2,3,0:T(8,128)S(1)} %get-tuple-element.47), kind=kOutput, calls=%fused_computation.23 | convolution fusion | flops 203415552 | bytes 5275648 | tf_op jit(solution)/shard_map/pihd,pjhd->phij/dot_general | solution.py:33
  136.3 3.4 %convolution_bitcast_fusion.2 = f32[2,128,32,16]{1,3,2,0:T(8,128)S(1)} fusion(f32[2,128,32,16]{1,3,2,0:T(8,128)S(1)} %copy-done.20, f32[2,32,128,128]{2,3,1,0:T(8,128)S(1)} %get-tuple-element.87, f32[2,32,128]{2,1,0:T(8,128)S(1)} %fusion.3, f32[2,32,128]{2,1,0:T(8,128)S(1)} %get-tuple-element.86), kind=kOutput, calls=%fused_computation.57 | convolution fusion | flops 103809024 | bytes 5308416 | tf_op jit(solution)/shard_map/phij,pihd->pjhd/dot_general | solution.py:53
  139.6 3.8 %multiply_reduce_fusion.1 = (f32[2,32,128]{2,1,0:T(8,128)S(1)}, f32[2,32,128,128]{2,3,1,0:T(8,128)S(1)}) fusion(f32[2,32,128]{2,1,0:T(8,128)S(1)} %fusion.3, f32[2,32,128]{2,1,0:T(8,128)S(1)} %get-tuple-element.86, f32[2,32,128,128]{2,3,1,0:T(8,128)S(1)} %get-tuple-element.87, f32[2,128,32,16]{1,3,2,0:T(8,128)S(1)} %copy-done.20, ...), kind=kOutput, calls=%fused_computation.20 | convolution fusion | flops 105897984 | bytes 9535488 | tf_op jit(solution)/shard_map/pihd,pjhd->phij/dot_general | solution.py:59
  143.4 3.8 %fusion.24 = f32[2,128,32,16]{1,3,2,0:T(8,128)S(1)} fusion(f32[2,32,128,128]{2,3,1,0:T(8,128)S(1)} %get-tuple-element.89, f32[2,32,128]{2,1,0:T(8,128)S(1)} %get-tuple-element.88, f32[2,128,32,16]{1,2,3,0:T(8,128)S(1)} %get-tuple-element.47, f32[2,32,128,128]{2,3,1,0:T(8,128)S(1)} %get-tuple-element.87, f32[2,32,128]{2,1,0:T(8,128)S(1)} %fusion.3, ...), kind=kOutput, calls=%fused_computation.54 | convolution fusion | flops 106954752 | bytes 9535488 | tf_op jit(solution)/shard_map/phij,pihd->pjhd/dot_general | solution.py:63
  147.2 3.2 %fusion.23 = f32[2,128,32,16]{1,3,2,0:T(8,128)S(1)} fusion(f32[2,32,128,128]{2,3,1,0:T(8,128)S(1)} %get-tuple-element.89, f32[2,32,128]{2,1,0:T(8,128)S(1)} %get-tuple-element.88, f32[2,128,32,16]{1,2,3,0:T(8,128)S(1)} %get-tuple-element.49, f32[2,32,128,128]{2,3,1,0:T(8,128)S(1)} %get-tuple-element.87, f32[2,32,128]{2,1,0:T(8,128)S(1)} %fusion.3, ...), kind=kOutput, calls=%fused_computation.53 | convolution fusion | flops 106954752 | bytes 9535488 | tf_op jit(solution)/shard_map/phij,pjhd->pihd/dot_general | solution.py:62
  150.5 5.4 %convolution_bitcast_fusion.1 = f32[2,128,32,16]{1,3,2,0:T(8,128)} fusion(f32[2,128,32,16]{1,2,3,0:T(8,128)S(1)} %get-tuple-element.48, f32[2,32,128,128]{2,3,1,0:T(8,128)} %copy-done.5, f32[2,32,128]{2,1,0:T(8,128)S(1)} %fusion.3, f32[2,32,128]{2,1,0:T(8,128)S(1)} %get-tuple-element.86), kind=kOutput, calls=%fused_computation.56 | convolution fusion | flops 103809024 | bytes 5308416 | tf_op jit(solution)/shard_map/phij,pjhd->pihd/dot_general | solution.py:37
  158.8 4.6 %multiply_reduce_fusion.7 = (f32[256]{0:T(256)S(1)}, f32[256,512]{1,0:T(8,128)S(1)}, f32[256,512]{1,0:T(8,128)S(1)}) fusion(f32[512]{0:T(512)S(1)} %bitcast.376, f32[256]{0:T(256)S(1)} %div.96, f32[16,16,512]{2,1,0:T(8,128)S(1)} %copy-done.6, f32[256,1536]{0,1:T(8,128)S(1)} %bitcast_dynamic-update-slice_fusion, f32[2,512,1536]{2,1,0:T(8,128)} %param.10), kind=kOutput, calls=%fused_computation.102 | convolution fusion | flops 1208483584 | bytes 6295552 | tf_op jit(solution)/shard_map/dot_general | solution.py:72
  173.7 3.5 %all-to-all-start.6 = ((f32[4,4,16,512]{3,2,1,0:T(8,128)}), f32[4,4,16,512]{3,2,1,0:T(8,128)S(1)}, u32[]{:S(2)}, u32[]{:S(2)}) async-start(f32[4,4,16,512]{3,2,1,0:T(8,128)} %bitcast.61), calls=%async_computation.6 | async-start | bytes 1048576 | tf_op jit(solution)/shard_map/all_to_all | solution.py:148
  177.4 8.6 %all-to-all-done.6 = f32[4,4,16,512]{3,2,1,0:T(8,128)S(1)} async-done(((f32[4,4,16,512]{3,2,1,0:T(8,128)}), f32[4,4,16,512]{3,2,1,0:T(8,128)S(1)}, u32[]{:S(2)}, u32[]{:S(2)}) %all-to-all-start.6) | async-done | bytes 524320 | tf_op jit(solution)/shard_map/all_to_all | solution.py:148
  190.2 3.6 %all-to-all-start.7 = ((f32[8,2,16,512]{3,2,1,0:T(8,128)}), f32[8,2,16,512]{3,2,1,0:T(8,128)S(1)}, u32[]{:S(2)}, u32[]{:S(2)}) async-start(f32[8,2,16,512]{3,2,1,0:T(8,128)} %scatter_fusion.7), calls=%async_computation.7 | async-start | bytes 1048576 | tf_op jit(solution)/shard_map/all_to_all | solution.py:119
  201.1 7.0 %all-to-all-done.7 = f32[8,2,16,512]{3,2,1,0:T(8,128)S(1)} async-done(((f32[8,2,16,512]{3,2,1,0:T(8,128)}), f32[8,2,16,512]{3,2,1,0:T(8,128)S(1)}, u32[]{:S(2)}, u32[]{:S(2)}) %all-to-all-start.7) | async-done | bytes 524320 | tf_op jit(solution)/shard_map/all_to_all | solution.py:119
  210.5 5.3 %convolution_bitcast_fusion = f32[2,128,32,16]{1,3,2,0:T(8,128)S(1)} fusion(f32[2,128,32,16]{1,3,2,0:T(8,128)S(1)} %fusion.109, f32[2,32,128,128]{2,3,1,0:T(8,128)} %copy-done.3, f32[2,32,128]{2,1,0:T(8,128)S(1)} %fusion.1, f32[2,32,128]{2,1,0:T(8,128)S(1)} %get-tuple-element.84), kind=kOutput, calls=%fused_computation.55 | convolution fusion | flops 103809024 | bytes 5308416 | tf_op jit(solution)/shard_map/phij,pihd->pjhd/dot_general | solution.py:53
  215.9 3.7 %multiply_reduce_fusion = (f32[2,32,128]{2,1,0:T(8,128)S(1)}, f32[2,32,128,128]{2,3,1,0:T(8,128)S(1)}) fusion(f32[2,32,128]{2,1,0:T(8,128)S(1)} %fusion.1, f32[2,32,128]{2,1,0:T(8,128)S(1)} %get-tuple-element.84, f32[2,32,128,128]{2,3,1,0:T(8,128)S(1)} %copy-done.4, f32[2,128,32,16]{1,3,2,0:T(8,128)S(1)} %fusion.109, f32[2,128,32,16]{1,2,3,0:T(8,128)S(1)} %copy-done.24), kind=kOutput, calls=%fused_computation.18 | convolution fusion | flops 105897984 | bytes 9535488 | tf_op jit(solution)/shard_map/pihd,pjhd->phij/dot_general | solution.py:59
  219.6 3.5 %fusion.21 = f32[2,128,32,16]{1,3,2,0:T(8,128)} fusion(f32[2,32,128,128]{2,3,1,0:T(8,128)S(1)} %get-tuple-element.92, f32[2,32,128]{2,1,0:T(8,128)S(1)} %get-tuple-element.91, f32[2,128,32,16]{1,2,3,0:T(8,128)S(1)} %copy-done.18, f32[2,32,128,128]{2,3,1,0:T(8,128)S(1)} %copy-done.4, f32[2,32,128]{2,1,0:T(8,128)S(1)} %fusion.1, ...), kind=kOutput, calls=%fused_computation.51 | convolution fusion | flops 106954752 | bytes 9535488 | tf_op jit(solution)/shard_map/phij,pjhd->pihd/dot_general | solution.py:62
  223.2 4.6 %fusion.22 = f32[2,128,32,16]{1,3,2,0:T(8,128)} fusion(f32[2,32,128,128]{2,3,1,0:T(8,128)S(1)} %get-tuple-element.92, f32[2,32,128]{2,1,0:T(8,128)S(1)} %get-tuple-element.91, f32[2,128,32,16]{1,2,3,0:T(8,128)S(1)} %copy-done.16, f32[2,32,128,128]{2,3,1,0:T(8,128)S(1)} %copy-done.4, f32[2,32,128]{2,1,0:T(8,128)S(1)} %fusion.1, ...), kind=kOutput, calls=%fused_computation.52 | convolution fusion | flops 106954752 | bytes 9535488 | tf_op jit(solution)/shard_map/phij,pihd->pjhd/dot_general | solution.py:63
  231.0 3.1 %copy.165 = f32[512,1024]{1,0:T(8,128)} copy(f32[512,1024]{0,1:T(8,128)} %pad_maximum_fusion.2) | data formatting | bytes 4194304 | tf_op jit(solution)/shard_map/concatenate | solution.py:245
  262.4 4.6 %all-to-all-start.8 = ((f32[8,2,16,512]{3,2,1,0:T(8,128)}), f32[8,2,16,512]{3,2,1,0:T(8,128)S(1)}, u32[]{:S(2)}, u32[]{:S(2)}) async-start(f32[8,2,16,512]{3,2,1,0:T(8,128)} %bitcast.90), calls=%async_computation.8 | async-start | bytes 1048576 | tf_op jit(solution)/shard_map/all_to_all | solution.py:129
  278.8 8.1 %collective-permute-done.19 = f32[16,1024]{1,0:T(8,128)S(1)} collective-permute-done((f32[16,1024]{1,0:T(8,128)S(1)}, f32[16,1024]{1,0:T(8,128)S(1)}, u32[]{:S(2)}, u32[]{:S(2)}) %collective-permute-start.19) | collective-permute-done | bytes 65568 | tf_op jit(solution)/shard_map/ppermute | solution.py:189
  287.0 3.9 %collective-permute-done.11 = f32[2,2,16,1152]{3,2,1,0:T(8,128)S(1)} collective-permute-done((f32[2,2,16,1152]{3,2,1,0:T(8,128)S(1)}, f32[2,2,16,1152]{3,2,1,0:T(8,128)S(1)}, u32[]{:S(2)}, u32[]{:S(2)}) %collective-permute-start.11) | collective-permute-done | bytes 294944 | tf_op jit(solution)/shard_map/ppermute | solution.py:189
  (238 shorter events, 147.1 us)
Async XLA Ops:
  5.8 8.0 %all-to-all-start.1 = ((s32[4,1,4]{2,1,0:T(1,128)}), s32[4,1,4]{2,1,0:T(1,128)S(1)}, u32[]{:S(2)}, u32[]{:S(2)}) async-start(s32[4,1,4]{2,1,0:T(1,128)} %bitcast.14), calls=%async_computation.1 | async-start | bytes 4096 | tf_op jit(solution)/shard_map/all_to_all | solution.py:139
  13.8 12.6 %all-to-all-start = ((s32[8,1,2]{2,1,0:T(1,128)}), s32[8,1,2]{2,1,0:T(1,128)S(1)}, u32[]{:S(2)}, u32[]{:S(2)}) async-start(s32[8,1,2]{2,1,0:T(1,128)} %copy.124), calls=%async_computation | async-start | bytes 8192 | tf_op jit(solution)/shard_map/all_to_all | solution.py:120
  26.4 18.2 %all-to-all-start.3 = ((f32[8,2,16,512]{3,2,1,0:T(8,128)}), f32[8,2,16,512]{3,2,1,0:T(8,128)}, u32[]{:S(2)}, u32[]{:S(2)}) async-start(f32[8,2,16,512]{3,2,1,0:T(8,128)} %scatter_fusion.3), calls=%async_computation.3 | async-start | bytes 1048576 | tf_op jit(solution)/shard_map/all_to_all | solution.py:119
  41.3 27.0 %copy-start.26 = (s32[16]{0:T(128)}, s32[16]{0:T(128)S(1)}, u32[]{:S(2)}) copy-start(s32[16]{0:T(128)S(1)} %fusion.78) | copy-start | bytes 196
  70.9 18.0 %all-to-all-start.4 = ((f32[8,2,16,512]{3,2,1,0:T(8,128)}), f32[8,2,16,512]{3,2,1,0:T(8,128)S(1)}, u32[]{:S(2)}, u32[]{:S(2)}) async-start(f32[8,2,16,512]{3,2,1,0:T(8,128)} %bitcast.37), calls=%async_computation.4 | async-start | bytes 1048576 | tf_op jit(solution)/shard_map/all_to_all | solution.py:129
  88.8 16.1 %all-to-all-start.2 = ((f32[4,4,16,512]{3,2,1,0:T(8,128)}), f32[4,4,16,512]{3,2,1,0:T(8,128)}, u32[]{:S(2)}, u32[]{:S(2)}) async-start(f32[4,4,16,512]{3,2,1,0:T(8,128)} %scatter_fusion.2), calls=%async_computation.2 | async-start | bytes 1048576 | tf_op jit(solution)/shard_map/all_to_all | solution.py:138
  104.9 13.0 %all-to-all-start.5 = ((f32[4,4,16,512]{3,2,1,0:T(8,128)}), f32[4,4,16,512]{3,2,1,0:T(8,128)}, u32[]{:S(2)}, u32[]{:S(2)}) async-start(f32[4,4,16,512]{3,2,1,0:T(8,128)} %scatter_fusion.5), calls=%async_computation.5 | async-start | bytes 1048576 | tf_op jit(solution)/shard_map/all_to_all | solution.py:138
  170.0 16.6 %collective-permute-start = (f32[2,2,2,2,16,2176]{5,4,3,2,1,0:T(8,128)S(1)}, f32[2,2,2,2,16,2176]{5,4,3,2,1,0:T(8,128)}, u32[]{:S(2)}, u32[]{:S(2)}) collective-permute-start(f32[2,2,2,2,16,2176]{5,4,3,2,1,0:T(8,128)S(1)} %dynamic-slice_bitcast_fusion), channel_id=1, source_target_pairs={{0,8},{1,9},{2,10},{3,11},{4,12},{5,13},{6,14},{7,15},{8,0},{9,1},... | collective-permute-start | bytes 6684680 | tf_op jit(solution)/shard_map/ppermute | solution.py:189
  173.7 12.3 %all-to-all-start.6 = ((f32[4,4,16,512]{3,2,1,0:T(8,128)}), f32[4,4,16,512]{3,2,1,0:T(8,128)S(1)}, u32[]{:S(2)}, u32[]{:S(2)}) async-start(f32[4,4,16,512]{3,2,1,0:T(8,128)} %bitcast.61), calls=%async_computation.6 | async-start | bytes 1048576 | tf_op jit(solution)/shard_map/all_to_all | solution.py:148
  190.2 17.9 %all-to-all-start.7 = ((f32[8,2,16,512]{3,2,1,0:T(8,128)}), f32[8,2,16,512]{3,2,1,0:T(8,128)S(1)}, u32[]{:S(2)}, u32[]{:S(2)}) async-start(f32[8,2,16,512]{3,2,1,0:T(8,128)} %scatter_fusion.7), calls=%async_computation.7 | async-start | bytes 1048576 | tf_op jit(solution)/shard_map/all_to_all | solution.py:119
  197.6 40.1 %collective-permute-start.1 = (f32[2,2,16,2176]{3,2,1,0:T(8,128)}, f32[2,2,16,2176]{3,2,1,0:T(8,128)}, u32[]{:S(2)}, u32[]{:S(2)}) collective-permute-start(f32[2,2,16,2176]{3,2,1,0:T(8,128)} %get-tuple-element.44), channel_id=1, source_target_pairs={{0,16},{1,17},{2,18},{3,19},{4,20},{5,21},{6,22},{7,23},{8,24},{9,... | collective-permute-start | bytes 1671176 | tf_op jit(solution)/shard_map/ppermute | solution.py:189
  198.0 39.7 %collective-permute-start.2 = (f32[2,2,16,2176]{3,2,1,0:T(8,128)}, f32[2,2,16,2176]{3,2,1,0:T(8,128)}, u32[]{:S(2)}, u32[]{:S(2)}) collective-permute-start(f32[2,2,16,2176]{3,2,1,0:T(8,128)} %get-tuple-element.43), channel_id=1, source_target_pairs={{0,1},{1,0},{2,3},{3,2},{4,5},{5,4},{6,7},{7,6},{8,9},{9,8},{10,11... | collective-permute-start | bytes 1671176 | tf_op jit(solution)/shard_map/ppermute | solution.py:189
  200.0 37.7 %collective-permute-start.3 = (f32[2,2,16,2176]{3,2,1,0:T(8,128)}, f32[2,2,16,2176]{3,2,1,0:T(8,128)}, u32[]{:S(2)}, u32[]{:S(2)}) collective-permute-start(f32[2,2,16,2176]{3,2,1,0:T(8,128)} %get-tuple-element.42), channel_id=1, source_target_pairs={{0,17},{1,16},{2,19},{3,18},{4,21},{5,20},{6,23},{7,22},{8,25},{9,... | collective-permute-start | bytes 1671176 | tf_op jit(solution)/shard_map/ppermute | solution.py:189
  235.5 8.4 %collective-permute-start.4 = (f32[2,2,2,2,16,1024]{5,4,3,2,1,0:T(8,128)S(1)}, f32[2,2,2,2,16,1024]{5,4,3,2,1,0:T(8,128)S(1)}, u32[]{:S(2)}, u32[]{:S(2)}) collective-permute-start(f32[2,2,2,2,16,1024]{5,4,3,2,1,0:T(8,128)S(1)} %dynamic-slice_bitcast_fusion.2), channel_id=1, source_target_pairs={{0,8},{1,9},{2,10},{3,11},{4,12},{5,13},{6,14},{7,15},{8,0},{9,1},... | collective-permute-start | bytes 3145736 | tf_op jit(solution)/shard_map/ppermute | solution.py:189
  239.5 10.7 %collective-permute-start.5 = (f32[16,2176]{1,0:T(8,128)S(1)}, f32[16,2176]{1,0:T(8,128)S(1)}, u32[]{:S(2)}, u32[]{:S(2)}) collective-permute-start(f32[16,2176]{1,0:T(8,128)S(1)} %get-tuple-element.61), channel_id=1, source_target_pairs={{0,2},{1,3},{2,0},{3,1},{4,6},{5,7},{6,4},{7,5},{8,10},{9,11},{10,... | collective-permute-start | bytes 417800 | tf_op jit(solution)/shard_map/ppermute | solution.py:189
  240.4 13.4 %collective-permute-start.6 = (f32[16,2176]{1,0:T(8,128)S(1)}, f32[16,2176]{1,0:T(8,128)S(1)}, u32[]{:S(2)}, u32[]{:S(2)}) collective-permute-start(f32[16,2176]{1,0:T(8,128)S(1)} %get-tuple-element.60), channel_id=1, source_target_pairs={{0,4},{1,5},{2,6},{3,7},{4,0},{5,1},{6,2},{7,3},{8,12},{9,13},{10,... | collective-permute-start | bytes 417800 | tf_op jit(solution)/shard_map/ppermute | solution.py:189
  241.3 12.5 %collective-permute-start.7 = (f32[16,2176]{1,0:T(8,128)S(1)}, f32[16,2176]{1,0:T(8,128)S(1)}, u32[]{:S(2)}, u32[]{:S(2)}) collective-permute-start(f32[16,2176]{1,0:T(8,128)S(1)} %get-tuple-element.59), channel_id=1, source_target_pairs={{0,6},{1,7},{2,4},{3,5},{4,2},{5,3},{6,0},{7,1},{8,14},{9,15},{10,... | collective-permute-start | bytes 417800 | tf_op jit(solution)/shard_map/ppermute | solution.py:189
  245.1 21.9 %collective-permute-start.15 = (f32[2,2,16,1024]{3,2,1,0:T(8,128)}, f32[2,2,16,1024]{3,2,1,0:T(8,128)}, u32[]{:S(2)}, u32[]{:S(2)}) collective-permute-start(f32[2,2,16,1024]{3,2,1,0:T(8,128)} %get-tuple-element.56), channel_id=1, source_target_pairs={{0,16},{1,17},{2,18},{3,19},{4,20},{5,21},{6,22},{7,23},{8,24},{9,... | collective-permute-start | bytes 786440 | tf_op jit(solution)/shard_map/ppermute | solution.py:189
  245.8 21.1 %collective-permute-start.16 = (f32[2,2,16,1024]{3,2,1,0:T(8,128)}, f32[2,2,16,1024]{3,2,1,0:T(8,128)}, u32[]{:S(2)}, u32[]{:S(2)}) collective-permute-start(f32[2,2,16,1024]{3,2,1,0:T(8,128)} %get-tuple-element.58), channel_id=1, source_target_pairs={{0,1},{1,0},{2,3},{3,2},{4,5},{5,4},{6,7},{7,6},{8,9},{9,8},{10,11... | collective-permute-start | bytes 786440 | tf_op jit(solution)/shard_map/ppermute | solution.py:189
  250.2 16.8 %collective-permute-start.17 = (f32[2,2,16,1024]{3,2,1,0:T(8,128)}, f32[2,2,16,1024]{3,2,1,0:T(8,128)}, u32[]{:S(2)}, u32[]{:S(2)}) collective-permute-start(f32[2,2,16,1024]{3,2,1,0:T(8,128)} %get-tuple-element.57), channel_id=1, source_target_pairs={{0,17},{1,16},{2,19},{3,18},{4,21},{5,20},{6,23},{7,22},{8,25},{9,... | collective-permute-start | bytes 786440 | tf_op jit(solution)/shard_map/ppermute | solution.py:189
  257.8 15.0 %collective-permute-start.8 = (f32[2,2,2,2,16,1152]{5,4,3,2,1,0:T(8,128)}, f32[2,2,2,2,16,1152]{5,4,3,2,1,0:T(8,128)}, u32[]{:S(2)}, u32[]{:S(2)}) collective-permute-start(f32[2,2,2,2,16,1152]{5,4,3,2,1,0:T(8,128)} %dynamic-slice_bitcast_fusion.1), channel_id=1, source_target_pairs={{0,8},{1,9},{2,10},{3,11},{4,12},{5,13},{6,14},{7,15},{8,0},{9,1},... | collective-permute-start | bytes 3538952 | tf_op jit(solution)/shard_map/ppermute | solution.py:189
  262.4 36.7 %all-to-all-start.8 = ((f32[8,2,16,512]{3,2,1,0:T(8,128)}), f32[8,2,16,512]{3,2,1,0:T(8,128)S(1)}, u32[]{:S(2)}, u32[]{:S(2)}) async-start(f32[8,2,16,512]{3,2,1,0:T(8,128)} %bitcast.90), calls=%async_computation.8 | async-start | bytes 1048576 | tf_op jit(solution)/shard_map/all_to_all | solution.py:129
  268.2 9.8 %collective-permute-start.18 = (f32[16,1024]{1,0:T(8,128)S(1)}, f32[16,1024]{1,0:T(8,128)S(1)}, u32[]{:S(2)}, u32[]{:S(2)}) collective-permute-start(f32[16,1024]{1,0:T(8,128)S(1)} %get-tuple-element.65), channel_id=1, source_target_pairs={{0,2},{1,3},{2,0},{3,1},{4,6},{5,7},{6,4},{7,5},{8,10},{9,11},{10,... | collective-permute-start | bytes 196616 | tf_op jit(solution)/shard_map/ppermute | solution.py:189
  270.3 16.7 %collective-permute-start.19 = (f32[16,1024]{1,0:T(8,128)S(1)}, f32[16,1024]{1,0:T(8,128)S(1)}, u32[]{:S(2)}, u32[]{:S(2)}) collective-permute-start(f32[16,1024]{1,0:T(8,128)S(1)} %get-tuple-element.67), channel_id=1, source_target_pairs={{0,4},{1,5},{2,6},{3,7},{4,0},{5,1},{6,2},{7,3},{8,12},{9,13},{10,... | collective-permute-start | bytes 196616 | tf_op jit(solution)/shard_map/ppermute | solution.py:189
  272.7 30.7 %copy-start.25 = (f32[1,16,1536]{2,1,0:T(8,128)S(1)}, f32[1,16,1536]{2,1,0:T(8,128)}, u32[]{:S(2)}) copy-start(f32[1,16,1536]{2,1,0:T(8,128)} %slice_bitcast_fusion.6) | copy-start | bytes 294916
  272.7 14.3 %collective-permute-start.20 = (f32[16,1024]{1,0:T(8,128)S(1)}, f32[16,1024]{1,0:T(8,128)S(1)}, u32[]{:S(2)}, u32[]{:S(2)}) collective-permute-start(f32[16,1024]{1,0:T(8,128)S(1)} %get-tuple-element.66), channel_id=1, source_target_pairs={{0,6},{1,7},{2,4},{3,5},{4,2},{5,3},{6,0},{7,1},{8,14},{9,15},{10,... | collective-permute-start | bytes 196616 | tf_op jit(solution)/shard_map/ppermute | solution.py:189
  274.2 12.8 %collective-permute-start.10 = (f32[2,2,16,1152]{3,2,1,0:T(8,128)S(1)}, f32[2,2,16,1152]{3,2,1,0:T(8,128)S(1)}, u32[]{:S(2)}, u32[]{:S(2)}) collective-permute-start(f32[2,2,16,1152]{3,2,1,0:T(8,128)S(1)} %get-tuple-element.55), channel_id=1, source_target_pairs={{0,1},{1,0},{2,3},{3,2},{4,5},{5,4},{6,7},{7,6},{8,9},{9,8},{10,11... | collective-permute-start | bytes 884744 | tf_op jit(solution)/shard_map/ppermute | solution.py:189
  276.3 14.7 %collective-permute-start.11 = (f32[2,2,16,1152]{3,2,1,0:T(8,128)S(1)}, f32[2,2,16,1152]{3,2,1,0:T(8,128)S(1)}, u32[]{:S(2)}, u32[]{:S(2)}) collective-permute-start(f32[2,2,16,1152]{3,2,1,0:T(8,128)S(1)} %get-tuple-element.54), channel_id=1, source_target_pairs={{0,17},{1,16},{2,19},{3,18},{4,21},{5,20},{6,23},{7,22},{8,25},{9,... | collective-permute-start | bytes 884744 | tf_op jit(solution)/shard_map/ppermute | solution.py:189
  278.1 14.4 %collective-permute-start.9 = (f32[2,2,16,1152]{3,2,1,0:T(8,128)S(1)}, f32[2,2,16,1152]{3,2,1,0:T(8,128)S(1)}, u32[]{:S(2)}, u32[]{:S(2)}) collective-permute-start(f32[2,2,16,1152]{3,2,1,0:T(8,128)S(1)} %get-tuple-element.53), channel_id=1, source_target_pairs={{0,16},{1,17},{2,18},{3,19},{4,20},{5,21},{6,22},{7,23},{8,24},{9,... | collective-permute-start | bytes 884744 | tf_op jit(solution)/shard_map/ppermute | solution.py:189
  292.6 7.8 %collective-permute-start.12 = (f32[16,1152]{1,0:T(8,128)S(1)}, f32[16,1152]{1,0:T(8,128)S(1)}, u32[]{:S(2)}, u32[]{:S(2)}) collective-permute-start(f32[16,1152]{1,0:T(8,128)S(1)} %get-tuple-element.62), channel_id=1, source_target_pairs={{0,2},{1,3},{2,0},{3,1},{4,6},{5,7},{6,4},{7,5},{8,10},{9,11},{10,... | collective-permute-start | bytes 221192 | tf_op jit(solution)/shard_map/ppermute | solution.py:189
  295.2 6.7 %collective-permute-start.13 = (f32[16,1152]{1,0:T(8,128)S(1)}, f32[16,1152]{1,0:T(8,128)S(1)}, u32[]{:S(2)}, u32[]{:S(2)}) collective-permute-start(f32[16,1152]{1,0:T(8,128)S(1)} %get-tuple-element.64), channel_id=1, source_target_pairs={{0,4},{1,5},{2,6},{3,7},{4,0},{5,1},{6,2},{7,3},{8,12},{9,13},{10,... | collective-permute-start | bytes 221192 | tf_op jit(solution)/shard_map/ppermute | solution.py:189
  297.0 6.3 %collective-permute-start.14 = (f32[16,1152]{1,0:T(8,128)S(1)}, f32[16,1152]{1,0:T(8,128)S(1)}, u32[]{:S(2)}, u32[]{:S(2)}) collective-permute-start(f32[16,1152]{1,0:T(8,128)S(1)} %get-tuple-element.63), channel_id=1, source_target_pairs={{0,6},{1,7},{2,4},{3,5},{4,2},{5,3},{6,0},{7,1},{8,14},{9,15},{10,... | collective-permute-start | bytes 221192 | tf_op jit(solution)/shard_map/ppermute | solution.py:189
  (28 other events, 145.8 us)
